TPU v7x, 32 devices: a whole 2x2x4 slice. The times are simulated.
32 devices in a mesh: depth: 32 (over z, y, x, core).
Axes of the slice: x: 2, y: 2, z: 4, core: 2. Of those that a mesh axis runs over, the one named last changes fastest.
Arguments:
- w_in: bfloat16 [64, 512, 1024], P('depth'), may hold values from -0.25 to 0.25
- w_out: bfloat16 [64, 1024, 512], P('depth'), may hold values from -0.0234375 to 0.0234375
- checkpoint: bfloat16 [32, 256, 512], P('depth'), may hold values from -6 to 6
- guess: float32 [32, 256, 512], P('depth'), may hold values from -6 to 6
- terminal: float32 [256, 512], replicated, may hold values from -6 to 6
Outputs:
- adjoint: float32 [64, 256, 512], P('depth')
- grad_in: bfloat16 [64, 512, 1024], P('depth')
- grad_out: bfloat16 [64, 1024, 512], P('depth')
All inputs are finite; a program needn't handle non-finite values.
Results may differ from a plain program's by a relative error of at most 0.017.
Values sent between devices are 32-bit elements; how exact they have to be, the bound alone decides.
No kernel may reach another device: no remote copies, remote signals or barrier semaphores. Data moves between devices by JAX's collectives and lax.ppermute only.
A program may use at most 64 MiB of HBM per device.

v0:
```python
import jax
import jax.numpy as jnp
from jax import lax
from jax.sharding import PartitionSpec as P

LEVELS = 4


def shifted(block, axis, distance):
    devices = range(lax.axis_size(axis))
    route = [(i - distance, i) for i in devices if i - distance in devices]
    return lax.ppermute(block, axis, route)


def tangent_of(vector, w_second, slope):
    product = jnp.dot(vector.astype(jnp.bfloat16), w_second.T, preferred_element_type=jnp.float32)
    return (product * slope).astype(jnp.bfloat16)


def apply_layer(vector, w_first, w_second, slope, factor):
    tangent = tangent_of(vector, w_second, slope)
    return (
        vector + factor * jnp.dot(tangent, w_first.T, preferred_element_type=jnp.float32),
        tangent,
    )


def local(w_in, w_out, checkpoint, guess, terminal):
    count = lax.axis_size("depth")
    place = lax.axis_index("depth")
    at_end = place == count - 1
    start = checkpoint[0]
    h_zero = jnp.tanh(jnp.dot(start, w_in[0], preferred_element_type=jnp.float32))
    act_zero = h_zero.astype(jnp.bfloat16)
    upper = start.astype(jnp.float32) + jnp.dot(
        act_zero, w_out[0], preferred_element_type=jnp.float32
    )
    upper_b = upper.astype(jnp.bfloat16)
    h_one = jnp.tanh(jnp.dot(upper_b, w_in[1], preferred_element_type=jnp.float32))
    act_one = h_one.astype(jnp.bfloat16)
    slope_zero = 1.0 - h_zero * h_zero
    slope_one = 1.0 - h_one * h_one

    def fine_next(values):
        moved = shifted(values, "depth", -1)
        return moved + jnp.where(at_end, terminal, jnp.zeros_like(terminal))

    def coarse_next(values, dist):
        return shifted(values, "depth", -dist)

    def cycle(level, rhs):
        dist = 2 ** (level - 1)
        active = place % dist == 0
        is_c = place % (2 * dist) == 0
        is_f = jnp.logical_and(active, jnp.logical_not(is_c))
        factor = float(2**level)

        def relax(values, mask):
            value, unused = apply_layer(
                coarse_next(values, dist), w_in[0], w_out[0], slope_zero, factor
            )
            return jnp.where(mask, value + rhs, values)

        values = jnp.where(is_f, rhs, jnp.zeros_like(rhs))
        values = relax(values, is_c)
        values = relax(values, is_f)
        if level == LEVELS - 1:
            return values
        value, unused = apply_layer(
            coarse_next(values, dist), w_in[0], w_out[0], slope_zero, factor
        )
        resid = jnp.where(is_c, value + rhs - values, jnp.zeros_like(rhs))
        values = values + cycle(level + 1, resid)
        return relax(values, is_f)

    even_value = guess[0]
    above = fine_next(even_value)
    odd_value, unused = apply_layer(above, w_in[1], w_out[1], slope_one, 1.0)
    value, unused = apply_layer(odd_value, w_in[0], w_out[0], slope_zero, 1.0)
    resid = value + 0.0 - even_value
    even_value = even_value + cycle(1, resid)
    above = fine_next(even_value)
    odd_value, tangent_one = apply_layer(above, w_in[1], w_out[1], slope_one, 1.0)
    odd_value = odd_value + 0.0
    tangent_zero = tangent_of(odd_value, w_out[0], slope_zero)
    grad_first = jnp.stack(
        [
            jnp.dot(start.T, tangent_zero, preferred_element_type=jnp.float32).astype(jnp.bfloat16),
            jnp.dot(upper_b.T, tangent_one, preferred_element_type=jnp.float32).astype(
                jnp.bfloat16
            ),
        ]
    )
    grad_second = jnp.stack(
        [
            jnp.dot(
                act_zero.T, odd_value.astype(jnp.bfloat16), preferred_element_type=jnp.float32
            ).astype(jnp.bfloat16),
            jnp.dot(
                act_one.T, above.astype(jnp.bfloat16), preferred_element_type=jnp.float32
            ).astype(jnp.bfloat16),
        ]
    )
    adjoint = jnp.stack([even_value, odd_value])
    return (adjoint, grad_first, grad_second)


def solution(mesh):
    placed = (
        P("depth", None, None),
        P("depth", None, None),
        P("depth", None, None),
        P("depth", None, None),
        P(),
    )
    return jax.shard_map(
        local,
        mesh=mesh,
        in_specs=placed,
        out_specs=(P("depth", None, None), P("depth", None, None), P("depth", None, None)),
        check_vma=False,
    )
```

profile of v0, /device:TPU:1, one launch (start us, length us, event | category | flops | bytes accessed | tf_op | source)
XLA Modules:
  0.0 228.6 jit_solution(15893562352857868741)
XLA Ops:
  0.6 1.9 collective-permute-start
  7.6 4.7 %collective-permute-done = f32[256,512]{1,0:T(8,128)} collective-permute-done((f32[256,512]{1,0:T(8,128)}, f32[256,512]{1,0:T(8,128)}, u32[]{:S(2)}, u32[]{:S(2)}) %collective-permute-start) | collective-permute-done | bytes 524320 | tf_op jit(solution)/shard_map/ppermute | solution.py:12
  12.3 3.5 %convolution_add_fusion.2 = f32[256,512]{1,0:T(8,128)} fusion(f32[256,1024]{1,0:T(8,128)} %convolution_tanh_fusion, bf16[2,1024,512]{2,1,0:T(8,128)(2,1)} %param.6, bf16[2,512,1024]{2,1,0:T(8,128)(2,1)S(1)} %copy-done, f32[256,512]{1,0:T(8,128)} %collective-permute-done, f32[256,512]{1,0:T(8,128)} %param.9, pred[]{:T(512)S(6)} %eq.23), kind=kOutput, calls=%fused_computation.52 | convolution fusion | flops 538705920 | bytes 5768192 | tf_op jit(solution)/shard_map/dot_general | solution.py:23
  15.8 3.4 %broadcast_select_fusion.2 = (f32[256,512]{1,0:T(8,128)}, f32[256,512]{1,0:T(8,128)}) fusion(pred[]{:T(512)S(6)} %not.9, f32[1,256,512]{2,1,0:T(8,128)} %param.8, f32[256,512]{1,0:T(8,128)} %convolution_add_fusion.2, bf16[2,512,1024]{2,1,0:T(8,128)(2,1)S(1)} %copy-done, f32[256,1024]{1,0:T(8,128)S(1)} %convolution_tanh_fusion.1, ...), kind=kOutput, calls=%fused_computation.151 | convolution fusion | flops 538443776 | bytes 5767169 | tf_op jit(solution)/shard_map/dot_general | solution.py:23
  19.2 1.9 collective-permute-start.1
  21.1 8.9 %collective-permute-done.1 = f32[256,512]{1,0:T(8,128)} collective-permute-done((f32[256,512]{1,0:T(8,128)}, f32[256,512]{1,0:T(8,128)}, u32[]{:S(2)}, u32[]{:S(2)}) %collective-permute-start.1) | collective-permute-done | bytes 524320 | tf_op jit(solution)/shard_map/ppermute | solution.py:12
  30.0 3.2 %fusion.53 = f32[256,512]{1,0:T(8,128)} fusion(f32[256,512]{1,0:T(8,128)} %get-tuple-element.7, f32[256,512]{1,0:T(8,128)} %collective-permute-done.1, pred[]{:T(512)S(6)} %eq.22, pred[]{:T(512)S(6)} %not.9, f32[256,1024]{1,0:T(8,128)S(1)} %convolution_tanh_fusion.1, bf16[2,512,1024]{2,1,0:T(8,128)(2,1)S(1)} %copy-done, bf16[2,1024,512]{2,1,0:T(8,128)(2,1)} %param.6), kind=kOutput, calls=%fused_computation.89 | convolution fusion | flops 538705920 | bytes 5242882 | tf_op jit(solution)/shard_map/dot_general | solution.py:23
  33.3 1.9 collective-permute-start.2
  35.2 8.9 %collective-permute-done.2 = f32[256,512]{1,0:T(8,128)} collective-permute-done((f32[256,512]{1,0:T(8,128)}, f32[256,512]{1,0:T(8,128)}, u32[]{:S(2)}, u32[]{:S(2)}) %collective-permute-start.2) | collective-permute-done | bytes 524320 | tf_op jit(solution)/shard_map/ppermute | solution.py:12
  44.1 3.2 %fusion.51 = f32[256,512]{1,0:T(8,128)} fusion(f32[256,512]{1,0:T(8,128)} %fusion.53, f32[256,512]{1,0:T(8,128)} %get-tuple-element.7, f32[256,512]{1,0:T(8,128)} %collective-permute-done.2, pred[]{:T(512)S(6)} %not.9, f32[256,1024]{1,0:T(8,128)S(1)} %convolution_tanh_fusion.1, bf16[2,512,1024]{2,1,0:T(8,128)(2,1)S(1)} %copy-done, ...), kind=kOutput, calls=%fused_computation.87 | convolution fusion | flops 538574848 | bytes 5767169 | tf_op jit(solution)/shard_map/dot_general | solution.py:23
  49.2 8.9 %collective-permute-done.3 = f32[256,512]{1,0:T(8,128)} collective-permute-done((f32[256,512]{1,0:T(8,128)}, f32[256,512]{1,0:T(8,128)}, u32[]{:S(2)}, u32[]{:S(2)}) %collective-permute-start.3) | collective-permute-done | bytes 524320 | tf_op jit(solution)/shard_map/ppermute | solution.py:12
  58.1 3.6 %broadcast_select_fusion.1 = (f32[256,512]{1,0:T(8,128)}, f32[256,512]{1,0:T(8,128)}) fusion(pred[]{:T(512)S(6)} %and.27, f32[256,512]{1,0:T(8,128)} %fusion.51, f32[256,512]{1,0:T(8,128)} %get-tuple-element.7, f32[256,512]{1,0:T(8,128)} %collective-permute-done.3, bf16[2,512,1024]{2,1,0:T(8,128)(2,1)S(1)} %copy-done, ...), kind=kOutput, calls=%fused_computation.150 | convolution fusion | flops 538836992 | bytes 6291458 | tf_op jit(solution)/shard_map/dot_general | solution.py:23
  63.0 13.2 %collective-permute-done.4 = f32[256,512]{1,0:T(8,128)} collective-permute-done((f32[256,512]{1,0:T(8,128)}, f32[256,512]{1,0:T(8,128)}, u32[]{:S(2)}, u32[]{:S(2)}) %collective-permute-start.4) | collective-permute-done | bytes 524320 | tf_op jit(solution)/shard_map/ppermute | solution.py:12
  76.2 3.2 %fusion.46 = f32[256,512]{1,0:T(8,128)} fusion(f32[256,512]{1,0:T(8,128)} %get-tuple-element.9, f32[256,512]{1,0:T(8,128)} %collective-permute-done.4, pred[]{:T(512)S(6)} %eq.24, pred[]{:T(512)S(6)} %and.27, f32[256,1024]{1,0:T(8,128)S(1)} %convolution_tanh_fusion.1, bf16[2,512,1024]{2,1,0:T(8,128)(2,1)S(1)} %copy-done, bf16[2,1024,512]{2,1,0:T(8,128)(2,1)} %param.6), kind=kOutput, calls=%fused_computation.82 | convolution fusion | flops 538705920 | bytes 5242882 | tf_op jit(solution)/shard_map/dot_general | solution.py:23
  80.7 16.5 %collective-permute-done.5 = f32[256,512]{1,0:T(8,128)} collective-permute-done((f32[256,512]{1,0:T(8,128)}, f32[256,512]{1,0:T(8,128)}, u32[]{:S(2)}, u32[]{:S(2)}) %collective-permute-start.5) | collective-permute-done | bytes 524320 | tf_op jit(solution)/shard_map/ppermute | solution.py:12
  97.2 3.4 %fusion.44 = f32[256,512]{1,0:T(8,128)} fusion(f32[256,512]{1,0:T(8,128)} %fusion.46, f32[256,512]{1,0:T(8,128)} %get-tuple-element.9, f32[256,512]{1,0:T(8,128)} %collective-permute-done.5, pred[]{:T(512)S(6)} %and.27, f32[256,1024]{1,0:T(8,128)S(1)} %convolution_tanh_fusion.1, bf16[2,512,1024]{2,1,0:T(8,128)(2,1)S(1)} %copy-done, ...), kind=kOutput, calls=%fused_computation.80 | convolution fusion | flops 538574848 | bytes 5767169 | tf_op jit(solution)/shard_map/dot_general | solution.py:23
  101.9 15.4 %collective-permute-done.6 = f32[256,512]{1,0:T(8,128)} collective-permute-done((f32[256,512]{1,0:T(8,128)}, f32[256,512]{1,0:T(8,128)}, u32[]{:S(2)}, u32[]{:S(2)}) %collective-permute-start.6) | collective-permute-done | bytes 524320 | tf_op jit(solution)/shard_map/ppermute | solution.py:12
  117.3 3.6 %broadcast_select_fusion = (f32[256,512]{1,0:T(8,128)}, f32[256,512]{1,0:T(8,128)}) fusion(pred[]{:T(512)S(6)} %and.29, f32[256,512]{1,0:T(8,128)} %fusion.44, f32[256,512]{1,0:T(8,128)} %get-tuple-element.9, f32[256,512]{1,0:T(8,128)} %collective-permute-done.6, bf16[2,512,1024]{2,1,0:T(8,128)(2,1)S(1)} %copy-done, ...), kind=kOutput, calls=%fused_computation.149 | convolution fusion | flops 538836992 | bytes 6291458 | tf_op jit(solution)/shard_map/dot_general | solution.py:23
  122.2 16.7 %collective-permute-done.7 = f32[256,512]{1,0:T(8,128)} collective-permute-done((f32[256,512]{1,0:T(8,128)}, f32[256,512]{1,0:T(8,128)}, u32[]{:S(2)}, u32[]{:S(2)}) %collective-permute-start.7) | collective-permute-done | bytes 524320 | tf_op jit(solution)/shard_map/ppermute | solution.py:12
  138.8 3.2 %fusion.39 = f32[256,512]{1,0:T(8,128)} fusion(f32[256,512]{1,0:T(8,128)} %get-tuple-element.11, f32[256,512]{1,0:T(8,128)} %collective-permute-done.7, pred[]{:T(512)S(6)} %eq.25, pred[]{:T(512)S(6)} %and.29, f32[256,1024]{1,0:T(8,128)S(1)} %convolution_tanh_fusion.1, bf16[2,512,1024]{2,1,0:T(8,128)(2,1)S(1)} %copy-done, bf16[2,1024,512]{2,1,0:T(8,128)(2,1)} %param.6), kind=kOutput, calls=%fused_computation.75 | convolution fusion | flops 538705920 | bytes 5242882 | tf_op jit(solution)/shard_map/dot_general | solution.py:23
  143.3 15.6 %collective-permute-done.8 = f32[256,512]{1,0:T(8,128)} collective-permute-done((f32[256,512]{1,0:T(8,128)}, f32[256,512]{1,0:T(8,128)}, u32[]{:S(2)}, u32[]{:S(2)}) %collective-permute-start.8) | collective-permute-done | bytes 524320 | tf_op jit(solution)/shard_map/ppermute | solution.py:12
  159.0 3.6 %fusion.37 = f32[256,512]{1,0:T(8,128)} fusion(f32[256,512]{1,0:T(8,128)} %fusion.44, f32[256,512]{1,0:T(8,128)} %fusion.39, f32[256,512]{1,0:T(8,128)} %get-tuple-element.11, f32[256,512]{1,0:T(8,128)} %collective-permute-done.8, pred[]{:T(512)S(6)} %and.29, f32[256,1024]{1,0:T(8,128)S(1)} %convolution_tanh_fusion.1, ...), kind=kOutput, calls=%fused_computation.73 | convolution fusion | flops 538705920 | bytes 6291457 | tf_op jit(solution)/shard_map/dot_general | solution.py:23
  163.8 15.5 %collective-permute-done.9 = f32[256,512]{1,0:T(8,128)} collective-permute-done((f32[256,512]{1,0:T(8,128)}, f32[256,512]{1,0:T(8,128)}, u32[]{:S(2)}, u32[]{:S(2)}) %collective-permute-start.9) | collective-permute-done | bytes 524320 | tf_op jit(solution)/shard_map/ppermute | solution.py:12
  179.3 3.6 %fusion.34 = f32[256,512]{1,0:T(8,128)} fusion(f32[256,512]{1,0:T(8,128)} %fusion.51, f32[256,512]{1,0:T(8,128)} %fusion.37, f32[256,512]{1,0:T(8,128)} %get-tuple-element.9, f32[256,512]{1,0:T(8,128)} %collective-permute-done.9, pred[]{:T(512)S(6)} %and.27, f32[256,1024]{1,0:T(8,128)S(1)} %convolution_tanh_fusion.1, bf16[2,512,1024]{2,1,0:T(8,128)(2,1)S(1)} %copy-done, ...), kind=kOutput, calls=%fused_computation.70 | convolution fusion | flops 538705920 | bytes 6291457 | tf_op jit(solution)/shard_map/dot_general | solution.py:23
  182.9 3.6 %collective-permute-start.10 = (f32[256,512]{1,0:T(8,128)}, f32[256,512]{1,0:T(8,128)}, u32[]{:S(2)}, u32[]{:S(2)}) collective-permute-start(f32[256,512]{1,0:T(8,128)} %fusion.34), channel_id=1, source_target_pairs={{1,0},{2,1},{3,2},{4,3},{5,4},{6,5},{7,6},{8,7},{9,8},{10,9},{11,1... | collective-permute-start | bytes 1572872 | tf_op jit(solution)/shard_map/ppermute | solution.py:12
  186.5 9.2 %collective-permute-done.10 = f32[256,512]{1,0:T(8,128)} collective-permute-done((f32[256,512]{1,0:T(8,128)}, f32[256,512]{1,0:T(8,128)}, u32[]{:S(2)}, u32[]{:S(2)}) %collective-permute-start.10) | collective-permute-done | bytes 524320 | tf_op jit(solution)/shard_map/ppermute | solution.py:12
  195.7 3.4 %fusion.31 = f32[256,512]{1,0:T(8,128)} fusion(f32[256,512]{1,0:T(8,128)} %fusion.34, f32[256,512]{1,0:T(8,128)} %get-tuple-element.7, f32[256,512]{1,0:T(8,128)} %collective-permute-done.10, pred[]{:T(512)S(6)} %not.9, f32[1,256,512]{2,1,0:T(8,128)} %param.8, f32[256,1024]{1,0:T(8,128)S(1)} %convolution_tanh_fusion.1, ...), kind=kOutput, calls=%fused_computation.67 | convolution fusion | flops 538705920 | bytes 6291457 | tf_op jit(solution)/shard_map/dot_general | solution.py:23
  199.1 2.2 collective-permute-start.11
  201.4 8.6 %collective-permute-done.11 = f32[256,512]{1,0:T(8,128)S(1)} collective-permute-done((f32[256,512]{1,0:T(8,128)}, f32[256,512]{1,0:T(8,128)S(1)}, u32[]{:S(2)}, u32[]{:S(2)}) %collective-permute-start.11) | collective-permute-done | bytes 524320 | tf_op jit(solution)/shard_map/ppermute | solution.py:12
  210.1 2.0 fusion.16
  218.3 2.8 %fusion = bf16[1,512,1024]{1,2,0:T(8,128)(2,1)} fusion(bf16[1,256,512]{2,1,0:T(8,128)(2,1)S(1)} %copy-done.8, f32[256,512]{1,0:T(8,128)} %copy-done.3, f32[256,1024]{1,0:T(8,128)S(1)} %convolution_tanh_fusion.1, bf16[2,1024,512]{2,1,0:T(8,128)(2,1)S(1)} %copy-done.1), kind=kOutput, calls=%fused_computation.6 | convolution fusion | flops 538574848 | bytes 3932160 | tf_op jit(solution)/shard_map/dot_general | solution.py:88
  222.8 2.4 %copy.9 = bf16[2,512,1024]{2,1,0:T(8,128)(2,1)} copy(bf16[2,512,1024]{1,2,0:T(8,128)(2,1)S(1)} %pad_maximum_fusion) | data formatting | bytes 4194304
  (40 shorter events, 26.0 us)
Async XLA Ops:
  0.6 11.7 %collective-permute-start = (f32[256,512]{1,0:T(8,128)}, f32[256,512]{1,0:T(8,128)}, u32[]{:S(2)}, u32[]{:S(2)}) collective-permute-start(f32[256,512]{1,0:T(8,128)} %bitcast.118), channel_id=1, source_target_pairs={{1,0},{2,1},{3,2},{4,3},{5,4},{6,5},{7,6},{8,7},{9,8},{10,9},{11,1... | collective-permute-start | bytes 1572872 | tf_op jit(solution)/shard_map/ppermute | solution.py:12
  2.6 1.9 copy-start.7
  2.6 3.6 %copy-start = (bf16[2,512,1024]{2,1,0:T(8,128)(2,1)S(1)}, bf16[2,512,1024]{2,1,0:T(8,128)(2,1)}, u32[]{:S(2)}) copy-start(bf16[2,512,1024]{2,1,0:T(8,128)(2,1)} %param.5) | copy-start | bytes 6291460
  19.2 10.8 %collective-permute-start.1 = (f32[256,512]{1,0:T(8,128)}, f32[256,512]{1,0:T(8,128)}, u32[]{:S(2)}, u32[]{:S(2)}) collective-permute-start(f32[256,512]{1,0:T(8,128)} %get-tuple-element.6), channel_id=1, source_target_pairs={{1,0},{2,1},{3,2},{4,3},{5,4},{6,5},{7,6},{8,7},{9,8},{10,9},{11,1... | collective-permute-start | bytes 1572872 | tf_op jit(solution)/shard_map/ppermute | solution.py:12
  33.3 10.8 %collective-permute-start.2 = (f32[256,512]{1,0:T(8,128)}, f32[256,512]{1,0:T(8,128)}, u32[]{:S(2)}, u32[]{:S(2)}) collective-permute-start(f32[256,512]{1,0:T(8,128)} %fusion.53), channel_id=1, source_target_pairs={{1,0},{2,1},{3,2},{4,3},{5,4},{6,5},{7,6},{8,7},{9,8},{10,9},{11,1... | collective-permute-start | bytes 1572872 | tf_op jit(solution)/shard_map/ppermute | solution.py:12
  47.3 10.8 %collective-permute-start.3 = (f32[256,512]{1,0:T(8,128)}, f32[256,512]{1,0:T(8,128)}, u32[]{:S(2)}, u32[]{:S(2)}) collective-permute-start(f32[256,512]{1,0:T(8,128)} %fusion.51), channel_id=1, source_target_pairs={{1,0},{2,1},{3,2},{4,3},{5,4},{6,5},{7,6},{8,7},{9,8},{10,9},{11,1... | collective-permute-start | bytes 1572872 | tf_op jit(solution)/shard_map/ppermute | solution.py:12
  61.7 14.5 %collective-permute-start.4 = (f32[256,512]{1,0:T(8,128)}, f32[256,512]{1,0:T(8,128)}, u32[]{:S(2)}, u32[]{:S(2)}) collective-permute-start(f32[256,512]{1,0:T(8,128)} %get-tuple-element.8), channel_id=1, source_target_pairs={{2,0},{3,1},{4,2},{5,3},{6,4},{7,5},{8,6},{9,7},{10,8},{11,9},{12,... | collective-permute-start | bytes 1572872 | tf_op jit(solution)/shard_map/ppermute | solution.py:12
  79.4 17.8 %collective-permute-start.5 = (f32[256,512]{1,0:T(8,128)}, f32[256,512]{1,0:T(8,128)}, u32[]{:S(2)}, u32[]{:S(2)}) collective-permute-start(f32[256,512]{1,0:T(8,128)} %fusion.46), channel_id=1, source_target_pairs={{2,0},{3,1},{4,2},{5,3},{6,4},{7,5},{8,6},{9,7},{10,8},{11,9},{12,... | collective-permute-start | bytes 1572872 | tf_op jit(solution)/shard_map/ppermute | solution.py:12
  100.6 16.7 %collective-permute-start.6 = (f32[256,512]{1,0:T(8,128)}, f32[256,512]{1,0:T(8,128)}, u32[]{:S(2)}, u32[]{:S(2)}) collective-permute-start(f32[256,512]{1,0:T(8,128)} %fusion.44), channel_id=1, source_target_pairs={{2,0},{3,1},{4,2},{5,3},{6,4},{7,5},{8,6},{9,7},{10,8},{11,9},{12,... | collective-permute-start | bytes 1572872 | tf_op jit(solution)/shard_map/ppermute | solution.py:12
  120.9 17.9 %collective-permute-start.7 = (f32[256,512]{1,0:T(8,128)}, f32[256,512]{1,0:T(8,128)}, u32[]{:S(2)}, u32[]{:S(2)}) collective-permute-start(f32[256,512]{1,0:T(8,128)} %get-tuple-element.10), channel_id=1, source_target_pairs={{4,0},{5,1},{6,2},{7,3},{8,4},{9,5},{10,6},{11,7},{12,8},{13,9},{1... | collective-permute-start | bytes 1572872 | tf_op jit(solution)/shard_map/ppermute | solution.py:12
  142.0 16.9 %collective-permute-start.8 = (f32[256,512]{1,0:T(8,128)}, f32[256,512]{1,0:T(8,128)}, u32[]{:S(2)}, u32[]{:S(2)}) collective-permute-start(f32[256,512]{1,0:T(8,128)} %fusion.39), channel_id=1, source_target_pairs={{4,0},{5,1},{6,2},{7,3},{8,4},{9,5},{10,6},{11,7},{12,8},{13,9},{1... | collective-permute-start | bytes 1572872 | tf_op jit(solution)/shard_map/ppermute | solution.py:12
  162.5 16.8 %collective-permute-start.9 = (f32[256,512]{1,0:T(8,128)}, f32[256,512]{1,0:T(8,128)}, u32[]{:S(2)}, u32[]{:S(2)}) collective-permute-start(f32[256,512]{1,0:T(8,128)} %fusion.37), channel_id=1, source_target_pairs={{2,0},{3,1},{4,2},{5,3},{6,4},{7,5},{8,6},{9,7},{10,8},{11,9},{12,... | collective-permute-start | bytes 1572872 | tf_op jit(solution)/shard_map/ppermute | solution.py:12
  182.9 12.9 %collective-permute-start.10 = (f32[256,512]{1,0:T(8,128)}, f32[256,512]{1,0:T(8,128)}, u32[]{:S(2)}, u32[]{:S(2)}) collective-permute-start(f32[256,512]{1,0:T(8,128)} %fusion.34), channel_id=1, source_target_pairs={{1,0},{2,1},{3,2},{4,3},{5,4},{6,5},{7,6},{8,7},{9,8},{10,9},{11,1... | collective-permute-start | bytes 1572872 | tf_op jit(solution)/shard_map/ppermute | solution.py:12
  199.1 13.0 %copy-start.2 = (f32[256,1024]{1,0:T(8,128)S(1)}, f32[256,1024]{1,0:T(8,128)}, u32[]{:S(2)}) copy-start(f32[256,1024]{1,0:T(8,128)} %convolution_tanh_fusion) | copy-start | bytes 3145732
  199.1 10.8 %collective-permute-start.11 = (f32[256,512]{1,0:T(8,128)}, f32[256,512]{1,0:T(8,128)S(1)}, u32[]{:S(2)}, u32[]{:S(2)}) collective-permute-start(f32[256,512]{1,0:T(8,128)} %fusion.31), channel_id=1, source_target_pairs={{1,0},{2,1},{3,2},{4,3},{5,4},{6,5},{7,6},{8,7},{9,8},{10,9},{11,1... | collective-permute-start | bytes 1572872 | tf_op jit(solution)/shard_map/ppermute | solution.py:12
  212.1 2.9 %copy-start.9 = (f32[256,512]{1,0:T(8,128)S(1)}, f32[256,512]{1,0:T(8,128)}, u32[]{:S(2)}) copy-start(f32[256,512]{1,0:T(8,128)} %param.9) | copy-start | bytes 1572868
  215.5 0.8 copy-start.3
  216.3 1.9 copy-start.1
  216.3 2.0 copy-start.8
  222.8 2.4 %copy-start.4 = (f32[256,512]{1,0:T(8,128)S(1)}, f32[256,512]{1,0:T(8,128)}, u32[]{:S(2)}) copy-start(f32[256,512]{1,0:T(8,128)} %copy-done.3) | copy-start | bytes 1572868
  222.8 2.4 %copy-start.10 = (f32[256,512]{1,0:T(8,128)S(1)}, f32[256,512]{1,0:T(8,128)}, u32[]{:S(2)}) copy-start(f32[256,512]{1,0:T(8,128)} %fusion.31) | copy-start | bytes 1572868
  225.2 1.6 copy-start.5
  225.2 1.9 copy-start.6
where the time goes:
time: 233 us; the launch traced here: 229 us
  waiting for transfers between devices  142 us (61%)
  matrix products  55.5 us (24%)
  starting transfers between devices  21.2 us (9%)
  local copies, waits for them, and re-layouts  4.58 us (2%)
  other arithmetic  4.38 us (2%)
    ppermute x12, waiting for transfers between devices, shifted(): return lax.ppermute(block, axis, route)  142 us
    dot_general x13, matrix products, apply_layer(): jnp.dot(tangent, w_first.T, preferred_element_type=jnp.float32)  41.3 us
    ppermute x12, starting transfers between devices, shifted(): return lax.ppermute(block, axis, route)  21.2 us
  transfers between devices with their start and end apart: 12, of which 12 were waited for; matrix products, arithmetic and copies ran while one was open for 2% of the time, Pallas kernels for 0%

commit v1 on v0

v1 whole, which is shorter than its diff:
```python
import functools

import jax
import jax.numpy as jnp
from jax import lax
from jax.experimental import pallas as pl
from jax.experimental.pallas import tpu as pltpu
from jax.sharding import PartitionSpec as P

LEVELS = 4
CHUNKS = 2
F32, BF16 = jnp.float32, jnp.bfloat16
VMEM = pl.BlockSpec(memory_space=pltpu.VMEM)
SMEM = pl.BlockSpec(memory_space=pltpu.SMEM)
ANY = pl.BlockSpec(memory_space=pl.ANY)


def dot(a, b):
    return jnp.dot(a, b, preferred_element_type=F32)


def held(value):
    return pltpu.with_memory_space_constraint(value, pltpu.VMEM)


def params(mib):
    return pltpu.CompilerParams(vmem_limit_bytes=mib * 2**20)


def forward_kernel(start, w_in, w_out, in_t0, in_t1, out_t0, out_t1, slope0, slope1, start_t, upper_t, act_t0, act_t1):
    first = start[0]
    h_zero = jnp.tanh(dot(first, w_in[0]))
    slope0[...] = 1.0 - h_zero * h_zero
    act_zero = h_zero.astype(BF16)
    upper = (first.astype(F32) + dot(act_zero, w_out[0])).astype(BF16)
    h_one = jnp.tanh(dot(upper, w_in[1]))
    slope1[...] = 1.0 - h_one * h_one
    in_t0[...] = w_in[0].T
    in_t1[...] = w_in[1].T
    out_t0[...] = w_out[0].T
    out_t1[...] = w_out[1].T
    start_t[...] = first.T
    upper_t[...] = upper.T
    act_t0[...] = act_zero.T
    act_t1[...] = h_one.astype(BF16).T


def forward(start, w_in, w_out):
    _, rows, d = start.shape
    ff = w_in.shape[2]
    return pl.pallas_call(
        forward_kernel,
        out_shape=(
            pltpu.VMEM((ff, d), BF16),
            pltpu.VMEM((ff, d), BF16),
            pltpu.VMEM((d, ff), BF16),
            pltpu.VMEM((d, ff), BF16),
            pltpu.VMEM((rows, ff), F32),
            pltpu.VMEM((rows, ff), F32),
            pltpu.VMEM((d, rows), BF16),
            pltpu.VMEM((d, rows), BF16),
            pltpu.VMEM((ff, rows), BF16),
            pltpu.VMEM((ff, rows), BF16),
        ),
        in_specs=[VMEM] * 3,
        out_specs=[VMEM] * 10,
        compiler_params=params(30),
        name="forward",
    )(start, w_in, w_out)


def tangent(vector, out_t, slope):
    return (dot(vector.astype(BF16), out_t) * slope).astype(BF16)


def first_kernel(low, size, at_end, moved, terminal, guess, in_t0, in_t1, out_t0, out_t1, slope0, slope1, above, resid):
    rows = pl.ds(low, size)

    @pl.when(at_end[0] == 1)
    def _():
        above[...] = terminal[rows, :]

    @pl.when(at_end[0] == 0)
    def _():
        above[...] = moved[...]

    value = above[...]
    odd = value + dot(tangent(value, out_t1[...], slope1[rows, :]), in_t1[...])
    even = odd + dot(tangent(odd, out_t0[...], slope0[rows, :]), in_t0[...])
    resid[...] = even - guess[0, rows, :]


def phi_kernel(low, size, factor, count, vector, in_t, out_t, slope, *refs):
    result = refs[count]
    value = vector[...]
    total = value + factor * dot(tangent(value, out_t[...], slope[pl.ds(low, size), :]), in_t[...])
    for addend in refs[:count]:
        total += addend[...] if len(addend.shape) == 2 else addend[0, pl.ds(low, size), :]
    result[...] = total


def next_kernel(low, size, is_odd, received, above, arrived, out_t0, out_t1, in_t1, slope0, slope1, odd, above_b, odd_b, tan1, tan0):
    rows = pl.ds(low, size)

    @pl.when(is_odd[0] == 1)
    def _():
        odd[...] = above[...] + received[...]

    @pl.when(is_odd[0] == 0)
    def _():
        odd[...] = arrived[...]

    nxt = odd[...]
    above_b[...] = nxt.astype(BF16)
    tan_one = tangent(nxt, out_t1[...], slope1[rows, :])
    tan1[...] = tan_one
    value = nxt + dot(tan_one, in_t1[...])
    odd[...] = value
    odd_b[...] = value.astype(BF16)
    tan0[...] = tangent(value, out_t0[...], slope0[rows, :])


def grads_kernel(chunks, start_t, upper_t, act_t0, act_t1, *refs):
    groups = [refs[i * chunks : (i + 1) * chunks] for i in range(6)]
    even, odd, above_b, odd_b, tan1, tan0 = groups
    adjoint, grad_in, grad_out, grad_in_v, grad_out_v, sems = refs[6 * chunks :]
    copies = []

    def send(source, target):
        copy = pltpu.make_async_copy(source, target, sems.at[len(copies)])
        copy.start()
        copies.append(copy)

    low = 0
    for part in range(chunks):
        size = even[part].shape[0]
        send(even[part], adjoint.at[0, pl.ds(low, size), :])
        send(odd[part], adjoint.at[1, pl.ds(low, size), :])
        low += size

    def product(left, right):
        low, total = 0, None
        for part in right:
            size = part.shape[0]
            term = dot(left[:, pl.ds(low, size)], part[...])
            total = term if total is None else total + term
            low += size
        return total.astype(BF16)

    for layer, left, right, buffer, target in (
        (1, act_t1, above_b, grad_out_v, grad_out),
        (1, upper_t, tan1, grad_in_v, grad_in),
        (0, act_t0, odd_b, grad_out_v, grad_out),
        (0, start_t, tan0, grad_in_v, grad_in),
    ):
        buffer[layer] = product(left, right)
        send(buffer.at[layer], target.at[layer])
    for copy in copies:
        copy.wait()


def local(w_in, w_out, checkpoint, guess, terminal):
    count = lax.axis_size("depth")
    place = lax.axis_index("depth")
    rows, d = terminal.shape
    ff = w_in.shape[2]
    size = rows // CHUNKS
    lows = [size * i for i in range(CHUNKS)]
    at_end = (place == count - 1).astype(jnp.int32).reshape(1)
    is_odd = (place % 2).astype(jnp.int32).reshape(1)

    def send(values, period, phase, distance):
        route = [(i, i - distance) for i in range(count) if i % period == phase and i >= distance]
        return [lax.ppermute(value, "depth", route) for value in values]

    moved = send([guess[0, low : low + size] for low in lows], 1, 0, 1)
    operands = forward(checkpoint, w_in, w_out)
    in_t0, in_t1, out_t0, out_t1, slope0, slope1, start_t, upper_t, act_t0, act_t1 = map(held, operands)

    def first(low, value):
        return pl.pallas_call(
            functools.partial(first_kernel, low, size),
            out_shape=(pltpu.VMEM((size, d), F32), pltpu.VMEM((size, d), F32)),
            in_specs=[SMEM] + [VMEM] * 9,
            out_specs=[VMEM] * 2,
            compiler_params=params(16),
            name="first",
        )(at_end, held(value), terminal, guess, in_t0, in_t1, out_t0, out_t1, slope0, slope1)

    def phi(values, factor, *addends):
        results = []
        for part, low in enumerate(lows):
            extra = [a[part] if isinstance(a, list) else a for a in addends]
            results.append(
                pl.pallas_call(
                    functools.partial(phi_kernel, low, size, factor, len(extra)),
                    out_shape=pltpu.VMEM((size, d), F32),
                    in_specs=[VMEM] * (4 + len(extra)),
                    out_specs=VMEM,
                    compiler_params=params(16),
                    name="phi",
                )(held(values[part]), in_t0, out_t0, slope0, *[held(e) if e.ndim == 2 else e for e in extra])
            )
        return results

    def cycle(level, rhs, addend):
        distance = 2 ** (level - 1)
        period, factor = 2 * distance, float(2**level)

        def to_even(values):
            return send(values, period, distance, distance)

        def to_odd(values):
            return send(values, period, 0, distance)

        values = phi(to_even(rhs), factor, rhs)
        if level < LEVELS - 1:
            resid = phi(to_even(phi(to_odd(values), factor)), factor)
            values, _ = cycle(level + 1, resid, values)
        received = to_odd(values)
        return phi(received, factor, values, addend), received

    firsts = [first(low, value) for low, value in zip(lows, moved)]
    above = [pair[0] for pair in firsts]
    even, received = cycle(1, [pair[1] for pair in firsts], guess)
    arrived = send(even, 2, 1, 1)

    lasts = []
    for part, low in enumerate(lows):
        lasts.append(
            pl.pallas_call(
                functools.partial(next_kernel, low, size),
                out_shape=(
                    pltpu.VMEM((size, d), F32),
                    pltpu.VMEM((size, d), BF16),
                    pltpu.VMEM((size, d), BF16),
                    pltpu.VMEM((size, ff), BF16),
                    pltpu.VMEM((size, ff), BF16),
                ),
                in_specs=[SMEM] + [VMEM] * 8,
                out_specs=[VMEM] * 5,
                compiler_params=params(16),
                name="last",
            )(
                is_odd,
                held(received[part]),
                held(above[part]),
                held(arrived[part]),
                out_t0,
                out_t1,
                in_t1,
                slope0,
                slope1,
            )
        )
    groups = [even] + [[last[i] for last in lasts] for i in range(5)]
    return pl.pallas_call(
        functools.partial(grads_kernel, CHUNKS),
        out_shape=(
            jax.ShapeDtypeStruct((2, rows, d), F32),
            jax.ShapeDtypeStruct((2, d, ff), BF16),
            jax.ShapeDtypeStruct((2, ff, d), BF16),
        ),
        in_specs=[VMEM] * (4 + 6 * CHUNKS),
        out_specs=[ANY] * 3,
        scratch_shapes=[
            pltpu.VMEM((2, d, ff), BF16),
            pltpu.VMEM((2, ff, d), BF16),
            pltpu.SemaphoreType.DMA((2 * CHUNKS + 4,)),
        ],
        compiler_params=params(24),
        name="grads",
    )(start_t, upper_t, act_t0, act_t1, *[held(value) for group in groups for value in group])


def solution(mesh):
    split = P("depth", None, None)
    return jax.shard_map(
        local,
        mesh=mesh,
        in_specs=(split, split, split, split, P()),
        out_specs=(split, split, split),
        check_vma=False,
    )
```

time: 233 us -> 109 us (0.47); the launches traced: 229 us -> 108 us
  waiting for transfers between devices: 142 us -> 46.2 us
  matrix products: 55.5 us -> 0 us
  Pallas kernels: 0 us -> 23.1 us
  local copies, waits for them, and re-layouts: 4.58 us -> 10.6 us
  starting transfers between devices: 21.2 us -> 26.3 us
  other arithmetic: 4.38 us -> 0 us
    ppermute x12 -> x24, waiting for transfers between devices: 142 us -> 46.2 us  [send(): return [lax.ppermute(value, 'depth', route) for value in values]]
    dot_general x21 -> x0, matrix products: 55.5 us -> none  [the longest x13 41.3 us: apply_layer(): jnp.dot(tangent, w_first.T, preferred_element_type=jnp.float32)]
    pallas_call x0 -> x26, Pallas kernels: none -> 23.1 us  [the longest x20 10.3 us: phi(): pl.pallas_call(functools.partial(phi_kernel, low, size, factor, len(extra...]
    ppermute x12 -> x24, starting transfers between devices: 21.2 us -> 26.3 us  [send(): return [lax.ppermute(value, 'depth', route) for value in values]]
    another operation x3 -> x0, other arithmetic: 4.27 us -> none  [the longest x1 1.73 us: local(): jnp.stack([jnp.dot(start.T, tangent_zero, preferred_element_type=jnp.floa...]
    unnamed x23 -> x50, local copies, waits for them, and re-layouts: 4.58 us -> 8.76 us
  transfers between devices with their start and end apart: 12 -> 24, of which waited for: 12 -> 4; matrix products, arithmetic and copies ran while one was open for 2% -> 0% of each run, Pallas kernels for 0% -> 16%
where the time goes in v1:
time: 109 us; the launch traced here: 108 us
  waiting for transfers between devices  46.2 us (42%)
  starting transfers between devices  26.3 us (24%)
  Pallas kernels  23.1 us (21%)
  local copies, waits for them, and re-layouts  10.6 us (10%)
  between operations  1.55 us (1%)
    ppermute x24, waiting for transfers between devices, send(): return [lax.ppermute(value, 'depth', route) for value in values]  46.2 us
    ppermute x24, starting transfers between devices, send(): return [lax.ppermute(value, 'depth', route) for value in values]  26.3 us
    pallas_call x20, Pallas kernels, phi(): pl.pallas_call(functools.partial(phi_kernel, low, size, factor, len(extra...  10.3 us
    unnamed x50, local copies, waits for them, and re-layouts  8.76 us
    pallas_call x1, Pallas kernels, local(): pl.pallas_call(functools.partial(grads_kernel, CHUNKS), out_shape=(jax.Sh...  4.53 us
    pallas_call x2, Pallas kernels, local(): pl.pallas_call(functools.partial(next_kernel, low, size), out_shape=(pltp...  3.58 us
    pallas_call x2, Pallas kernels, first(): pl.pallas_call(functools.partial(first_kernel, low, size), out_shape=(plt...  2.97 us
  transfers between devices with their start and end apart: 24, of which 4 were waited for; matrix products, arithmetic and copies ran while one was open for 0% of the time, Pallas kernels for 16%

profile of v1, /device:TPU:1, one launch (start us, length us, event | category | flops | bytes accessed | tf_op | source)
XLA Modules:
  0.0 107.8 jit_solution(5438707149025766951)
XLA Ops:
  0.6 1.9 %slice_bitcast_fusion = (f32[128,512]{1,0:T(8,128)}, f32[128,512]{1,0:T(8,128)}) fusion(f32[1,256,512]{2,1,0:T(8,128)} %refs_1_.3), kind=kLoop, calls=%fused_computation | loop fusion | bytes 1048576 | tf_op jit(solution)/shard_map/squeeze | solution.py:176
  2.5 1.9 %collective-permute-start = (f32[128,512]{1,0:T(8,128)}, f32[128,512]{1,0:T(8,128)}, u32[]{:S(2)}, u32[]{:S(2)}) collective-permute-start(f32[128,512]{1,0:T(8,128)} %get-tuple-element.52), channel_id=1, source_target_pairs={{1,0},{2,1},{3,2},{4,3},{5,4},{6,5},{7,6},{8,7},{9,8},{10,9},{11,1... | collective-permute-start | bytes 786440 | tf_op jit(solution)/shard_map/ppermute | solution.py:174
  4.4 1.9 %collective-permute-start.11 = (f32[128,512]{1,0:T(8,128)}, f32[128,512]{1,0:T(8,128)S(1)}, u32[]{:S(2)}, u32[]{:S(2)}) collective-permute-start(f32[128,512]{1,0:T(8,128)} %get-tuple-element.51), channel_id=1, source_target_pairs={{1,0},{2,1},{3,2},{4,3},{5,4},{6,5},{7,6},{8,7},{9,8},{10,9},{11,1... | collective-permute-start | bytes 786440 | tf_op jit(solution)/shard_map/ppermute | solution.py:174
  6.4 1.6 %copy-done.5 = bf16[2,512,1024]{2,1,0:T(8,128)(2,1)S(1)} copy-done((bf16[2,512,1024]{2,1,0:T(8,128)(2,1)S(1)}, bf16[2,512,1024]{2,1,0:T(8,128)(2,1)}, u32[]{:S(2)}) %copy-start.5) | copy-done | bytes 2097176
  8.0 1.6 %copy-done.6 = bf16[2,1024,512]{2,1,0:T(8,128)(2,1)S(1)} copy-done((bf16[2,1024,512]{2,1,0:T(8,128)(2,1)S(1)}, bf16[2,1024,512]{2,1,0:T(8,128)(2,1)}, u32[]{:S(2)}) %copy-start.6) | copy-done | bytes 2097176
  9.6 0.9 copy-done.16
  10.5 1.7 %forward.1 = (bf16[1024,512]{1,0:T(8,128)(2,1)S(1)}, bf16[1024,512]{1,0:T(8,128)(2,1)S(1)}, bf16[512,1024]{1,0:T(8,128)(2,1)S(1)}, bf16[512,1024]{1,0:T(8,128)(2...) custom-call(bf16[1,256,512]{2,1,0:T(8,128)(2,1)S(1)} %copy-done.16, ...), custom_call_target="tpu_custom_call" | custom-call | tf_op jit(solution)/shard_map/forward/pallas_call | solution.py:51
  12.3 2.1 %first.2 = (f32[128,512]{1,0:T(8,128)S(1)}, f32[128,512]{1,0:T(8,128)S(1)}) custom-call(s32[1]{0:T(128)} %bitcast.at_end, f32[128,512]{1,0:T(8,128)} %collective-permute-done.moved, f32[256,512]{1,0:T(8,128)S(1)} %copy-done.7, f32[1,256,512]{2,1,0:T(8,128)S(1)} %copy-done.4, bf16[1024,512]{1,0:T(8,128)(2,1)S(1)} %get-tuple-element.31.in_t0.in_t, ...), custom_call_target="tpu_custom_call" | custom-call | tf_op jit(solution)/shard_map/first/pallas_call | solution.py:181
  14.5 1.3 %collective-permute-start.1 = (f32[128,512]{1,0:T(8,128)S(1)}, f32[128,512]{1,0:T(8,128)S(1)}, u32[]{:S(2)}, u32[]{:S(2)}) collective-permute-start(f32[128,512]{1,0:T(8,128)S(1)} %get-tuple-element.37.refs_0_), channel_id=1, source_target_pairs={{1,0},{3,2},{5,4},{7,6},{9,8},{11,10},{13,12},{15,14},{17,16},{19,... | collective-permute-start | bytes 786440 | tf_op jit(solution)/shard_map/ppermute | solution.py:174
  15.8 0.9 first.3
  16.7 1.3 %collective-permute-start.12 = (f32[128,512]{1,0:T(8,128)S(1)}, f32[128,512]{1,0:T(8,128)S(1)}, u32[]{:S(2)}, u32[]{:S(2)}) collective-permute-start(f32[128,512]{1,0:T(8,128)S(1)} %get-tuple-element.38.refs_0_), channel_id=1, source_target_pairs={{1,0},{3,2},{5,4},{7,6},{9,8},{11,10},{13,12},{15,14},{17,16},{19,... | collective-permute-start | bytes 786440 | tf_op jit(solution)/shard_map/ppermute | solution.py:174
  18.5 1.3 %collective-permute-start.2 = (f32[128,512]{1,0:T(8,128)S(1)}, f32[128,512]{1,0:T(8,128)S(1)}, u32[]{:S(2)}, u32[]{:S(2)}) collective-permute-start(f32[128,512]{1,0:T(8,128)S(1)} %phi.20.refs_1_), channel_id=1, source_target_pairs={{2,1},{4,3},{6,5},{8,7},{10,9},{12,11},{14,13},{16,15},{18,17},{20... | collective-permute-start | bytes 786440 | tf_op jit(solution)/shard_map/ppermute | solution.py:174
  20.3 1.3 %collective-permute-start.13 = (f32[128,512]{1,0:T(8,128)S(1)}, f32[128,512]{1,0:T(8,128)S(1)}, u32[]{:S(2)}, u32[]{:S(2)}) collective-permute-start(f32[128,512]{1,0:T(8,128)S(1)} %phi.30.refs_1_), channel_id=1, source_target_pairs={{2,1},{4,3},{6,5},{8,7},{10,9},{12,11},{14,13},{16,15},{18,17},{20... | collective-permute-start | bytes 786440 | tf_op jit(solution)/shard_map/ppermute | solution.py:174
  21.6 4.8 %collective-permute-done.2.vector = f32[128,512]{1,0:T(8,128)S(1)} collective-permute-done((f32[128,512]{1,0:T(8,128)S(1)}, f32[128,512]{1,0:T(8,128)S(1)}, u32[]{:S(2)}, u32[]{:S(2)}) %collective-permute-start.2) | collective-permute-done | bytes 262176 | tf_op jit(solution)/shard_map/ppermute | solution.py:174
  26.9 1.3 %collective-permute-start.3 = (f32[128,512]{1,0:T(8,128)S(1)}, f32[128,512]{1,0:T(8,128)S(1)}, u32[]{:S(2)}, u32[]{:S(2)}) collective-permute-start(f32[128,512]{1,0:T(8,128)S(1)} %phi.21), channel_id=1, source_target_pairs={{1,0},{3,2},{5,4},{7,6},{9,8},{11,10},{13,12},{15,14},{17,16},{19,... | collective-permute-start | bytes 786440 | tf_op jit(solution)/shard_map/ppermute | solution.py:174
  28.2 1.0 collective-permute-done.13.vector
  29.7 1.3 %collective-permute-start.14 = (f32[128,512]{1,0:T(8,128)S(1)}, f32[128,512]{1,0:T(8,128)S(1)}, u32[]{:S(2)}, u32[]{:S(2)}) collective-permute-start(f32[128,512]{1,0:T(8,128)S(1)} %phi.31), channel_id=1, source_target_pairs={{1,0},{3,2},{5,4},{7,6},{9,8},{11,10},{13,12},{15,14},{17,16},{19,... | collective-permute-start | bytes 786440 | tf_op jit(solution)/shard_map/ppermute | solution.py:174
  31.5 0.7 collective-permute-start.4
  39.8 0.7 collective-permute-start.18
  45.7 1.3 %collective-permute-start.10 = (f32[128,512]{1,0:T(8,128)S(1)}, f32[128,512]{1,0:T(8,128)S(1)}, u32[]{:S(2)}, u32[]{:S(2)}) collective-permute-start(f32[128,512]{1,0:T(8,128)S(1)} %phi.28.refs_0_), channel_id=1, source_target_pairs={{2,1},{4,3},{6,5},{8,7},{10,9},{12,11},{14,13},{16,15},{18,17},{20... | collective-permute-start | bytes 786440 | tf_op jit(solution)/shard_map/ppermute | solution.py:174
  47.5 1.3 %collective-permute-start.21 = (f32[128,512]{1,0:T(8,128)S(1)}, f32[128,512]{1,0:T(8,128)S(1)}, u32[]{:S(2)}, u32[]{:S(2)}) collective-permute-start(f32[128,512]{1,0:T(8,128)S(1)} %phi.38.refs_0_), channel_id=1, source_target_pairs={{2,1},{4,3},{6,5},{8,7},{10,9},{12,11},{14,13},{16,15},{18,17},{20... | collective-permute-start | bytes 786440 | tf_op jit(solution)/shard_map/ppermute | solution.py:174
  48.8 40.3 %collective-permute-done.10.vector.received = f32[128,512]{1,0:T(8,128)S(1)} collective-permute-done((f32[128,512]{1,0:T(8,128)S(1)}, f32[128,512]{1,0:T(8,128)S(1)}, u32[]{:S(2)}, u32[]{:S(2)}) %collective-permute-start.10) | collective-permute-done | bytes 262176 | tf_op jit(solution)/shard_map/ppermute | solution.py:174
  89.7 2.0 %collective-permute-start.22 = (f32[128,512]{1,0:T(8,128)S(1)}, f32[128,512]{1,0:T(8,128)}, u32[]{:S(2)}, u32[]{:S(2)}) collective-permute-start(f32[128,512]{1,0:T(8,128)S(1)} %phi.29.refs_0_), channel_id=1, source_target_pairs={{1,0},{3,2},{5,4},{7,6},{9,8},{11,10},{13,12},{15,14},{17,16},{19,... | collective-permute-start | bytes 786440 | tf_op jit(solution)/shard_map/ppermute | solution.py:174
  91.9 1.2 %phi.39.refs_1_ = f32[128,512]{1,0:T(8,128)} custom-call(f32[128,512]{1,0:T(8,128)S(1)} %collective-permute-done.21.vector.received, bf16[1024,512]{1,0:T(8,128)(2,1)S(1)} %get-tuple-element.31.in_t0.in_t, bf16[512,1024]{1,0:T(8,128)(2,1)S(1)} %get-tuple-element.33.out_t0.out_t, f32[256,1024]{1,0:T(8,128)S(1)} %get-tuple-element.35.slope0.slope, ...), custom_call_target="tpu_custom_call" | custom-call | tf_op jit(solution)/shard_map/phi/pallas_call | solution.py:195
  93.1 2.0 %collective-permute-start.23 = (f32[128,512]{1,0:T(8,128)}, f32[128,512]{1,0:T(8,128)}, u32[]{:S(2)}, u32[]{:S(2)}) collective-permute-start(f32[128,512]{1,0:T(8,128)} %phi.39.refs_1_), channel_id=1, source_target_pairs={{1,0},{3,2},{5,4},{7,6},{9,8},{11,10},{13,12},{15,14},{17,16},{19,... | collective-permute-start | bytes 786440 | tf_op jit(solution)/shard_map/ppermute | solution.py:174
  95.1 1.2 %copy-done.1 = bf16[512,1024]{1,0:T(8,128)(2,1)S(1)} copy-done((bf16[512,1024]{1,0:T(8,128)(2,1)S(1)}, bf16[512,1024]{1,0:T(8,128)(2,1)}, u32[]{:S(2)}) %copy-start.1) | copy-done | bytes 1048600
  96.3 1.2 %copy-done.3 = f32[256,1024]{1,0:T(8,128)S(1)} copy-done((f32[256,1024]{1,0:T(8,128)S(1)}, f32[256,1024]{1,0:T(8,128)}, u32[]{:S(2)}) %copy-start.3) | copy-done | bytes 1048600
  97.5 0.9 copy-done.11
  98.5 0.9 copy-done.24
  99.4 1.8 %last.2 = (f32[128,512]{1,0:T(8,128)S(1)}, bf16[128,512]{1,0:T(8,128)(2,1)S(1)}, bf16[128,512]{1,0:T(8,128)(2,1)S(1)}, bf16[128,1024]{1,0:T(8,128)(2,1)S(1)}, bf16[128,1024]{1,0:T(8,128)(2,1)S(1)}) custom-call(s32[1]{0:T(128)} %bitcast.3.is_odd, f32[128,512]{1,0:T(8,128)S(1)} %copy-done.11, f32[128,512]{1,0:T(8,128)S(1)} %copy-done.24, ...), custom_call_target="tpu_custom_call" | custom-call | tf_op jit(solution)/shard_map/last/pallas_call | solution.py:231
  101.3 1.8 %last.3 = (f32[128,512]{1,0:T(8,128)S(1)}, bf16[128,512]{1,0:T(8,128)(2,1)S(1)}, bf16[128,512]{1,0:T(8,128)(2,1)S(1)}, bf16[128,1024]{1,0:T(8,128)(2,1)S(1)}, bf16[128,1024]{1,0:T(8,128)(2,1)S(1)}) custom-call(s32[1]{0:T(128)} %bitcast.3.is_odd, f32[128,512]{1,0:T(8,128)S(1)} %copy-done.9, f32[128,512]{1,0:T(8,128)S(1)} %copy-done.22, ...), custom_call_target="tpu_custom_call" | custom-call | tf_op jit(solution)/shard_map/last/pallas_call | solution.py:231
  103.1 4.5 %grads.1 = (f32[2,256,512]{2,1,0:T(8,128)}, bf16[2,512,1024]{2,1,0:T(8,128)(2,1)}, bf16[2,1024,512]{2,1,0:T(8,128)(2,1)}) custom-call(bf16[512,256]{1,0:T(8,128)(2,1)S(1)} %copy-done.18, bf16[512,256]{1,0:T(8,128)(2,1)S(1)} %copy-done.20, bf16[1024,256]{1,0:T(8,128)(2,1)S(1)} %copy-done.13, bf16[1024,256]{1,0:T(8,128)(2,1)S(1)} %copy-done.15, ...), custom_call_target="tpu_custom_call" | custom-call | tf_op jit(solution)/shard_map/grads/pallas_call | solution.py:257
  (93 shorter events, 16.3 us)
Async XLA Ops:
  2.5 9.8 %collective-permute-start = (f32[128,512]{1,0:T(8,128)}, f32[128,512]{1,0:T(8,128)}, u32[]{:S(2)}, u32[]{:S(2)}) collective-permute-start(f32[128,512]{1,0:T(8,128)} %get-tuple-element.52), channel_id=1, source_target_pairs={{1,0},{2,1},{3,2},{4,3},{5,4},{6,5},{7,6},{8,7},{9,8},{10,9},{11,1... | collective-permute-start | bytes 786440 | tf_op jit(solution)/shard_map/ppermute | solution.py:174
  4.4 11.3 %collective-permute-start.11 = (f32[128,512]{1,0:T(8,128)}, f32[128,512]{1,0:T(8,128)S(1)}, u32[]{:S(2)}, u32[]{:S(2)}) collective-permute-start(f32[128,512]{1,0:T(8,128)} %get-tuple-element.51), channel_id=1, source_target_pairs={{1,0},{2,1},{3,2},{4,3},{5,4},{6,5},{7,6},{8,7},{9,8},{10,9},{11,1... | collective-permute-start | bytes 786440 | tf_op jit(solution)/shard_map/ppermute | solution.py:174
  12.3 2.2 %copy-start.12 = (bf16[1024,256]{1,0:T(8,128)(2,1)}, bf16[1024,256]{1,0:T(8,128)(2,1)S(1)}, u32[]{:S(2)}) copy-start(bf16[1024,256]{1,0:T(8,128)(2,1)S(1)} %get-tuple-element.29.act_t0) | copy-start | bytes 1572868
  12.3 2.2 %copy-start.14 = (bf16[1024,256]{1,0:T(8,128)(2,1)}, bf16[1024,256]{1,0:T(8,128)(2,1)S(1)}, u32[]{:S(2)}) copy-start(bf16[1024,256]{1,0:T(8,128)(2,1)S(1)} %get-tuple-element.30.act_t1) | copy-start | bytes 1572868
  12.3 2.2 %copy-start.17 = (bf16[512,256]{1,0:T(8,128)(2,1)}, bf16[512,256]{1,0:T(8,128)(2,1)S(1)}, u32[]{:S(2)}) copy-start(bf16[512,256]{1,0:T(8,128)(2,1)S(1)} %get-tuple-element.27.start_t) | copy-start | bytes 786436
  12.3 2.2 %copy-start.19 = (bf16[512,256]{1,0:T(8,128)(2,1)}, bf16[512,256]{1,0:T(8,128)(2,1)S(1)}, u32[]{:S(2)}) copy-start(bf16[512,256]{1,0:T(8,128)(2,1)S(1)} %get-tuple-element.28.upper_t) | copy-start | bytes 786436
  12.3 3.5 %copy-start = (bf16[512,1024]{1,0:T(8,128)(2,1)}, bf16[512,1024]{1,0:T(8,128)(2,1)S(1)}, u32[]{:S(2)}) copy-start(bf16[512,1024]{1,0:T(8,128)(2,1)S(1)} %get-tuple-element.34.out_t1) | copy-start | bytes 3145732
  12.3 3.5 %copy-start.2 = (f32[256,1024]{1,0:T(8,128)}, f32[256,1024]{1,0:T(8,128)S(1)}, u32[]{:S(2)}) copy-start(f32[256,1024]{1,0:T(8,128)S(1)} %get-tuple-element.36.slope1) | copy-start | bytes 3145732
  14.4 2.3 %copy-start.23 = (f32[128,512]{1,0:T(8,128)}, f32[128,512]{1,0:T(8,128)S(1)}, u32[]{:S(2)}) copy-start(f32[128,512]{1,0:T(8,128)S(1)} %get-tuple-element.39.above) | copy-start | bytes 786436
  14.5 3.6 %collective-permute-start.1 = (f32[128,512]{1,0:T(8,128)S(1)}, f32[128,512]{1,0:T(8,128)S(1)}, u32[]{:S(2)}, u32[]{:S(2)}) collective-permute-start(f32[128,512]{1,0:T(8,128)S(1)} %get-tuple-element.37.refs_0_), channel_id=1, source_target_pairs={{1,0},{3,2},{5,4},{7,6},{9,8},{11,10},{13,12},{15,14},{17,16},{19,... | collective-permute-start | bytes 786440 | tf_op jit(solution)/shard_map/ppermute | solution.py:174
  16.7 3.6 %copy-start.21 = (f32[128,512]{1,0:T(8,128)}, f32[128,512]{1,0:T(8,128)S(1)}, u32[]{:S(2)}) copy-start(f32[128,512]{1,0:T(8,128)S(1)} %get-tuple-element.41.above) | copy-start | bytes 786436
  16.7 3.1 %collective-permute-start.12 = (f32[128,512]{1,0:T(8,128)S(1)}, f32[128,512]{1,0:T(8,128)S(1)}, u32[]{:S(2)}, u32[]{:S(2)}) collective-permute-start(f32[128,512]{1,0:T(8,128)S(1)} %get-tuple-element.38.refs_0_), channel_id=1, source_target_pairs={{1,0},{3,2},{5,4},{7,6},{9,8},{11,10},{13,12},{15,14},{17,16},{19,... | collective-permute-start | bytes 786440 | tf_op jit(solution)/shard_map/ppermute | solution.py:174
  18.5 7.9 %collective-permute-start.2 = (f32[128,512]{1,0:T(8,128)S(1)}, f32[128,512]{1,0:T(8,128)S(1)}, u32[]{:S(2)}, u32[]{:S(2)}) collective-permute-start(f32[128,512]{1,0:T(8,128)S(1)} %phi.20.refs_1_), channel_id=1, source_target_pairs={{2,1},{4,3},{6,5},{8,7},{10,9},{12,11},{14,13},{16,15},{18,17},{20... | collective-permute-start | bytes 786440 | tf_op jit(solution)/shard_map/ppermute | solution.py:174
  20.3 8.9 %collective-permute-start.13 = (f32[128,512]{1,0:T(8,128)S(1)}, f32[128,512]{1,0:T(8,128)S(1)}, u32[]{:S(2)}, u32[]{:S(2)}) collective-permute-start(f32[128,512]{1,0:T(8,128)S(1)} %phi.30.refs_1_), channel_id=1, source_target_pairs={{2,1},{4,3},{6,5},{8,7},{10,9},{12,11},{14,13},{16,15},{18,17},{20... | collective-permute-start | bytes 786440 | tf_op jit(solution)/shard_map/ppermute | solution.py:174
  26.9 4.1 %collective-permute-start.3 = (f32[128,512]{1,0:T(8,128)S(1)}, f32[128,512]{1,0:T(8,128)S(1)}, u32[]{:S(2)}, u32[]{:S(2)}) collective-permute-start(f32[128,512]{1,0:T(8,128)S(1)} %phi.21), channel_id=1, source_target_pairs={{1,0},{3,2},{5,4},{7,6},{9,8},{11,10},{13,12},{15,14},{17,16},{19,... | collective-permute-start | bytes 786440 | tf_op jit(solution)/shard_map/ppermute | solution.py:174
  29.7 2.5 %collective-permute-start.14 = (f32[128,512]{1,0:T(8,128)S(1)}, f32[128,512]{1,0:T(8,128)S(1)}, u32[]{:S(2)}, u32[]{:S(2)}) collective-permute-start(f32[128,512]{1,0:T(8,128)S(1)} %phi.31), channel_id=1, source_target_pairs={{1,0},{3,2},{5,4},{7,6},{9,8},{11,10},{13,12},{15,14},{17,16},{19,... | collective-permute-start | bytes 786440 | tf_op jit(solution)/shard_map/ppermute | solution.py:174
  31.5 1.9 %collective-permute-start.4 = (f32[128,512]{1,0:T(8,128)S(1)}, f32[128,512]{1,0:T(8,128)S(1)}, u32[]{:S(2)}, u32[]{:S(2)}) collective-permute-start(f32[128,512]{1,0:T(8,128)S(1)} %phi.22.refs_0_), channel_id=1, source_target_pairs={{2,0},{6,4},{10,8},{14,12},{18,16},{22,20},{26,24},{30,28}} | collective-permute-start | bytes 786440 | tf_op jit(solution)/shard_map/ppermute | solution.py:174
  32.7 1.9 %collective-permute-start.15 = (f32[128,512]{1,0:T(8,128)S(1)}, f32[128,512]{1,0:T(8,128)S(1)}, u32[]{:S(2)}, u32[]{:S(2)}) collective-permute-start(f32[128,512]{1,0:T(8,128)S(1)} %phi.32.refs_0_), channel_id=1, source_target_pairs={{2,0},{6,4},{10,8},{14,12},{18,16},{22,20},{26,24},{30,28}} | collective-permute-start | bytes 786440 | tf_op jit(solution)/shard_map/ppermute | solution.py:174
  33.9 1.9 %collective-permute-start.5 = (f32[128,512]{1,0:T(8,128)S(1)}, f32[128,512]{1,0:T(8,128)S(1)}, u32[]{:S(2)}, u32[]{:S(2)}) collective-permute-start(f32[128,512]{1,0:T(8,128)S(1)} %phi.23.refs_1_), channel_id=1, source_target_pairs={{4,2},{8,6},{12,10},{16,14},{20,18},{24,22},{28,26}} | collective-permute-start | bytes 786440 | tf_op jit(solution)/shard_map/ppermute | solution.py:174
  35.1 1.9 %collective-permute-start.16 = (f32[128,512]{1,0:T(8,128)S(1)}, f32[128,512]{1,0:T(8,128)S(1)}, u32[]{:S(2)}, u32[]{:S(2)}) collective-permute-start(f32[128,512]{1,0:T(8,128)S(1)} %phi.33.refs_1_), channel_id=1, source_target_pairs={{4,2},{8,6},{12,10},{16,14},{20,18},{24,22},{28,26}} | collective-permute-start | bytes 786440 | tf_op jit(solution)/shard_map/ppermute | solution.py:174
  36.2 1.9 %collective-permute-start.6 = (f32[128,512]{1,0:T(8,128)S(1)}, f32[128,512]{1,0:T(8,128)S(1)}, u32[]{:S(2)}, u32[]{:S(2)}) collective-permute-start(f32[128,512]{1,0:T(8,128)S(1)} %phi.24), channel_id=1, source_target_pairs={{2,0},{6,4},{10,8},{14,12},{18,16},{22,20},{26,24},{30,28}} | collective-permute-start | bytes 786440 | tf_op jit(solution)/shard_map/ppermute | solution.py:174
  37.4 1.9 %collective-permute-start.17 = (f32[128,512]{1,0:T(8,128)S(1)}, f32[128,512]{1,0:T(8,128)S(1)}, u32[]{:S(2)}, u32[]{:S(2)}) collective-permute-start(f32[128,512]{1,0:T(8,128)S(1)} %phi.34), channel_id=1, source_target_pairs={{2,0},{6,4},{10,8},{14,12},{18,16},{22,20},{26,24},{30,28}} | collective-permute-start | bytes 786440 | tf_op jit(solution)/shard_map/ppermute | solution.py:174
  38.6 1.9 %collective-permute-start.7 = (f32[128,512]{1,0:T(8,128)S(1)}, f32[128,512]{1,0:T(8,128)S(1)}, u32[]{:S(2)}, u32[]{:S(2)}) collective-permute-start(f32[128,512]{1,0:T(8,128)S(1)} %phi.25.refs_0_), channel_id=1, source_target_pairs={{4,0},{12,8},{20,16},{28,24}} | collective-permute-start | bytes 786440 | tf_op jit(solution)/shard_map/ppermute | solution.py:174
  39.8 1.9 %collective-permute-start.18 = (f32[128,512]{1,0:T(8,128)S(1)}, f32[128,512]{1,0:T(8,128)S(1)}, u32[]{:S(2)}, u32[]{:S(2)}) collective-permute-start(f32[128,512]{1,0:T(8,128)S(1)} %phi.35.refs_0_), channel_id=1, source_target_pairs={{4,0},{12,8},{20,16},{28,24}} | collective-permute-start | bytes 786440 | tf_op jit(solution)/shard_map/ppermute | solution.py:174
  40.9 1.9 %collective-permute-start.8 = (f32[128,512]{1,0:T(8,128)S(1)}, f32[128,512]{1,0:T(8,128)S(1)}, u32[]{:S(2)}, u32[]{:S(2)}) collective-permute-start(f32[128,512]{1,0:T(8,128)S(1)} %phi.26.refs_0_), channel_id=1, source_target_pairs={{8,4},{16,12},{24,20}} | collective-permute-start | bytes 786440 | tf_op jit(solution)/shard_map/ppermute | solution.py:174
  42.1 1.9 %collective-permute-start.19 = (f32[128,512]{1,0:T(8,128)S(1)}, f32[128,512]{1,0:T(8,128)S(1)}, u32[]{:S(2)}, u32[]{:S(2)}) collective-permute-start(f32[128,512]{1,0:T(8,128)S(1)} %phi.36.refs_0_), channel_id=1, source_target_pairs={{8,4},{16,12},{24,20}} | collective-permute-start | bytes 786440 | tf_op jit(solution)/shard_map/ppermute | solution.py:174
  43.3 1.9 %collective-permute-start.9 = (f32[128,512]{1,0:T(8,128)S(1)}, f32[128,512]{1,0:T(8,128)S(1)}, u32[]{:S(2)}, u32[]{:S(2)}) collective-permute-start(f32[128,512]{1,0:T(8,128)S(1)} %phi.27.refs_0_), channel_id=1, source_target_pairs={{4,2},{8,6},{12,10},{16,14},{20,18},{24,22},{28,26}} | collective-permute-start | bytes 786440 | tf_op jit(solution)/shard_map/ppermute | solution.py:174
  44.5 2.5 %collective-permute-start.20 = (f32[128,512]{1,0:T(8,128)S(1)}, f32[128,512]{1,0:T(8,128)S(1)}, u32[]{:S(2)}, u32[]{:S(2)}) collective-permute-start(f32[128,512]{1,0:T(8,128)S(1)} %phi.37.refs_0_), channel_id=1, source_target_pairs={{4,2},{8,6},{12,10},{16,14},{20,18},{24,22},{28,26}} | collective-permute-start | bytes 786440 | tf_op jit(solution)/shard_map/ppermute | solution.py:174
  45.7 43.4 %collective-permute-start.10 = (f32[128,512]{1,0:T(8,128)S(1)}, f32[128,512]{1,0:T(8,128)S(1)}, u32[]{:S(2)}, u32[]{:S(2)}) collective-permute-start(f32[128,512]{1,0:T(8,128)S(1)} %phi.28.refs_0_), channel_id=1, source_target_pairs={{2,1},{4,3},{6,5},{8,7},{10,9},{12,11},{14,13},{16,15},{18,17},{20... | collective-permute-start | bytes 786440 | tf_op jit(solution)/shard_map/ppermute | solution.py:174
  47.5 44.4 %collective-permute-start.21 = (f32[128,512]{1,0:T(8,128)S(1)}, f32[128,512]{1,0:T(8,128)S(1)}, u32[]{:S(2)}, u32[]{:S(2)}) collective-permute-start(f32[128,512]{1,0:T(8,128)S(1)} %phi.38.refs_0_), channel_id=1, source_target_pairs={{2,1},{4,3},{6,5},{8,7},{10,9},{12,11},{14,13},{16,15},{18,17},{20... | collective-permute-start | bytes 786440 | tf_op jit(solution)/shard_map/ppermute | solution.py:174
  89.7 5.3 %collective-permute-start.22 = (f32[128,512]{1,0:T(8,128)S(1)}, f32[128,512]{1,0:T(8,128)}, u32[]{:S(2)}, u32[]{:S(2)}) collective-permute-start(f32[128,512]{1,0:T(8,128)S(1)} %phi.29.refs_0_), channel_id=1, source_target_pairs={{1,0},{3,2},{5,4},{7,6},{9,8},{11,10},{13,12},{15,14},{17,16},{19,... | collective-permute-start | bytes 786440 | tf_op jit(solution)/shard_map/ppermute | solution.py:174
  93.1 8.1 %collective-permute-start.23 = (f32[128,512]{1,0:T(8,128)}, f32[128,512]{1,0:T(8,128)}, u32[]{:S(2)}, u32[]{:S(2)}) collective-permute-start(f32[128,512]{1,0:T(8,128)} %phi.39.refs_1_), channel_id=1, source_target_pairs={{1,0},{3,2},{5,4},{7,6},{9,8},{11,10},{13,12},{15,14},{17,16},{19,... | collective-permute-start | bytes 786440 | tf_op jit(solution)/shard_map/ppermute | solution.py:174
  (17 other events, 25.1 us)

commit v2 on v1

v2 whole, which is shorter than its diff:
```python
import functools

import jax
import jax.numpy as jnp
from jax import lax
from jax.experimental import pallas as pl
from jax.experimental.pallas import tpu as pltpu
from jax.sharding import PartitionSpec as P

LEVELS = 4
CHUNKS = 2
F32, BF16 = jnp.float32, jnp.bfloat16
VMEM = pl.BlockSpec(memory_space=pltpu.VMEM)
SMEM = pl.BlockSpec(memory_space=pltpu.SMEM)
ANY = pl.BlockSpec(memory_space=pl.ANY)


def dot(a, b):
    return jnp.dot(a, b, preferred_element_type=F32)


def held(value):
    return pltpu.with_memory_space_constraint(value, pltpu.VMEM)


def params(mib):
    return pltpu.CompilerParams(vmem_limit_bytes=mib * 2**20)


def forward_kernel(
    start_h, w_in_h, w_out_h, in_t, out_t, slope, state_t, act_t, start, w_in, w_out, sems
):
    copies = [
        pltpu.make_async_copy(source, target, sems.at[i])
        for i, (source, target) in enumerate(
            [
                (start_h.at[0], start),
                (w_in_h.at[0], w_in.at[0]),
                (w_out_h.at[0], w_out.at[0]),
                (w_in_h.at[1], w_in.at[1]),
                (w_out_h.at[1], w_out.at[1]),
            ]
        )
    ]
    for copy in copies:
        copy.start()
    copies[0].wait()
    copies[1].wait()
    first = start[...]
    h_zero = jnp.tanh(dot(first, w_in[0]))
    slope[0] = 1.0 - h_zero * h_zero
    act_zero = h_zero.astype(BF16)
    in_t[0] = w_in[0].T
    copies[2].wait()
    upper = (first.astype(F32) + dot(act_zero, w_out[0])).astype(BF16)
    copies[3].wait()
    h_one = jnp.tanh(dot(upper, w_in[1]))
    slope[1] = 1.0 - h_one * h_one
    out_t[0] = w_out[0].T
    in_t[1] = w_in[1].T
    state_t[0] = first.T
    state_t[1] = upper.T
    act_t[0] = act_zero.T
    act_t[1] = h_one.astype(BF16).T
    copies[4].wait()
    out_t[1] = w_out[1].T


def forward(start, w_in, w_out):
    _, rows, d = start.shape
    ff = w_in.shape[2]
    return pl.pallas_call(
        forward_kernel,
        out_shape=(
            pltpu.VMEM((2, ff, d), BF16),
            pltpu.VMEM((2, d, ff), BF16),
            pltpu.VMEM((2, rows, ff), F32),
            pltpu.VMEM((2, d, rows), BF16),
            pltpu.VMEM((2, ff, rows), BF16),
        ),
        in_specs=[ANY] * 3,
        out_specs=[VMEM] * 5,
        scratch_shapes=[
            pltpu.VMEM((rows, d), BF16),
            pltpu.VMEM((2, d, ff), BF16),
            pltpu.VMEM((2, ff, d), BF16),
            pltpu.SemaphoreType.DMA((5,)),
        ],
        compiler_params=params(24),
        name="forward",
    )(*[pltpu.with_memory_space_constraint(v, pltpu.HBM) for v in (start, w_in, w_out)])


def tangent(vector, out_t, slope):
    return (dot(vector.astype(BF16), out_t) * slope).astype(BF16)


def first_kernel(low, size, moved, terminal, guess, in_t, out_t, slope, above, resid):
    rows = pl.ds(low, size)
    at_end = lax.axis_index("depth") == lax.axis_size("depth") - 1

    @pl.when(at_end)
    def _():
        above[...] = terminal[rows, :]

    @pl.when(jnp.logical_not(at_end))
    def _():
        above[...] = moved[rows, :]

    value = above[...]
    odd = value + dot(tangent(value, out_t[1], slope[1, rows, :]), in_t[1])
    even = odd + dot(tangent(odd, out_t[0], slope[0, rows, :]), in_t[0])
    resid[...] = even - guess[0, rows, :]


def phi_kernel(low, size, factor, period, phase, count, vector, in_t, out_t, slope, state_t, act_t, above, *refs):
    result = refs[count]
    terms = [a[...] if len(a.shape) == 2 else a[0, pl.ds(low, size), :] for a in refs[:count]]
    active = lax.rem(lax.axis_index("depth"), period) == phase

    @pl.when(active)
    def _():
        value = vector[...]
        total = value + factor * dot(tangent(value, out_t[0], slope[0, pl.ds(low, size), :]), in_t[0])
        for term in terms:
            total += term
        result[...] = total

    @pl.when(jnp.logical_not(active))
    def _():
        total = jnp.zeros(result.shape, F32)
        for term in terms:
            total += term
        result[...] = total


def next_kernel(low, size, received, above, arrived, in_t, out_t, slope, state_t, act_t, odd, above_b, odd_b, tan):
    relax_last(low, size, received, above, arrived, in_t, out_t, slope, odd, above_b, odd_b, tan)


def relax_last(low, size, received, above, arrived, in_t, out_t, slope, odd, above_b, odd_b, tan):
    rows = pl.ds(low, size)
    is_odd = lax.rem(lax.axis_index("depth"), 2) == 1

    @pl.when(is_odd)
    def _():
        odd[...] = above[...] + received[...]

    @pl.when(jnp.logical_not(is_odd))
    def _():
        odd[...] = arrived[...]

    nxt = odd[...]
    above_b[...] = nxt.astype(BF16)
    tan_one = tangent(nxt, out_t[1], slope[1, rows, :])
    tan[1] = tan_one
    value = nxt + dot(tan_one, in_t[1])
    odd[...] = value
    odd_b[...] = value.astype(BF16)
    tan[0] = tangent(value, out_t[0], slope[0, rows, :])


def grads_kernel(lows, *refs):
    chunks = len(lows)
    state_t, act_t = refs[:2]
    even, odd, above_b, odd_b, tan = [refs[2 + i * chunks : 2 + (i + 1) * chunks] for i in range(5)]
    adjoint, grad_in, grad_out, grad_in_v, grad_out_v, sems = refs[2 + 5 * chunks :]
    copies = []

    def send(source, target):
        copy = pltpu.make_async_copy(source, target, sems.at[len(copies)])
        copy.start()
        copies.append(copy)

    for part, low in enumerate(lows):
        size = even[part].shape[0]
        send(even[part], adjoint.at[0, pl.ds(low, size), :])
        send(odd[part], adjoint.at[1, pl.ds(low, size), :])

    def joined(values):
        return jnp.concatenate([value[...] for value in values], 0)

    def layer(i, vectors, tangents):
        grad_out_v[i] = dot(act_t[i], joined(vectors)).astype(BF16)
        send(grad_out_v.at[i], grad_out.at[i])
        grad_in_v[i] = dot(state_t[i], joined(tangents)).astype(BF16)
        send(grad_in_v.at[i], grad_in.at[i])

    layer(1, above_b, [value.at[1] for value in tan])
    layer(0, odd_b, [value.at[0] for value in tan])
    for copy in copies:
        copy.wait()


def local(w_in, w_out, checkpoint, guess, terminal):
    count = lax.axis_size("depth")
    rows, d = terminal.shape
    ff = w_in.shape[2]
    sizes = [rows * (i + 1) // CHUNKS // 16 * 16 - rows * i // CHUNKS // 16 * 16 for i in range(CHUNKS)]
    lows = [sum(sizes[:i]) for i in range(CHUNKS)]

    def send(values, period, phase, distance):
        route = [(i, i - distance) for i in range(count) if i % period == phase and i >= distance]
        return [held(lax.ppermute(value, "depth", route)) for value in values]

    (moved,) = send([guess.reshape(rows, d)], 1, 0, 1)
    weights = list(map(held, forward(checkpoint, w_in, w_out)))
    in_t, out_t, slope, state_t, act_t = weights

    def first(low, size):
        return pl.pallas_call(
            functools.partial(first_kernel, low, size),
            out_shape=(pltpu.VMEM((size, d), F32), pltpu.VMEM((size, d), F32)),
            in_specs=[VMEM] * 6,
            out_specs=[VMEM] * 2,
            compiler_params=params(16),
            name="first",
        )(moved, held(terminal), held(guess), in_t, out_t, slope)

    firsts = [first(low, size) for low, size in zip(lows, sizes)]
    above = [held(pair[0]) for pair in firsts]

    def phi(values, factor, period, phase, *addends):
        results = []
        for part, (low, size) in enumerate(zip(lows, sizes)):
            extra = [a[part] if isinstance(a, list) else a for a in addends]
            results.append(
                held(
                    pl.pallas_call(
                        functools.partial(phi_kernel, low, size, factor, period, phase, len(extra)),
                        out_shape=pltpu.VMEM((size, d), F32),
                        in_specs=[VMEM] * (7 + len(extra)),
                        out_specs=VMEM,
                        compiler_params=params(16),
                        name="phi",
                    )(values[part], *weights, above[part], *extra)
                )
            )
        return results

    def cycle(level, rhs, addend):
        distance = 2 ** (level - 1)
        period, factor = 2 * distance, float(2**level)

        def even(values, *addends):
            return phi(send(values, period, distance, distance), factor, period, 0, *addends)

        values = even(rhs, rhs)
        if level < LEVELS - 1:
            resid = even(phi(send(values, period, 0, distance), factor, period, distance))
            values, _ = cycle(level + 1, resid, values)
        received = send(values, period, 0, distance)
        return phi(received, factor, period, distance, values, addend), received

    even, received = cycle(1, [held(pair[1]) for pair in firsts], held(guess))
    arrived = send(even, 2, 1, 1)

    lasts = []
    for part, (low, size) in enumerate(zip(lows, sizes)):
        lasts.append(
            pl.pallas_call(
                functools.partial(next_kernel, low, size),
                out_shape=(
                    pltpu.VMEM((size, d), F32),
                    pltpu.VMEM((size, d), BF16),
                    pltpu.VMEM((size, d), BF16),
                    pltpu.VMEM((2, size, ff), BF16),
                ),
                in_specs=[VMEM] * 8,
                out_specs=[VMEM] * 4,
                compiler_params=params(16),
                name="last",
            )(received[part], above[part], arrived[part], *weights)
        )
    groups = [even] + [[held(last[i]) for last in lasts] for i in range(4)]
    return pl.pallas_call(
        functools.partial(grads_kernel, lows),
        out_shape=(
            jax.ShapeDtypeStruct((2, rows, d), F32),
            jax.ShapeDtypeStruct((2, d, ff), BF16),
            jax.ShapeDtypeStruct((2, ff, d), BF16),
        ),
        in_specs=[VMEM] * (2 + 5 * CHUNKS),
        out_specs=[ANY] * 3,
        scratch_shapes=[
            pltpu.VMEM((2, d, ff), BF16),
            pltpu.VMEM((2, ff, d), BF16),
            pltpu.SemaphoreType.DMA((2 * CHUNKS + 4,)),
        ],
        compiler_params=params(24),
        name="grads",
    )(state_t, act_t, *[value for group in groups for value in group])


def solution(mesh):
    split = P("depth", None, None)
    return jax.shard_map(
        local,
        mesh=mesh,
        in_specs=(split, split, split, split, P()),
        out_specs=(split, split, split),
        check_vma=False,
    )
```

time: 109 us -> 95.8 us (0.88)
  waiting for transfers between devices: 46.2 us -> 57.9 us
  Pallas kernels: 23.1 us -> 12.3 us
  local copies, waits for them, and re-layouts: 10.6 us -> 0.01 us
  starting transfers between devices: 26.3 us -> 23.4 us
    ppermute x24 -> x23, waiting for transfers between devices: 46.2 us -> 57.9 us  [send(): return [held(lax.ppermute(value, 'depth', route)) for value in values]]
    unnamed x50 -> x4, local copies, waits for them, and re-layouts: 8.76 us -> 0.01 us
    pallas_call x22, Pallas kernels: 16.5 us -> 8.98 us  [the longest x1 3.69 us: forward(): pl.pallas_call(forward_kernel, out_shape=(pltpu.VMEM((2, ff, d), BF16), p...]
    ppermute x24 -> x23, starting transfers between devices: 26.3 us -> 23.4 us  [send(): return [held(lax.ppermute(value, 'depth', route)) for value in values]]
    pallas_call x2, Pallas kernels: 3.58 us -> 1.54 us  [local(): pl.pallas_call(functools.partial(next_kernel, low, size), out_shape=(pltp...]
    squeeze x1 -> x0, local copies, waits for them, and re-layouts: 1.88 us -> none  [local(): moved = send([guess[0, low:low + size] for low in lows], 1, 0, 1)]
    pallas_call x2, Pallas kernels: 2.97 us -> 1.82 us  [first(): pl.pallas_call(functools.partial(first_kernel, low, size), out_shape=(plt...]
  transfers between devices with their start and end apart: 24 -> 23, of which waited for: 4 -> 7; matrix products, arithmetic and copies ran while one was open for 0% -> 0% of each run, Pallas kernels for 16% -> 8%
where the time goes in v2:
time: 95.8 us; the launch traced here: 94.9 us
  waiting for transfers between devices  57.9 us (60%)
  starting transfers between devices  23.4 us (24%)
  Pallas kernels  12.3 us (13%)
  between operations  1.31 us (1%)
    ppermute x23, waiting for transfers between devices, send(): return [held(lax.ppermute(value, 'depth', route)) for value in values]  57.9 us
    ppermute x23, starting transfers between devices, send(): return [held(lax.ppermute(value, 'depth', route)) for value in values]  23.4 us
    pallas_call x1, Pallas kernels, forward(): pl.pallas_call(forward_kernel, out_shape=(pltpu.VMEM((2, ff, d), BF16), p...  3.69 us
    pallas_call x20, Pallas kernels, phi(): pl.pallas_call(functools.partial(phi_kernel, low, size, factor, period, p...  2.67 us
    pallas_call x1, Pallas kernels, local(): pl.pallas_call(functools.partial(grads_kernel, lows), out_shape=(jax.Shap...  2.63 us
  transfers between devices with their start and end apart: 23, of which 7 were waited for; matrix products, arithmetic and copies ran while one was open for 0% of the time, Pallas kernels for 8%

profile of v2, /device:TPU:1, one launch (start us, length us, event | category | flops | bytes accessed | tf_op | source)
XLA Modules:
  0.0 94.9 jit_solution(14494047187452080024)
XLA Ops:
  0.7 2.1 %collective-permute-start = (f32[256,512]{1,0:T(8,128)}, f32[256,512]{1,0:T(8,128)S(1)}, u32[]{:S(2)}, u32[]{:S(2)}) collective-permute-start(f32[256,512]{1,0:T(8,128)} %bitcast.1), channel_id=1, source_target_pairs={{1,0},{2,1},{3,2},{4,3},{5,4},{6,5},{7,6},{8,7},{9,8},{10,9},{11,1... | collective-permute-start | bytes 1572872 | tf_op jit(solution)/shard_map/ppermute | solution.py:204
  2.7 3.7 %forward.1 = (bf16[2,1024,512]{2,1,0:T(8,128)(2,1)S(1)}, bf16[2,512,1024]{2,1,0:T(8,128)(2,1)S(1)}, f32[2,256,1024]{2,1,0:T(8,128)S(1)}, bf16[2,512,256]{2,1,0:T(8,128)(2,1)S(1)}, bf16[2,1024,256]{2,1,0:T(8,128)(2,1)S(1)}) custom-call(bf16[1,256,512]{2,1,0:T(8,128)(2,1)} %start_h.1, bf16[2,512,1024]{2,1,0:T(8,128)(2,1)} %w_in_h.1, bf16[2,1024,512]{2,1,0:T(8,128)(2,1)} %w_out_h.1), custom_call_target="tpu_custom_call" | custom-call | tf_op jit(solution)/shard_map/forward/pallas_call | solution.py:72
  6.4 5.9 %collective-permute-done.moved = f32[256,512]{1,0:T(8,128)S(1)} collective-permute-done((f32[256,512]{1,0:T(8,128)}, f32[256,512]{1,0:T(8,128)S(1)}, u32[]{:S(2)}, u32[]{:S(2)}) %collective-permute-start) | collective-permute-done | bytes 524320 | tf_op jit(solution)/shard_map/ppermute | solution.py:204
  12.4 0.9 first.2
  13.3 1.3 %collective-permute-start.1 = (f32[128,512]{1,0:T(8,128)S(1)}, f32[128,512]{1,0:T(8,128)S(1)}, u32[]{:S(2)}, u32[]{:S(2)}) collective-permute-start(f32[128,512]{1,0:T(8,128)S(1)} %get-tuple-element.25.refs_0_), channel_id=1, source_target_pairs={{1,0},{3,2},{5,4},{7,6},{9,8},{11,10},{13,12},{15,14},{17,16},{19,... | collective-permute-start | bytes 786440 | tf_op jit(solution)/shard_map/ppermute | solution.py:204
  14.6 0.9 first.3
  15.5 1.3 %collective-permute-start.11 = (f32[128,512]{1,0:T(8,128)S(1)}, f32[128,512]{1,0:T(8,128)S(1)}, u32[]{:S(2)}, u32[]{:S(2)}) collective-permute-start(f32[128,512]{1,0:T(8,128)S(1)} %get-tuple-element.27.refs_0_), channel_id=1, source_target_pairs={{1,0},{3,2},{5,4},{7,6},{9,8},{11,10},{13,12},{15,14},{17,16},{19,... | collective-permute-start | bytes 786440 | tf_op jit(solution)/shard_map/ppermute | solution.py:204
  16.9 1.3 %collective-permute-start.2 = (f32[128,512]{1,0:T(8,128)S(1)}, f32[128,512]{1,0:T(8,128)S(1)}, u32[]{:S(2)}, u32[]{:S(2)}) collective-permute-start(f32[128,512]{1,0:T(8,128)S(1)} %phi.20.refs_1_), channel_id=1, source_target_pairs={{2,1},{4,3},{6,5},{8,7},{10,9},{12,11},{14,13},{16,15},{18,17},{20... | collective-permute-start | bytes 786440 | tf_op jit(solution)/shard_map/ppermute | solution.py:204
  18.2 1.3 %collective-permute-start.12 = (f32[128,512]{1,0:T(8,128)S(1)}, f32[128,512]{1,0:T(8,128)S(1)}, u32[]{:S(2)}, u32[]{:S(2)}) collective-permute-start(f32[128,512]{1,0:T(8,128)S(1)} %phi.30.refs_1_), channel_id=1, source_target_pairs={{2,1},{4,3},{6,5},{8,7},{10,9},{12,11},{14,13},{16,15},{18,17},{20... | collective-permute-start | bytes 786440 | tf_op jit(solution)/shard_map/ppermute | solution.py:204
  19.5 5.0 %collective-permute-done.2.vector = f32[128,512]{1,0:T(8,128)S(1)} collective-permute-done((f32[128,512]{1,0:T(8,128)S(1)}, f32[128,512]{1,0:T(8,128)S(1)}, u32[]{:S(2)}, u32[]{:S(2)}) %collective-permute-start.2) | collective-permute-done | bytes 262176 | tf_op jit(solution)/shard_map/ppermute | solution.py:204
  25.1 1.3 %collective-permute-start.3 = (f32[128,512]{1,0:T(8,128)S(1)}, f32[128,512]{1,0:T(8,128)S(1)}, u32[]{:S(2)}, u32[]{:S(2)}) collective-permute-start(f32[128,512]{1,0:T(8,128)S(1)} %phi.21), channel_id=1, source_target_pairs={{1,0},{3,2},{5,4},{7,6},{9,8},{11,10},{13,12},{15,14},{17,16},{19,... | collective-permute-start | bytes 786440 | tf_op jit(solution)/shard_map/ppermute | solution.py:204
  26.4 1.0 %collective-permute-done.12.vector = f32[128,512]{1,0:T(8,128)S(1)} collective-permute-done((f32[128,512]{1,0:T(8,128)S(1)}, f32[128,512]{1,0:T(8,128)S(1)}, u32[]{:S(2)}, u32[]{:S(2)}) %collective-permute-start.12) | collective-permute-done | bytes 262176 | tf_op jit(solution)/shard_map/ppermute | solution.py:204
  27.9 1.3 %collective-permute-start.13 = (f32[128,512]{1,0:T(8,128)S(1)}, f32[128,512]{1,0:T(8,128)S(1)}, u32[]{:S(2)}, u32[]{:S(2)}) collective-permute-start(f32[128,512]{1,0:T(8,128)S(1)} %phi.31), channel_id=1, source_target_pairs={{1,0},{3,2},{5,4},{7,6},{9,8},{11,10},{13,12},{15,14},{17,16},{19,... | collective-permute-start | bytes 786440 | tf_op jit(solution)/shard_map/ppermute | solution.py:204
  29.2 0.7 collective-permute-start.4
  30.3 0.7 collective-permute-start.14
  31.1 0.7 collective-permute-start.5
  31.8 0.7 collective-permute-start.15
  32.5 0.7 collective-permute-start.6
  33.3 0.7 collective-permute-start.16
  34.8 0.7 collective-permute-start.17
  35.5 0.7 collective-permute-start.8
  36.2 0.7 collective-permute-start.18
  37.0 0.7 collective-permute-start.9
  38.6 1.3 %collective-permute-start.10 = (f32[128,512]{1,0:T(8,128)S(1)}, f32[128,512]{1,0:T(8,128)S(1)}, u32[]{:S(2)}, u32[]{:S(2)}) collective-permute-start(f32[128,512]{1,0:T(8,128)S(1)} %phi.28.refs_0_), channel_id=1, source_target_pairs={{2,1},{4,3},{6,5},{8,7},{10,9},{12,11},{14,13},{16,15},{18,17},{20... | collective-permute-start | bytes 786440 | tf_op jit(solution)/shard_map/ppermute | solution.py:204
  39.9 1.5 %collective-permute-start.20 = (f32[128,512]{1,0:T(8,128)S(1)}, f32[128,512]{1,0:T(8,128)S(1)}, u32[]{:S(2)}, u32[]{:S(2)}) collective-permute-start(f32[128,512]{1,0:T(8,128)S(1)} %phi.38.refs_0_), channel_id=1, source_target_pairs={{2,1},{4,3},{6,5},{8,7},{10,9},{12,11},{14,13},{16,15},{18,17},{20... | collective-permute-start | bytes 786440 | tf_op jit(solution)/shard_map/ppermute | solution.py:204
  41.4 44.2 %collective-permute-done.10.vector.received = f32[128,512]{1,0:T(8,128)S(1)} collective-permute-done((f32[128,512]{1,0:T(8,128)S(1)}, f32[128,512]{1,0:T(8,128)S(1)}, u32[]{:S(2)}, u32[]{:S(2)}) %collective-permute-start.10) | collective-permute-done | bytes 262176 | tf_op jit(solution)/shard_map/ppermute | solution.py:204
  86.1 1.3 %collective-permute-start.21 = (f32[128,512]{1,0:T(8,128)S(1)}, f32[128,512]{1,0:T(8,128)S(1)}, u32[]{:S(2)}, u32[]{:S(2)}) collective-permute-start(f32[128,512]{1,0:T(8,128)S(1)} %phi.29.refs_2_), channel_id=1, source_target_pairs={{1,0},{3,2},{5,4},{7,6},{9,8},{11,10},{13,12},{15,14},{17,16},{19,... | collective-permute-start | bytes 786440 | tf_op jit(solution)/shard_map/ppermute | solution.py:204
  87.4 1.0 %collective-permute-done.20.vector.received = f32[128,512]{1,0:T(8,128)S(1)} collective-permute-done((f32[128,512]{1,0:T(8,128)S(1)}, f32[128,512]{1,0:T(8,128)S(1)}, u32[]{:S(2)}, u32[]{:S(2)}) %collective-permute-start.20) | collective-permute-done | bytes 262176 | tf_op jit(solution)/shard_map/ppermute | solution.py:204
  88.9 1.3 %collective-permute-start.22 = (f32[128,512]{1,0:T(8,128)S(1)}, f32[128,512]{1,0:T(8,128)S(1)}, u32[]{:S(2)}, u32[]{:S(2)}) collective-permute-start(f32[128,512]{1,0:T(8,128)S(1)} %phi.39.refs_3_), channel_id=1, source_target_pairs={{1,0},{3,2},{5,4},{7,6},{9,8},{11,10},{13,12},{15,14},{17,16},{19,... | collective-permute-start | bytes 786440 | tf_op jit(solution)/shard_map/ppermute | solution.py:204
  90.3 0.8 last.2
  91.4 0.8 last.3
  92.2 2.6 %grads.1 = (f32[2,256,512]{2,1,0:T(8,128)}, bf16[2,512,1024]{2,1,0:T(8,128)(2,1)}, bf16[2,1024,512]{2,1,0:T(8,128)(2,1)}) custom-call(bf16[2,512,256]{2,1,0:T(8,128)(2,1)S(1)} %get-tuple-element.20.state_t.refs_0_, bf16[2,1024,256]{2,1,0:T(8,128)(2,1)S(1)} %get-tuple-element.21.act_t.refs_1_, f32[128,512]{1,0:T(8,128)S(1)} %phi.29.refs_2_, ...), custom_call_target="tpu_custom_call" | custom-call | tf_op jit(solution)/shard_map/grads/pallas_call | solution.py:276
  (44 shorter events, 4.8 us)
Async XLA Ops:
  0.6 11.7 %copy-start = (f32[1,256,512]{2,1,0:T(8,128)S(1)}, f32[1,256,512]{2,1,0:T(8,128)}, u32[]{:S(2)}) copy-start(f32[1,256,512]{2,1,0:T(8,128)} %refs_1_.3) | copy-start | bytes 1572868
  0.6 11.7 %copy-start.1 = (f32[256,512]{1,0:T(8,128)S(1)}, f32[256,512]{1,0:T(8,128)}, u32[]{:S(2)}) copy-start(f32[256,512]{1,0:T(8,128)} %terminal.3) | copy-start | bytes 1572868
  0.7 11.7 %collective-permute-start = (f32[256,512]{1,0:T(8,128)}, f32[256,512]{1,0:T(8,128)S(1)}, u32[]{:S(2)}, u32[]{:S(2)}) collective-permute-start(f32[256,512]{1,0:T(8,128)} %bitcast.1), channel_id=1, source_target_pairs={{1,0},{2,1},{3,2},{4,3},{5,4},{6,5},{7,6},{8,7},{9,8},{10,9},{11,1... | collective-permute-start | bytes 1572872 | tf_op jit(solution)/shard_map/ppermute | solution.py:204
  13.3 3.6 %collective-permute-start.1 = (f32[128,512]{1,0:T(8,128)S(1)}, f32[128,512]{1,0:T(8,128)S(1)}, u32[]{:S(2)}, u32[]{:S(2)}) collective-permute-start(f32[128,512]{1,0:T(8,128)S(1)} %get-tuple-element.25.refs_0_), channel_id=1, source_target_pairs={{1,0},{3,2},{5,4},{7,6},{9,8},{11,10},{13,12},{15,14},{17,16},{19,... | collective-permute-start | bytes 786440 | tf_op jit(solution)/shard_map/ppermute | solution.py:204
  15.5 2.7 %collective-permute-start.11 = (f32[128,512]{1,0:T(8,128)S(1)}, f32[128,512]{1,0:T(8,128)S(1)}, u32[]{:S(2)}, u32[]{:S(2)}) collective-permute-start(f32[128,512]{1,0:T(8,128)S(1)} %get-tuple-element.27.refs_0_), channel_id=1, source_target_pairs={{1,0},{3,2},{5,4},{7,6},{9,8},{11,10},{13,12},{15,14},{17,16},{19,... | collective-permute-start | bytes 786440 | tf_op jit(solution)/shard_map/ppermute | solution.py:204
  16.9 7.7 %collective-permute-start.2 = (f32[128,512]{1,0:T(8,128)S(1)}, f32[128,512]{1,0:T(8,128)S(1)}, u32[]{:S(2)}, u32[]{:S(2)}) collective-permute-start(f32[128,512]{1,0:T(8,128)S(1)} %phi.20.refs_1_), channel_id=1, source_target_pairs={{2,1},{4,3},{6,5},{8,7},{10,9},{12,11},{14,13},{16,15},{18,17},{20... | collective-permute-start | bytes 786440 | tf_op jit(solution)/shard_map/ppermute | solution.py:204
  18.2 9.1 %collective-permute-start.12 = (f32[128,512]{1,0:T(8,128)S(1)}, f32[128,512]{1,0:T(8,128)S(1)}, u32[]{:S(2)}, u32[]{:S(2)}) collective-permute-start(f32[128,512]{1,0:T(8,128)S(1)} %phi.30.refs_1_), channel_id=1, source_target_pairs={{2,1},{4,3},{6,5},{8,7},{10,9},{12,11},{14,13},{16,15},{18,17},{20... | collective-permute-start | bytes 786440 | tf_op jit(solution)/shard_map/ppermute | solution.py:204
  25.1 4.1 %collective-permute-start.3 = (f32[128,512]{1,0:T(8,128)S(1)}, f32[128,512]{1,0:T(8,128)S(1)}, u32[]{:S(2)}, u32[]{:S(2)}) collective-permute-start(f32[128,512]{1,0:T(8,128)S(1)} %phi.21), channel_id=1, source_target_pairs={{1,0},{3,2},{5,4},{7,6},{9,8},{11,10},{13,12},{15,14},{17,16},{19,... | collective-permute-start | bytes 786440 | tf_op jit(solution)/shard_map/ppermute | solution.py:204
  27.9 2.4 %collective-permute-start.13 = (f32[128,512]{1,0:T(8,128)S(1)}, f32[128,512]{1,0:T(8,128)S(1)}, u32[]{:S(2)}, u32[]{:S(2)}) collective-permute-start(f32[128,512]{1,0:T(8,128)S(1)} %phi.31), channel_id=1, source_target_pairs={{1,0},{3,2},{5,4},{7,6},{9,8},{11,10},{13,12},{15,14},{17,16},{19,... | collective-permute-start | bytes 786440 | tf_op jit(solution)/shard_map/ppermute | solution.py:204
  29.2 1.8 %collective-permute-start.4 = (f32[128,512]{1,0:T(8,128)S(1)}, f32[128,512]{1,0:T(8,128)S(1)}, u32[]{:S(2)}, u32[]{:S(2)}) collective-permute-start(f32[128,512]{1,0:T(8,128)S(1)} %phi.22.refs_0_), channel_id=1, source_target_pairs={{2,0},{6,4},{10,8},{14,12},{18,16},{22,20},{26,24},{30,28}} | collective-permute-start | bytes 786440 | tf_op jit(solution)/shard_map/ppermute | solution.py:204
  30.3 1.4 %collective-permute-start.14 = (f32[128,512]{1,0:T(8,128)S(1)}, f32[128,512]{1,0:T(8,128)S(1)}, u32[]{:S(2)}, u32[]{:S(2)}) collective-permute-start(f32[128,512]{1,0:T(8,128)S(1)} %phi.32.refs_0_), channel_id=1, source_target_pairs={{2,0},{6,4},{10,8},{14,12},{18,16},{22,20},{26,24},{30,28}} | collective-permute-start | bytes 786440 | tf_op jit(solution)/shard_map/ppermute | solution.py:204
  31.1 1.4 %collective-permute-start.5 = (f32[128,512]{1,0:T(8,128)S(1)}, f32[128,512]{1,0:T(8,128)S(1)}, u32[]{:S(2)}, u32[]{:S(2)}) collective-permute-start(f32[128,512]{1,0:T(8,128)S(1)} %phi.23.refs_1_), channel_id=1, source_target_pairs={{4,2},{8,6},{12,10},{16,14},{20,18},{24,22},{28,26}} | collective-permute-start | bytes 786440 | tf_op jit(solution)/shard_map/ppermute | solution.py:204
  31.8 1.4 %collective-permute-start.15 = (f32[128,512]{1,0:T(8,128)S(1)}, f32[128,512]{1,0:T(8,128)S(1)}, u32[]{:S(2)}, u32[]{:S(2)}) collective-permute-start(f32[128,512]{1,0:T(8,128)S(1)} %phi.33.refs_1_), channel_id=1, source_target_pairs={{4,2},{8,6},{12,10},{16,14},{20,18},{24,22},{28,26}} | collective-permute-start | bytes 786440 | tf_op jit(solution)/shard_map/ppermute | solution.py:204
  32.5 1.4 %collective-permute-start.6 = (f32[128,512]{1,0:T(8,128)S(1)}, f32[128,512]{1,0:T(8,128)S(1)}, u32[]{:S(2)}, u32[]{:S(2)}) collective-permute-start(f32[128,512]{1,0:T(8,128)S(1)} %phi.24), channel_id=1, source_target_pairs={{2,0},{6,4},{10,8},{14,12},{18,16},{22,20},{26,24},{30,28}} | collective-permute-start | bytes 786440 | tf_op jit(solution)/shard_map/ppermute | solution.py:204
  33.3 1.4 %collective-permute-start.16 = (f32[128,512]{1,0:T(8,128)S(1)}, f32[128,512]{1,0:T(8,128)S(1)}, u32[]{:S(2)}, u32[]{:S(2)}) collective-permute-start(f32[128,512]{1,0:T(8,128)S(1)} %phi.34), channel_id=1, source_target_pairs={{2,0},{6,4},{10,8},{14,12},{18,16},{22,20},{26,24},{30,28}} | collective-permute-start | bytes 786440 | tf_op jit(solution)/shard_map/ppermute | solution.py:204
  34.0 1.4 %collective-permute-start.7 = (f32[128,512]{1,0:T(8,128)S(1)}, f32[128,512]{1,0:T(8,128)S(1)}, u32[]{:S(2)}, u32[]{:S(2)}) collective-permute-start(f32[128,512]{1,0:T(8,128)S(1)} %phi.25.refs_0_), channel_id=1, source_target_pairs={{4,0},{12,8},{20,16},{28,24}} | collective-permute-start | bytes 786440 | tf_op jit(solution)/shard_map/ppermute | solution.py:204
  34.8 1.4 %collective-permute-start.17 = (f32[128,512]{1,0:T(8,128)S(1)}, f32[128,512]{1,0:T(8,128)S(1)}, u32[]{:S(2)}, u32[]{:S(2)}) collective-permute-start(f32[128,512]{1,0:T(8,128)S(1)} %phi.35.refs_0_), channel_id=1, source_target_pairs={{4,0},{12,8},{20,16},{28,24}} | collective-permute-start | bytes 786440 | tf_op jit(solution)/shard_map/ppermute | solution.py:204
  35.5 1.4 %collective-permute-start.8 = (f32[128,512]{1,0:T(8,128)S(1)}, f32[128,512]{1,0:T(8,128)S(1)}, u32[]{:S(2)}, u32[]{:S(2)}) collective-permute-start(f32[128,512]{1,0:T(8,128)S(1)} %phi.26.refs_0_), channel_id=1, source_target_pairs={{8,4},{16,12},{24,20}} | collective-permute-start | bytes 786440 | tf_op jit(solution)/shard_map/ppermute | solution.py:204
  36.2 1.5 %collective-permute-start.18 = (f32[128,512]{1,0:T(8,128)S(1)}, f32[128,512]{1,0:T(8,128)S(1)}, u32[]{:S(2)}, u32[]{:S(2)}) collective-permute-start(f32[128,512]{1,0:T(8,128)S(1)} %phi.36.refs_0_), channel_id=1, source_target_pairs={{8,4},{16,12},{24,20}} | collective-permute-start | bytes 786440 | tf_op jit(solution)/shard_map/ppermute | solution.py:204
  37.0 1.5 %collective-permute-start.9 = (f32[128,512]{1,0:T(8,128)S(1)}, f32[128,512]{1,0:T(8,128)S(1)}, u32[]{:S(2)}, u32[]{:S(2)}) collective-permute-start(f32[128,512]{1,0:T(8,128)S(1)} %phi.27.refs_0_), channel_id=1, source_target_pairs={{4,2},{8,6},{12,10},{16,14},{20,18},{24,22},{28,26}} | collective-permute-start | bytes 786440 | tf_op jit(solution)/shard_map/ppermute | solution.py:204
  37.8 2.1 %collective-permute-start.19 = (f32[128,512]{1,0:T(8,128)S(1)}, f32[128,512]{1,0:T(8,128)S(1)}, u32[]{:S(2)}, u32[]{:S(2)}) collective-permute-start(f32[128,512]{1,0:T(8,128)S(1)} %phi.37.refs_0_), channel_id=1, source_target_pairs={{4,2},{8,6},{12,10},{16,14},{20,18},{24,22},{28,26}} | collective-permute-start | bytes 786440 | tf_op jit(solution)/shard_map/ppermute | solution.py:204
  38.6 47.1 %collective-permute-start.10 = (f32[128,512]{1,0:T(8,128)S(1)}, f32[128,512]{1,0:T(8,128)S(1)}, u32[]{:S(2)}, u32[]{:S(2)}) collective-permute-start(f32[128,512]{1,0:T(8,128)S(1)} %phi.28.refs_0_), channel_id=1, source_target_pairs={{2,1},{4,3},{6,5},{8,7},{10,9},{12,11},{14,13},{16,15},{18,17},{20... | collective-permute-start | bytes 786440 | tf_op jit(solution)/shard_map/ppermute | solution.py:204
  39.9 48.5 %collective-permute-start.20 = (f32[128,512]{1,0:T(8,128)S(1)}, f32[128,512]{1,0:T(8,128)S(1)}, u32[]{:S(2)}, u32[]{:S(2)}) collective-permute-start(f32[128,512]{1,0:T(8,128)S(1)} %phi.38.refs_0_), channel_id=1, source_target_pairs={{2,1},{4,3},{6,5},{8,7},{10,9},{12,11},{14,13},{16,15},{18,17},{20... | collective-permute-start | bytes 786440 | tf_op jit(solution)/shard_map/ppermute | solution.py:204
  86.1 4.1 %collective-permute-start.21 = (f32[128,512]{1,0:T(8,128)S(1)}, f32[128,512]{1,0:T(8,128)S(1)}, u32[]{:S(2)}, u32[]{:S(2)}) collective-permute-start(f32[128,512]{1,0:T(8,128)S(1)} %phi.29.refs_2_), channel_id=1, source_target_pairs={{1,0},{3,2},{5,4},{7,6},{9,8},{11,10},{13,12},{15,14},{17,16},{19,... | collective-permute-start | bytes 786440 | tf_op jit(solution)/shard_map/ppermute | solution.py:204
  88.9 2.4 %collective-permute-start.22 = (f32[128,512]{1,0:T(8,128)S(1)}, f32[128,512]{1,0:T(8,128)S(1)}, u32[]{:S(2)}, u32[]{:S(2)}) collective-permute-start(f32[128,512]{1,0:T(8,128)S(1)} %phi.39.refs_3_), channel_id=1, source_target_pairs={{1,0},{3,2},{5,4},{7,6},{9,8},{11,10},{13,12},{15,14},{17,16},{19,... | collective-permute-start | bytes 786440 | tf_op jit(solution)/shard_map/ppermute | solution.py:204

commit v3 on v0

v3 whole, which is shorter than its diff:
```python
import functools

import jax
import jax.numpy as jnp
from jax import lax
from jax.experimental import pallas as pl
from jax.experimental.pallas import tpu as pltpu
from jax.sharding import PartitionSpec as P


LEVELS = 4
CHUNKS = 2
F32, BF16 = jnp.float32, jnp.bfloat16
VMEM = pl.BlockSpec(memory_space=pltpu.VMEM)
ANY = pl.BlockSpec(memory_space=pl.ANY)


def dot(a, b):
    return jnp.dot(a, b, preferred_element_type=F32)


def held(value):
    return pltpu.with_memory_space_constraint(value, pltpu.VMEM)


def in_hbm(value):
    return pltpu.with_memory_space_constraint(value, pltpu.HBM)


def core():
    return lax.rem(lax.axis_index("depth"), 2)


def half_of(which, half):
    return pl.ds(pl.multiple_of(which * half, half), half)


def tangent(vector, out_t, slope):
    return (dot(vector.astype(BF16), out_t) * slope).astype(BF16)


def by_core(even, odd):
    pl.when(core() == 0)(even)
    pl.when(core() == 1)(odd)


def pack_kernel(start_h, w_in_h, w_out_h, packed, start, w_in, w_out, sems):
    copies = [
        pltpu.make_async_copy(w_in_h.at[0], w_in, sems.at[0]),
        pltpu.make_async_copy(w_out_h.at[0], w_out, sems.at[1]),
        pltpu.make_async_copy(start_h.at[0], start, sems.at[2]),
    ]
    for copy in copies:
        copy.start()
    d, ff = w_in.shape
    half = start.shape[0] // 2
    copies[0].wait()
    for i in range(ff // d):
        packed[i * d : (i + 1) * d, :] = w_in[:, i * d : (i + 1) * d].astype(F32)
    copies[1].wait()
    packed[ff : 2 * ff, :] = w_out[...].astype(F32)
    copies[2].wait()
    packed[2 * ff :, :] = start[half_of(1 - core(), half), :].astype(F32)


def forward_kernel(
    token, w_in_h, w_out_h, start, w_in0, w_out0,
    in2, out2, slope2, in1, out1, slope, state_t, act_t,
    w_in1, w_out1, upper_v, act_v, sems,
):
    mine = core()
    half = start.shape[0] // 2
    own, other = half_of(mine, half), half_of(1 - mine, half)
    copies = [
        pltpu.make_async_copy(w_in_h.at[1], w_in1, sems.at[0]),
        pltpu.make_async_copy(w_out_h.at[1], w_out1, sems.at[1]),
    ]
    for copy in copies:
        copy.start()
    h_zero = jnp.tanh(dot(start[...], w_in0[...]))
    slope[0] = 1.0 - h_zero * h_zero
    slope2[mine] = slope[0, own, :]
    act_v[0] = h_zero.astype(BF16)
    upper_v[...] = (start[...].astype(F32) + dot(act_v[0], w_out0[...])).astype(BF16)
    copies[0].wait()
    h_one = jnp.tanh(dot(upper_v[...], w_in1[...]))
    slope[1] = 1.0 - h_one * h_one
    act_v[1] = h_one.astype(BF16)
    in2[mine] = w_in0[...].T
    out2[mine] = w_out0[...].T
    in1[...] = w_in1[...].T
    for low, rows in ((0, own), (half, other)):
        columns = pl.ds(low, half)
        state_t[0, :, columns] = start[rows, :].T
        state_t[1, :, columns] = upper_v[rows, :].T
        act_t[0, :, columns] = act_v[0, rows, :].T
        act_t[1, :, columns] = act_v[1, rows, :].T
    copies[1].wait()
    out1[...] = w_out1[...].T


def adopt_kernel(token, packed, in2_in, out2_in, slope2_in, in2, out2, slope2):
    slot = 1 - core()
    ff, d = in2.shape[1:]
    for i in range(ff // d):
        in2[slot, i * d : (i + 1) * d, :] = packed[i * d : (i + 1) * d, :].astype(BF16).T
    out2[slot] = packed[ff : 2 * ff, :].astype(BF16).T
    state = packed[2 * ff :, :].astype(BF16)
    for i in range(ff // d):
        h = jnp.tanh(dot(state, packed[i * d : (i + 1) * d, :].astype(BF16)))
        slope2[slot, :, i * d : (i + 1) * d] = 1.0 - h * h


def first_kernel(own, token, moved, terminal, guess, in2, out2, in1, out1, slope, above, resid):
    mine = core()
    rows = half_of(mine if own else 1 - mine, resid.shape[0])
    at_end = lax.axis_index("depth") == lax.axis_size("depth") - 1

    @pl.when(at_end)
    def _():
        above[...] = terminal[rows, :]

    @pl.when(jnp.logical_not(at_end))
    def _():
        above[...] = moved[rows, :]

    value = above[...]
    odd = value + dot(tangent(value, out1[...], slope[1, rows, :]), in1[...])
    even = odd + dot(tangent(odd, out2[mine], slope[0, rows, :]), in2[mine])
    resid[...] = even - guess[rows, :]


def apply_slot(value, factor, slot, rows, in2, out2, slope2):
    return value + factor * dot(tangent(value, out2[slot], slope2[slot, rows, :]), in2[slot])


def value_kernel(token, own, arrived, in2, out2, slope2, *refs):
    values, resid_odd, resid_even = refs[:CHUNKS], refs[CHUNKS : 2 * CHUNKS], refs[-2]
    joined = refs[-1]

    def even():
        resid_even[...] = own[...]
        joined[...] = arrived[...]

    def odd():
        resid_even[...] = arrived[...]
        joined[...] = own[...]

    by_core(even, odd)
    total = apply_slot(joined[...], 2.0, 0, slice(None), in2, out2, slope2) + resid_even[...]
    size = values[0].shape[0]
    for i in range(CHUNKS):
        values[i][...] = total[i * size : (i + 1) * size]
        resid_odd[i][...] = joined[i * size : (i + 1) * size, :]


def phi_kernel(low, size, steps, period, phase, token, vector, in2, out2, slope2, *refs):
    result = refs[-1]
    chip = lax.axis_index("depth") // 2
    active = lax.rem(chip, period) == phase
    rows = pl.ds(low, size)

    def finish(total):
        for addend in refs[:-1]:
            total = total + addend[...]
        result[...] = total

    @pl.when(active)
    def _():
        value = vector[...]
        for slot, factor in steps:
            value = apply_slot(value, factor, slot, rows, in2, out2, slope2)
        finish(value)

    @pl.when(jnp.logical_not(active))
    def _():
        finish(jnp.zeros(result.shape, F32))


def final_kernel(low, size, token, arrived, values, resid_odd, guess, above0, in2, out2, slope2, swap, even, above):
    rows = pl.ds(low, size)
    half = above0.shape[0]
    mine = guess[pl.ds(pl.multiple_of(core() * half + low, size), size), :]
    last = apply_slot(arrived[...], 2.0, 1, rows, in2, out2, slope2) + resid_odd[...]
    swap[0] = last

    def of_even():
        swap[1] = arrived[...]
        even[...] = mine + values[...]
        above[...] = above0[rows, :] + swap[0]

    def of_odd():
        swap[1] = values[...]
        even[...] = mine + swap[0]
        above[...] = above0[rows, :] + arrived[...]

    by_core(of_even, of_odd)


def own_kernel(token, in2, out2, in1, out1, slope, *refs):
    above, (odd, above_b, odd_b, tan) = refs[:CHUNKS], refs[CHUNKS:]
    mine = core()
    rows = half_of(mine, odd.shape[0])
    value = jnp.concatenate([part[...] for part in above], 0)
    above_b[...] = value.astype(BF16)
    tan_one = tangent(value, out1[...], slope[1, rows, :])
    tan[1] = tan_one
    value = value + dot(tan_one, in1[...])
    odd[...] = value
    odd_b[...] = value.astype(BF16)
    tan[0] = tangent(value, out2[mine], slope[0, rows, :])


def finish_kernel(token, in2, out2, in1, out1, slope, state_t, act_t, guess, above0, odd, above_b, odd_b, tan, *refs):
    swapped, even = refs[:CHUNKS], refs[CHUNKS : 2 * CHUNKS]
    adjoint, grad_in, grad_out = refs[2 * CHUNKS : 2 * CHUNKS + 3]
    even_x, odd_x, above_x, grad_in_v, grad_out_v, sems = refs[2 * CHUNKS + 3 :]
    mine = core()
    half, size = odd.shape[0], even[0].shape[0]
    own, other = half_of(mine, half), half_of(1 - mine, half)
    copies = []

    def send(source, target):
        copy = pltpu.make_async_copy(source, target, sems.at[len(copies)])
        copy.start()
        copies.append(copy)

    for i in range(CHUNKS):
        low = pl.multiple_of(mine * half + i * size, size)
        send(even[i], adjoint.at[0, pl.ds(low, size), :])
    send(odd, adjoint.at[1, own, :])

    def fill(even_part, above_part):
        for i in range(CHUNKS):
            rows = pl.ds(i * size, size)
            low = pl.multiple_of((1 - mine) * half + i * size, size)
            even_x[rows, :] = guess[pl.ds(low, size), :] + swapped[i][even_part]
            above_x[rows, :] = above0[rows, :] + swapped[i][above_part]

    by_core(lambda: fill(1, 0), lambda: fill(0, 1))
    send(even_x, adjoint.at[0, other, :])

    def product(left, first, second):
        return dot(left, jnp.concatenate([first, second], 0)).astype(BF16)

    value = above_x[...]
    grad_out_v[1] = product(act_t[1], above_b[...], value.astype(BF16))
    send(grad_out_v.at[1], grad_out.at[1])
    tan_one = tangent(value, out1[...], slope[1, other, :])
    grad_in_v[1] = product(state_t[1], tan[1], tan_one)
    send(grad_in_v.at[1], grad_in.at[1])
    value = value + dot(tan_one, in1[...])
    odd_x[...] = value
    send(odd_x, adjoint.at[1, other, :])
    grad_out_v[0] = product(act_t[0], odd_b[...], value.astype(BF16))
    send(grad_out_v.at[0], grad_out.at[0])
    tan_zero = tangent(value, out2[mine], slope[0, other, :])
    grad_in_v[0] = product(state_t[0], tan[0], tan_zero)
    send(grad_in_v.at[0], grad_in.at[0])
    for copy in copies:
        copy.wait()


def local(w_in, w_out, checkpoint, guess, terminal):
    count = lax.axis_size("depth")
    rows, d = terminal.shape
    ff = w_in.shape[2]
    half = rows // 2
    size = half // CHUNKS
    token = []

    def run(kernel, shapes, operands, spaces=None, outs=None, mib=16, **options):
        operands = tuple(token) + tuple(operands)
        specs = [VMEM] * (len(operands) - len(spaces or ())) + list(spaces or ())
        if spaces:
            specs = [VMEM] * len(token) + list(spaces)
        results = pl.pallas_call(
            kernel,
            out_shape=tuple(shapes),
            in_specs=specs,
            out_specs=outs or [VMEM] * len(shapes),
            compiler_params=pltpu.CompilerParams(vmem_limit_bytes=mib * 2**20),
            **options,
        )(*operands)
        if outs:
            return results
        results = [held(result) for result in results]
        token[:] = [results[-1]]
        return results

    def permute(value, route):
        return held(lax.ppermute(value, "depth", route))

    swap_route = [(i, i + 1 - 2 * (i % 2)) for i in range(count)]

    def shift(value, period, phase, distance):
        route = [
            (2 * c + k, 2 * (c - distance) + k)
            for c in range(distance, count // 2)
            if c % period == phase
            for k in range(2)
        ]
        return permute(value, route)

    def vmem(*shape, kind=F32):
        return pltpu.VMEM(shape, kind)

    guess = guess.reshape(rows, d)
    moved = permute(guess, [(i, i - 1) for i in range(1, count)])
    guess, terminal = held(guess), held(terminal)
    packed, start, w_in0, w_out0 = run(
        pack_kernel,
        (vmem(2 * ff + half, d), vmem(rows, d, kind=BF16), vmem(d, ff, kind=BF16), vmem(ff, d, kind=BF16)),
        (in_hbm(checkpoint), in_hbm(w_in), in_hbm(w_out)),
        spaces=[ANY] * 3,
        scratch_shapes=[pltpu.SemaphoreType.DMA((3,))],
    )
    packed = permute(packed, swap_route)
    in2, out2, slope2, in1, out1, slope, state_t, act_t = run(
        forward_kernel,
        (
            vmem(2, ff, d, kind=BF16),
            vmem(2, d, ff, kind=BF16),
            vmem(2, half, ff),
            vmem(ff, d, kind=BF16),
            vmem(d, ff, kind=BF16),
            vmem(2, rows, ff),
            vmem(2, d, rows, kind=BF16),
            vmem(2, ff, rows, kind=BF16),
        ),
        (in_hbm(w_in), in_hbm(w_out), start, w_in0, w_out0),
        spaces=[ANY] * 2 + [VMEM] * 3,
        mib=24,
        scratch_shapes=[
            vmem(d, ff, kind=BF16),
            vmem(ff, d, kind=BF16),
            vmem(rows, d, kind=BF16),
            vmem(2, rows, ff, kind=BF16),
            pltpu.SemaphoreType.DMA((2,)),
        ],
    )

    def first(own):
        return run(
            functools.partial(first_kernel, own),
            (vmem(half, d), vmem(half, d)),
            (moved, terminal, guess, in2, out2, in1, out1, slope),
        )

    above_other, resid = first(False)
    arrived = permute(resid, swap_route)
    above_own, resid = first(True)
    in2, out2, slope2 = run(
        adopt_kernel,
        (vmem(2, ff, d, kind=BF16), vmem(2, d, ff, kind=BF16), vmem(2, half, ff)),
        (packed, in2, out2, slope2),
        input_output_aliases={2: 0, 3: 1, 4: 2},
    )
    results = run(
        value_kernel,
        (vmem(size, d),) * (2 * CHUNKS),
        (resid, arrived, in2, out2, slope2),
        scratch_shapes=[vmem(half, d), vmem(half, d)],
    )
    values, resid_odd = results[:CHUNKS], results[CHUNKS:]

    def phi(received, steps, period, phase, send, *addends):
        results, sent = [], []
        for i in range(CHUNKS):
            (result,) = run(
                functools.partial(phi_kernel, i * size, size, steps, period, phase),
                (vmem(size, d),),
                (received[i], in2, out2, slope2, *[addend[i] for addend in addends]),
            )
            results.append(result)
            sent.append(send(result))
        return results, sent

    def cycle(level, rhs, sent, addend, send):
        distance = 2 ** (level - 2)
        period, steps = 2 * distance, ((0, float(2**level)),)

        def down(value):
            return shift(value, period, distance, distance)

        def up(value):
            return shift(value, period, 0, distance)

        point, sent = phi(sent, steps, period, 0, up, rhs)
        if level < LEVELS - 1:
            _, sent = phi(sent, steps, period, distance, down)
            deeper = 2 * distance
            resid, sent = phi(sent, steps, period, 0, lambda value: shift(value, 2 * deeper, deeper, deeper))
            point, sent = cycle(level + 1, resid, sent, point, up)
        return phi(sent, steps, period, distance, send, point, addend)

    def next_chip(value):
        return shift(value, 1, 0, 1)

    sent = [next_chip(value) for value in values]
    resid, sent = phi(sent, ((1, 2.0), (0, 2.0)), 1, 0, lambda value: shift(value, 2, 1, 1))
    values, sent = cycle(2, resid, sent, values, next_chip)

    swapped, even, above = [], [], []
    for i in range(CHUNKS):
        swap, mine, upper = run(
            functools.partial(final_kernel, i * size, size),
            (vmem(2, size, d), vmem(size, d), vmem(size, d)),
            (sent[i], values[i], resid_odd[i], guess, above_own, in2, out2, slope2),
        )
        swapped.append(permute(swap, swap_route))
        even.append(mine)
        above.append(upper)
    fine = (in2, out2, in1, out1, slope)
    owned = run(
        own_kernel,
        (vmem(half, d), vmem(half, d, kind=BF16), vmem(half, d, kind=BF16), vmem(2, half, ff, kind=BF16)),
        (*fine, *above),
    )
    return run(
        finish_kernel,
        (
            jax.ShapeDtypeStruct((2, rows, d), F32),
            jax.ShapeDtypeStruct((2, d, ff), BF16),
            jax.ShapeDtypeStruct((2, ff, d), BF16),
        ),
        (*fine, state_t, act_t, guess, above_other, *owned, *swapped, *even),
        outs=[ANY] * 3,
        mib=24,
        scratch_shapes=[
            vmem(half, d),
            vmem(half, d),
            vmem(half, d),
            vmem(2, d, ff, kind=BF16),
            vmem(2, ff, d, kind=BF16),
            pltpu.SemaphoreType.DMA((CHUNKS + 7,)),
        ],
    )


def solution(mesh):
    split = P("depth", None, None)

    return jax.shard_map(
        local,
        mesh=mesh,
        in_specs=(split, split, split, split, P()),
        out_specs=(split, split, split),
        check_vma=False,
    )
```

time: 233 us -> 91.3 us (0.39); the launches traced: 229 us -> 90.1 us
  waiting for transfers between devices: 142 us -> 43.6 us
  matrix products: 55.5 us -> 0 us
  Pallas kernels: 0 us -> 17.9 us
  starting transfers between devices: 21.2 us -> 27.6 us
  local copies, waits for them, and re-layouts: 4.58 us -> 0.01 us
  other arithmetic: 4.38 us -> 0 us
    ppermute x12 -> x21, waiting for transfers between devices: 142 us -> 43.6 us  [permute(): return held(lax.ppermute(value, 'depth', route))]
    dot_general x21 -> x0, matrix products: 55.5 us -> none  [the longest x13 41.3 us: apply_layer(): jnp.dot(tangent, w_first.T, preferred_element_type=jnp.float32)]
    pallas_call x0 -> x24, Pallas kernels: none -> 17.9 us  [run(): pl.pallas_call(kernel, out_shape=tuple(shapes), in_specs=specs, out_specs...]
    ppermute x12 -> x21, starting transfers between devices: 21.2 us -> 27.6 us  [permute(): return held(lax.ppermute(value, 'depth', route))]
    unnamed x23 -> x4, local copies, waits for them, and re-layouts: 4.58 us -> 0.01 us
    another operation x3 -> x0, other arithmetic: 4.27 us -> none  [the longest x1 1.73 us: local(): jnp.stack([jnp.dot(start.T, tangent_zero, preferred_element_type=jnp.floa...]
  transfers between devices with their start and end apart: 12 -> 21, of which waited for: 12 -> 12; matrix products, arithmetic and copies ran while one was open for 2% -> 0% of each run, Pallas kernels for 0% -> 13%
where the time goes in v3:
time: 91.3 us; the launch traced here: 90.1 us
  waiting for transfers between devices  43.6 us (48%)
  starting transfers between devices  27.6 us (30%)
  Pallas kernels  17.9 us (20%)
  between operations  1.05 us (1%)
    ppermute x21, waiting for transfers between devices, permute(): return held(lax.ppermute(value, 'depth', route))  43.6 us
    ppermute x21, starting transfers between devices, permute(): return held(lax.ppermute(value, 'depth', route))  27.6 us
    pallas_call x24, Pallas kernels, run(): pl.pallas_call(kernel, out_shape=tuple(shapes), in_specs=specs, out_specs...  17.9 us
  transfers between devices with their start and end apart: 21, of which 12 were waited for; matrix products, arithmetic and copies ran while one was open for 0% of the time, Pallas kernels for 13%

profile of v3, /device:TPU:1, one launch (start us, length us, event | category | flops | bytes accessed | tf_op | source)
XLA Modules:
  0.0 90.1 jit_solution(17478255805584377185)
XLA Ops:
  0.6 1.8 %shard_map.76 = (f32[2176,512]{1,0:T(8,128)S(1)}, bf16[256,512]{1,0:T(8,128)(2,1)S(1)}, bf16[512,1024]{1,0:T(8,128)(2,1)S(1)}, bf16[1024,512]{1,0:T(8,128)(2,1)S(1)}) custom-call(bf16[1,256,512]{2,1,0:T(8,128)(2,1)} %start_h.1, bf16[2,512,1024]{2,1,0:T(8,128)(2,1)} %w_in_h.3, bf16[2,1024,512]{2,1,0:T(8,128)(2,1)} %w_out_h.3), custom_call_target="tpu_custom_call" | custom-call | tf_op jit(solution)/shard_map/pallas_call | solution.py:277
  2.5 2.4 %collective-permute-start = (f32[256,512]{1,0:T(8,128)S(1)}, f32[256,512]{1,0:T(8,128)S(1)}, u32[]{:S(2)}, u32[]{:S(2)}) collective-permute-start(f32[256,512]{1,0:T(8,128)S(1)} %bitcast.1), channel_id=1, source_target_pairs={{1,0},{2,1},{3,2},{4,3},{5,4},{6,5},{7,6},{8,7},{9,8},{10,9},{11,1... | collective-permute-start | bytes 1572872 | tf_op jit(solution)/shard_map/ppermute | solution.py:292
  4.9 3.0 %shard_map.77 = (bf16[2,1024,512]{2,1,0:T(8,128)(2,1)S(1)}, bf16[2,512,1024]{2,1,0:T(8,128)(2,1)S(1)}, f32[2,128,1024]{2,1,0:T(8,128)S(1)}, bf16[1024,512]{1,0:T...) custom-call(bf16[1024,512]{1,0:T(8,128)(2,1)S(1)} %get-tuple-element, ...), custom_call_target="tpu_custom_call" | custom-call | tf_op jit(solution)/shard_map/pallas_call | solution.py:277
  7.9 6.0 %collective-permute-done.moved = f32[256,512]{1,0:T(8,128)S(1)} collective-permute-done((f32[256,512]{1,0:T(8,128)S(1)}, f32[256,512]{1,0:T(8,128)S(1)}, u32[]{:S(2)}, u32[]{:S(2)}) %collective-permute-start) | collective-permute-done | bytes 524320 | tf_op jit(solution)/shard_map/ppermute | solution.py:292
  13.9 0.9 %shard_map.78 = (f32[128,512]{1,0:T(8,128)S(1)}, f32[128,512]{1,0:T(8,128)S(1)}) custom-call(bf16[2,1024,256]{2,1,0:T(8,128)(2,1)S(1)} %get-tuple-element.39.token.act_t, f32[256,512]{1,0:T(8,128)S(1)} %collective-permute-done.moved, f32[256,512]{1,0:T(8,128)S(1)} %copy-done.1, f32[256,512]{1,0:T(8,128)S(1)} %bitcast.2, ...), custom_call_target="tpu_custom_call" | custom-call | tf_op jit(solution)/shard_map/pallas_call | solution.py:277
  14.9 0.9 %shard_map.79 = (f32[128,512]{1,0:T(8,128)S(1)}, f32[128,512]{1,0:T(8,128)S(1)}) custom-call(f32[128,512]{1,0:T(8,128)S(1)} %get-tuple-element.45.token, f32[256,512]{1,0:T(8,128)S(1)} %collective-permute-done.moved, f32[256,512]{1,0:T(8,128)S(1)} %copy-done.1, f32[256,512]{1,0:T(8,128)S(1)} %bitcast.3, ...), custom_call_target="tpu_custom_call" | custom-call | tf_op jit(solution)/shard_map/pallas_call | solution.py:277
  17.0 1.3 %collective-permute-start.3 = (f32[64,512]{1,0:T(8,128)S(1)}, f32[64,512]{1,0:T(8,128)S(1)}, u32[]{:S(2)}, u32[]{:S(2)}) collective-permute-start(f32[64,512]{1,0:T(8,128)S(1)} %get-tuple-element.53.refs_1_), channel_id=1, source_target_pairs={{2,0},{3,1},{4,2},{5,3},{6,4},{7,5},{8,6},{9,7},{10,8},{11,9},{12,... | collective-permute-start | bytes 393224 | tf_op jit(solution)/shard_map/ppermute | solution.py:292
  18.3 1.3 %collective-permute-start.4 = (f32[64,512]{1,0:T(8,128)S(1)}, f32[64,512]{1,0:T(8,128)S(1)}, u32[]{:S(2)}, u32[]{:S(2)}) collective-permute-start(f32[64,512]{1,0:T(8,128)S(1)} %get-tuple-element.54.refs_1_), channel_id=1, source_target_pairs={{2,0},{3,1},{4,2},{5,3},{6,4},{7,5},{8,6},{9,7},{10,8},{11,9},{12,... | collective-permute-start | bytes 393224 | tf_op jit(solution)/shard_map/ppermute | solution.py:292
  19.6 5.4 %collective-permute-done.3.vector = f32[64,512]{1,0:T(8,128)S(1)} collective-permute-done((f32[64,512]{1,0:T(8,128)S(1)}, f32[64,512]{1,0:T(8,128)S(1)}, u32[]{:S(2)}, u32[]{:S(2)}) %collective-permute-start.3) | collective-permute-done | bytes 131104 | tf_op jit(solution)/shard_map/ppermute | solution.py:292
  25.0 0.9 %shard_map.82.token.refs_0_ = f32[64,512]{1,0:T(8,128)S(1)} custom-call(f32[64,512]{1,0:T(8,128)S(1)} %get-tuple-element.52.token.resid_odd, f32[64,512]{1,0:T(8,128)S(1)} %collective-permute-done.3.vector, bf16[2,1024,512]{2,1,0:T(8,128)(2,1)S(1)} %get-tuple-element.50.in2, bf16[2,512,1024]{2,1,0:T(8,128)(2,1)S(1)} %get-tuple-element.51.out2, ...), custom_call_target="tpu_custom_call" | custom-call | tf_op jit(solution)/shard_map/pallas_call | solution.py:277
  26.0 1.3 %collective-permute-start.5 = (f32[64,512]{1,0:T(8,128)S(1)}, f32[64,512]{1,0:T(8,128)S(1)}, u32[]{:S(2)}, u32[]{:S(2)}) collective-permute-start(f32[64,512]{1,0:T(8,128)S(1)} %shard_map.82.token.refs_0_), channel_id=1, source_target_pairs={{2,0},{3,1},{6,4},{7,5},{10,8},{11,9},{14,12},{15,13},{18,16},{19,... | collective-permute-start | bytes 393224 | tf_op jit(solution)/shard_map/ppermute | solution.py:292
  27.8 0.9 %shard_map.83.token.refs_0_ = f32[64,512]{1,0:T(8,128)S(1)} custom-call(f32[64,512]{1,0:T(8,128)S(1)} %shard_map.82.token.refs_0_, f32[64,512]{1,0:T(8,128)S(1)} %collective-permute-done.4.vector, bf16[2,1024,512]{2,1,0:T(8,128)(2,1)S(1)} %get-tuple-element.50.in2, bf16[2,512,1024]{2,1,0:T(8,128)(2,1)S(1)} %get-tuple-element.51.out2, ...), custom_call_target="tpu_custom_call" | custom-call | tf_op jit(solution)/shard_map/pallas_call | solution.py:277
  28.8 1.3 %collective-permute-start.6 = (f32[64,512]{1,0:T(8,128)S(1)}, f32[64,512]{1,0:T(8,128)S(1)}, u32[]{:S(2)}, u32[]{:S(2)}) collective-permute-start(f32[64,512]{1,0:T(8,128)S(1)} %shard_map.83.token.refs_0_), channel_id=1, source_target_pairs={{2,0},{3,1},{6,4},{7,5},{10,8},{11,9},{14,12},{15,13},{18,16},{19,... | collective-permute-start | bytes 393224 | tf_op jit(solution)/shard_map/ppermute | solution.py:292
  30.1 1.6 %collective-permute-done.5.vector = f32[64,512]{1,0:T(8,128)S(1)} collective-permute-done((f32[64,512]{1,0:T(8,128)S(1)}, f32[64,512]{1,0:T(8,128)S(1)}, u32[]{:S(2)}, u32[]{:S(2)}) %collective-permute-start.5) | collective-permute-done | bytes 131104 | tf_op jit(solution)/shard_map/ppermute | solution.py:292
  32.2 0.7 collective-permute-start.7
  32.9 3.4 %collective-permute-done.6.vector = f32[64,512]{1,0:T(8,128)S(1)} collective-permute-done((f32[64,512]{1,0:T(8,128)S(1)}, f32[64,512]{1,0:T(8,128)S(1)}, u32[]{:S(2)}, u32[]{:S(2)}) %collective-permute-start.6) | collective-permute-done | bytes 131104 | tf_op jit(solution)/shard_map/ppermute | solution.py:292
  36.7 0.7 collective-permute-start.8
  37.5 1.3 %collective-permute-start.9 = (f32[64,512]{1,0:T(8,128)S(1)}, f32[64,512]{1,0:T(8,128)S(1)}, u32[]{:S(2)}, u32[]{:S(2)}) collective-permute-start(f32[64,512]{1,0:T(8,128)S(1)} %shard_map.86.token), channel_id=1, source_target_pairs={{2,0},{3,1},{6,4},{7,5},{10,8},{11,9},{14,12},{15,13},{18,16},{19,... | collective-permute-start | bytes 393224 | tf_op jit(solution)/shard_map/ppermute | solution.py:292
  38.8 1.3 %collective-permute-start.10 = (f32[64,512]{1,0:T(8,128)S(1)}, f32[64,512]{1,0:T(8,128)S(1)}, u32[]{:S(2)}, u32[]{:S(2)}) collective-permute-start(f32[64,512]{1,0:T(8,128)S(1)} %shard_map.87.token), channel_id=1, source_target_pairs={{2,0},{3,1},{6,4},{7,5},{10,8},{11,9},{14,12},{15,13},{18,16},{19,... | collective-permute-start | bytes 393224 | tf_op jit(solution)/shard_map/ppermute | solution.py:292
  40.1 4.0 %collective-permute-done.9.vector = f32[64,512]{1,0:T(8,128)S(1)} collective-permute-done((f32[64,512]{1,0:T(8,128)S(1)}, f32[64,512]{1,0:T(8,128)S(1)}, u32[]{:S(2)}, u32[]{:S(2)}) %collective-permute-start.9) | collective-permute-done | bytes 131104 | tf_op jit(solution)/shard_map/ppermute | solution.py:292
  44.6 1.3 %collective-permute-start.11 = (f32[64,512]{1,0:T(8,128)S(1)}, f32[64,512]{1,0:T(8,128)S(1)}, u32[]{:S(2)}, u32[]{:S(2)}) collective-permute-start(f32[64,512]{1,0:T(8,128)S(1)} %shard_map.88.token.refs_0_), channel_id=1, source_target_pairs={{4,0},{5,1},{12,8},{13,9},{20,16},{21,17},{28,24},{29,25}} | collective-permute-start | bytes 393224 | tf_op jit(solution)/shard_map/ppermute | solution.py:292
  45.9 6.2 %collective-permute-done.10.vector = f32[64,512]{1,0:T(8,128)S(1)} collective-permute-done((f32[64,512]{1,0:T(8,128)S(1)}, f32[64,512]{1,0:T(8,128)S(1)}, u32[]{:S(2)}, u32[]{:S(2)}) %collective-permute-start.10) | collective-permute-done | bytes 131104 | tf_op jit(solution)/shard_map/ppermute | solution.py:292
  52.6 1.3 %collective-permute-start.12 = (f32[64,512]{1,0:T(8,128)S(1)}, f32[64,512]{1,0:T(8,128)S(1)}, u32[]{:S(2)}, u32[]{:S(2)}) collective-permute-start(f32[64,512]{1,0:T(8,128)S(1)} %shard_map.89.token.refs_0_), channel_id=1, source_target_pairs={{4,0},{5,1},{12,8},{13,9},{20,16},{21,17},{28,24},{29,25}} | collective-permute-start | bytes 393224 | tf_op jit(solution)/shard_map/ppermute | solution.py:292
  54.4 0.7 collective-permute-start.13
  55.1 4.4 %collective-permute-done.12.vector = f32[64,512]{1,0:T(8,128)S(1)} collective-permute-done((f32[64,512]{1,0:T(8,128)S(1)}, f32[64,512]{1,0:T(8,128)S(1)}, u32[]{:S(2)}, u32[]{:S(2)}) %collective-permute-start.12) | collective-permute-done | bytes 131104 | tf_op jit(solution)/shard_map/ppermute | solution.py:292
  62.2 1.3 %collective-permute-start.17 = (f32[64,512]{1,0:T(8,128)S(1)}, f32[64,512]{1,0:T(8,128)S(1)}, u32[]{:S(2)}, u32[]{:S(2)}) collective-permute-start(f32[64,512]{1,0:T(8,128)S(1)} %shard_map.94.token.values), channel_id=1, source_target_pairs={{2,0},{3,1},{4,2},{5,3},{6,4},{7,5},{8,6},{9,7},{10,8},{11,9},{12,... | collective-permute-start | bytes 393224 | tf_op jit(solution)/shard_map/ppermute | solution.py:292
  63.6 1.3 %collective-permute-start.18 = (f32[64,512]{1,0:T(8,128)S(1)}, f32[64,512]{1,0:T(8,128)S(1)}, u32[]{:S(2)}, u32[]{:S(2)}) collective-permute-start(f32[64,512]{1,0:T(8,128)S(1)} %shard_map.95.token.values), channel_id=1, source_target_pairs={{2,0},{3,1},{4,2},{5,3},{6,4},{7,5},{8,6},{9,7},{10,8},{11,9},{12,... | collective-permute-start | bytes 393224 | tf_op jit(solution)/shard_map/ppermute | solution.py:292
  64.9 7.9 %collective-permute-done.17.arrived = f32[64,512]{1,0:T(8,128)S(1)} collective-permute-done((f32[64,512]{1,0:T(8,128)S(1)}, f32[64,512]{1,0:T(8,128)S(1)}, u32[]{:S(2)}, u32[]{:S(2)}) %collective-permute-start.17) | collective-permute-done | bytes 131104 | tf_op jit(solution)/shard_map/ppermute | solution.py:292
  73.3 3.5 %collective-permute-done.18.arrived = f32[64,512]{1,0:T(8,128)S(1)} collective-permute-done((f32[64,512]{1,0:T(8,128)S(1)}, f32[64,512]{1,0:T(8,128)S(1)}, u32[]{:S(2)}, u32[]{:S(2)}) %collective-permute-start.18) | collective-permute-done | bytes 131104 | tf_op jit(solution)/shard_map/ppermute | solution.py:292
  77.2 8.0 %collective-permute-start.20 = (f32[2,64,512]{2,1,0:T(8,128)S(1)}, f32[2,64,512]{2,1,0:T(8,128)S(1)}, u32[]{:S(2)}, u32[]{:S(2)}) collective-permute-start(f32[2,64,512]{2,1,0:T(8,128)S(1)} %get-tuple-element.66), channel_id=1, source_target_pairs={{0,1},{1,0},{2,3},{3,2},{4,5},{5,4},{6,7},{7,6},{8,9},{9,8},{10,11... | collective-permute-start | bytes 786440 | tf_op jit(solution)/shard_map/ppermute | solution.py:292
  85.3 0.7 shard_map.98
  86.8 3.3 %shard_map.99 = (f32[2,256,512]{2,1,0:T(8,128)}, bf16[2,512,1024]{2,1,0:T(8,128)(2,1)}, bf16[2,1024,512]{2,1,0:T(8,128)(2,1)}) custom-call(bf16[2,128,1024]{2,1,0:T(8,128)(2,1)S(1)} %get-tuple-element.59.token.tan, bf16[2,1024,512]{2,1,0:T(8,128)(2,1)S(1)} %get-tuple-element.50.in2, bf16[2,512,1024]{2,1,0:T(8,128)(2,1)S(1)} %get-tuple-element.51.out2, ...), custom_call_target="tpu_custom_call" | custom-call | tf_op jit(solution)/shard_map/pallas_call | solution.py:277
  (38 shorter events, 9.0 us)
Async XLA Ops:
  0.6 1.9 %copy-start = (f32[1,256,512]{2,1,0:T(8,128)S(1)}, f32[1,256,512]{2,1,0:T(8,128)}, u32[]{:S(2)}) copy-start(f32[1,256,512]{2,1,0:T(8,128)} %param.8) | copy-start | bytes 1572868
  2.4 13.4 %collective-permute-start.1 = (f32[2176,512]{1,0:T(8,128)S(1)}, f32[2176,512]{1,0:T(8,128)S(1)}, u32[]{:S(2)}, u32[]{:S(2)}) collective-permute-start(f32[2176,512]{1,0:T(8,128)S(1)} %get-tuple-element.47), channel_id=1, source_target_pairs={{0,1},{1,0},{2,3},{3,2},{4,5},{5,4},{6,7},{7,6},{8,9},{9,8},{10,11... | collective-permute-start | bytes 13369352 | tf_op jit(solution)/shard_map/ppermute | solution.py:292
  2.5 11.4 %collective-permute-start = (f32[256,512]{1,0:T(8,128)S(1)}, f32[256,512]{1,0:T(8,128)S(1)}, u32[]{:S(2)}, u32[]{:S(2)}) collective-permute-start(f32[256,512]{1,0:T(8,128)S(1)} %bitcast.1), channel_id=1, source_target_pairs={{1,0},{2,1},{3,2},{4,3},{5,4},{6,5},{7,6},{8,7},{9,8},{10,9},{11,1... | collective-permute-start | bytes 1572872 | tf_op jit(solution)/shard_map/ppermute | solution.py:292
  4.9 9.0 %copy-start.1 = (f32[256,512]{1,0:T(8,128)S(1)}, f32[256,512]{1,0:T(8,128)}, u32[]{:S(2)}) copy-start(f32[256,512]{1,0:T(8,128)} %terminal.3) | copy-start | bytes 1572868
  14.8 1.7 %collective-permute-start.2 = (f32[128,512]{1,0:T(8,128)S(1)}, f32[128,512]{1,0:T(8,128)S(1)}, u32[]{:S(2)}, u32[]{:S(2)}) collective-permute-start(f32[128,512]{1,0:T(8,128)S(1)} %get-tuple-element.45.token), channel_id=1, source_target_pairs={{0,1},{1,0},{2,3},{3,2},{4,5},{5,4},{6,7},{7,6},{8,9},{9,8},{10,11... | collective-permute-start | bytes 786440 | tf_op jit(solution)/shard_map/ppermute | solution.py:292
  17.0 8.0 %collective-permute-start.3 = (f32[64,512]{1,0:T(8,128)S(1)}, f32[64,512]{1,0:T(8,128)S(1)}, u32[]{:S(2)}, u32[]{:S(2)}) collective-permute-start(f32[64,512]{1,0:T(8,128)S(1)} %get-tuple-element.53.refs_1_), channel_id=1, source_target_pairs={{2,0},{3,1},{4,2},{5,3},{6,4},{7,5},{8,6},{9,7},{10,8},{11,9},{12,... | collective-permute-start | bytes 393224 | tf_op jit(solution)/shard_map/ppermute | solution.py:292
  18.3 9.5 %collective-permute-start.4 = (f32[64,512]{1,0:T(8,128)S(1)}, f32[64,512]{1,0:T(8,128)S(1)}, u32[]{:S(2)}, u32[]{:S(2)}) collective-permute-start(f32[64,512]{1,0:T(8,128)S(1)} %get-tuple-element.54.refs_1_), channel_id=1, source_target_pairs={{2,0},{3,1},{4,2},{5,3},{6,4},{7,5},{8,6},{9,7},{10,8},{11,9},{12,... | collective-permute-start | bytes 393224 | tf_op jit(solution)/shard_map/ppermute | solution.py:292
  26.0 5.7 %collective-permute-start.5 = (f32[64,512]{1,0:T(8,128)S(1)}, f32[64,512]{1,0:T(8,128)S(1)}, u32[]{:S(2)}, u32[]{:S(2)}) collective-permute-start(f32[64,512]{1,0:T(8,128)S(1)} %shard_map.82.token.refs_0_), channel_id=1, source_target_pairs={{2,0},{3,1},{6,4},{7,5},{10,8},{11,9},{14,12},{15,13},{18,16},{19,... | collective-permute-start | bytes 393224 | tf_op jit(solution)/shard_map/ppermute | solution.py:292
  28.8 7.5 %collective-permute-start.6 = (f32[64,512]{1,0:T(8,128)S(1)}, f32[64,512]{1,0:T(8,128)S(1)}, u32[]{:S(2)}, u32[]{:S(2)}) collective-permute-start(f32[64,512]{1,0:T(8,128)S(1)} %shard_map.83.token.refs_0_), channel_id=1, source_target_pairs={{2,0},{3,1},{6,4},{7,5},{10,8},{11,9},{14,12},{15,13},{18,16},{19,... | collective-permute-start | bytes 393224 | tf_op jit(solution)/shard_map/ppermute | solution.py:292
  32.2 5.2 %collective-permute-start.7 = (f32[64,512]{1,0:T(8,128)S(1)}, f32[64,512]{1,0:T(8,128)S(1)}, u32[]{:S(2)}, u32[]{:S(2)}) collective-permute-start(f32[64,512]{1,0:T(8,128)S(1)} %shard_map.84.token.refs_1_), channel_id=1, source_target_pairs={{4,2},{5,3},{8,6},{9,7},{12,10},{13,11},{16,14},{17,15},{20,18},{2... | collective-permute-start | bytes 393224 | tf_op jit(solution)/shard_map/ppermute | solution.py:292
  36.7 2.0 %collective-permute-start.8 = (f32[64,512]{1,0:T(8,128)S(1)}, f32[64,512]{1,0:T(8,128)S(1)}, u32[]{:S(2)}, u32[]{:S(2)}) collective-permute-start(f32[64,512]{1,0:T(8,128)S(1)} %shard_map.85.token.refs_1_), channel_id=1, source_target_pairs={{4,2},{5,3},{8,6},{9,7},{12,10},{13,11},{16,14},{17,15},{20,18},{2... | collective-permute-start | bytes 393224 | tf_op jit(solution)/shard_map/ppermute | solution.py:292
  37.5 6.7 %collective-permute-start.9 = (f32[64,512]{1,0:T(8,128)S(1)}, f32[64,512]{1,0:T(8,128)S(1)}, u32[]{:S(2)}, u32[]{:S(2)}) collective-permute-start(f32[64,512]{1,0:T(8,128)S(1)} %shard_map.86.token), channel_id=1, source_target_pairs={{2,0},{3,1},{6,4},{7,5},{10,8},{11,9},{14,12},{15,13},{18,16},{19,... | collective-permute-start | bytes 393224 | tf_op jit(solution)/shard_map/ppermute | solution.py:292
  38.8 13.3 %collective-permute-start.10 = (f32[64,512]{1,0:T(8,128)S(1)}, f32[64,512]{1,0:T(8,128)S(1)}, u32[]{:S(2)}, u32[]{:S(2)}) collective-permute-start(f32[64,512]{1,0:T(8,128)S(1)} %shard_map.87.token), channel_id=1, source_target_pairs={{2,0},{3,1},{6,4},{7,5},{10,8},{11,9},{14,12},{15,13},{18,16},{19,... | collective-permute-start | bytes 393224 | tf_op jit(solution)/shard_map/ppermute | solution.py:292
  44.6 9.3 %collective-permute-start.11 = (f32[64,512]{1,0:T(8,128)S(1)}, f32[64,512]{1,0:T(8,128)S(1)}, u32[]{:S(2)}, u32[]{:S(2)}) collective-permute-start(f32[64,512]{1,0:T(8,128)S(1)} %shard_map.88.token.refs_0_), channel_id=1, source_target_pairs={{4,0},{5,1},{12,8},{13,9},{20,16},{21,17},{28,24},{29,25}} | collective-permute-start | bytes 393224 | tf_op jit(solution)/shard_map/ppermute | solution.py:292
  52.6 6.9 %collective-permute-start.12 = (f32[64,512]{1,0:T(8,128)S(1)}, f32[64,512]{1,0:T(8,128)S(1)}, u32[]{:S(2)}, u32[]{:S(2)}) collective-permute-start(f32[64,512]{1,0:T(8,128)S(1)} %shard_map.89.token.refs_0_), channel_id=1, source_target_pairs={{4,0},{5,1},{12,8},{13,9},{20,16},{21,17},{28,24},{29,25}} | collective-permute-start | bytes 393224 | tf_op jit(solution)/shard_map/ppermute | solution.py:292
  54.4 6.3 %collective-permute-start.13 = (f32[64,512]{1,0:T(8,128)S(1)}, f32[64,512]{1,0:T(8,128)S(1)}, u32[]{:S(2)}, u32[]{:S(2)}) collective-permute-start(f32[64,512]{1,0:T(8,128)S(1)} %shard_map.90.token.refs_0_), channel_id=1, source_target_pairs={{8,4},{9,5},{16,12},{17,13},{24,20},{25,21}} | collective-permute-start | bytes 393224 | tf_op jit(solution)/shard_map/ppermute | solution.py:292
  60.0 1.4 %collective-permute-start.14 = (f32[64,512]{1,0:T(8,128)S(1)}, f32[64,512]{1,0:T(8,128)S(1)}, u32[]{:S(2)}, u32[]{:S(2)}) collective-permute-start(f32[64,512]{1,0:T(8,128)S(1)} %shard_map.91.token.refs_0_), channel_id=1, source_target_pairs={{8,4},{9,5},{16,12},{17,13},{24,20},{25,21}} | collective-permute-start | bytes 393224 | tf_op jit(solution)/shard_map/ppermute | solution.py:292
  60.8 1.4 %collective-permute-start.15 = (f32[64,512]{1,0:T(8,128)S(1)}, f32[64,512]{1,0:T(8,128)S(1)}, u32[]{:S(2)}, u32[]{:S(2)}) collective-permute-start(f32[64,512]{1,0:T(8,128)S(1)} %shard_map.92.token.refs_0_), channel_id=1, source_target_pairs={{4,2},{5,3},{8,6},{9,7},{12,10},{13,11},{16,14},{17,15},{20,18},{2... | collective-permute-start | bytes 393224 | tf_op jit(solution)/shard_map/ppermute | solution.py:292
  61.5 2.0 %collective-permute-start.16 = (f32[64,512]{1,0:T(8,128)S(1)}, f32[64,512]{1,0:T(8,128)S(1)}, u32[]{:S(2)}, u32[]{:S(2)}) collective-permute-start(f32[64,512]{1,0:T(8,128)S(1)} %shard_map.93.token.refs_0_), channel_id=1, source_target_pairs={{4,2},{5,3},{8,6},{9,7},{12,10},{13,11},{16,14},{17,15},{20,18},{2... | collective-permute-start | bytes 393224 | tf_op jit(solution)/shard_map/ppermute | solution.py:292
  62.2 10.5 %collective-permute-start.17 = (f32[64,512]{1,0:T(8,128)S(1)}, f32[64,512]{1,0:T(8,128)S(1)}, u32[]{:S(2)}, u32[]{:S(2)}) collective-permute-start(f32[64,512]{1,0:T(8,128)S(1)} %shard_map.94.token.values), channel_id=1, source_target_pairs={{2,0},{3,1},{4,2},{5,3},{6,4},{7,5},{8,6},{9,7},{10,8},{11,9},{12,... | collective-permute-start | bytes 393224 | tf_op jit(solution)/shard_map/ppermute | solution.py:292
  63.6 13.1 %collective-permute-start.18 = (f32[64,512]{1,0:T(8,128)S(1)}, f32[64,512]{1,0:T(8,128)S(1)}, u32[]{:S(2)}, u32[]{:S(2)}) collective-permute-start(f32[64,512]{1,0:T(8,128)S(1)} %shard_map.95.token.values), channel_id=1, source_target_pairs={{2,0},{3,1},{4,2},{5,3},{6,4},{7,5},{8,6},{9,7},{10,8},{11,9},{12,... | collective-permute-start | bytes 393224 | tf_op jit(solution)/shard_map/ppermute | solution.py:292
  77.2 9.2 %collective-permute-start.20 = (f32[2,64,512]{2,1,0:T(8,128)S(1)}, f32[2,64,512]{2,1,0:T(8,128)S(1)}, u32[]{:S(2)}, u32[]{:S(2)}) collective-permute-start(f32[2,64,512]{2,1,0:T(8,128)S(1)} %get-tuple-element.66), channel_id=1, source_target_pairs={{0,1},{1,0},{2,3},{3,2},{4,5},{5,4},{6,7},{7,6},{8,9},{9,8},{10,11... | collective-permute-start | bytes 786440 | tf_op jit(solution)/shard_map/ppermute | solution.py:292
  85.3 1.5 %collective-permute-start.19 = (f32[2,64,512]{2,1,0:T(8,128)S(1)}, f32[2,64,512]{2,1,0:T(8,128)S(1)}, u32[]{:S(2)}, u32[]{:S(2)}) collective-permute-start(f32[2,64,512]{2,1,0:T(8,128)S(1)} %get-tuple-element.65), channel_id=1, source_target_pairs={{0,1},{1,0},{2,3},{3,2},{4,5},{5,4},{6,7},{7,6},{8,9},{9,8},{10,11... | collective-permute-start | bytes 786440 | tf_op jit(solution)/shard_map/ppermute | solution.py:292

commit v4 on v3

v4 whole, which is shorter than its diff:
```python
import functools

import jax
import jax.numpy as jnp
from jax import lax
from jax.experimental import pallas as pl
from jax.experimental.pallas import tpu as pltpu
from jax.sharding import PartitionSpec as P


LEVELS = 4
CHUNKS = 2
F32, BF16 = jnp.float32, jnp.bfloat16
VMEM = pl.BlockSpec(memory_space=pltpu.VMEM)
ANY = pl.BlockSpec(memory_space=pl.ANY)


def dot(a, b):
    return jnp.dot(a, b, preferred_element_type=F32)


def held(value):
    return pltpu.with_memory_space_constraint(value, pltpu.VMEM)


def in_hbm(value):
    return pltpu.with_memory_space_constraint(value, pltpu.HBM)


def core():
    return lax.rem(lax.axis_index("depth"), 2)


def on_core(which):
    return pl.when(core() == which)


def tangent(vector, out_t, slope):
    return (dot(vector.astype(BF16), out_t) * slope).astype(BF16)


def apply_slot(value, factor, slot, rows, in3, out3, slope3):
    return value + factor * dot(tangent(value, out3[slot], slope3[slot, rows, :]), in3[slot])


def pack_kernel(start_h, w_in_h, w_out_h, packed, start, w_in, w_out, sems):
    copies = [
        pltpu.make_async_copy(w_in_h.at[0], w_in, sems.at[0]),
        pltpu.make_async_copy(w_out_h.at[0], w_out, sems.at[1]),
        pltpu.make_async_copy(start_h.at[0], start, sems.at[2]),
    ]
    for copy in copies:
        copy.start()
    d, ff = w_in.shape
    copies[0].wait()

    @on_core(0)
    def _():
        for i in range(ff // d):
            packed[i * d : (i + 1) * d, :] = w_in[:, i * d : (i + 1) * d].astype(F32)

    copies[1].wait()
    copies[2].wait()

    @on_core(0)
    def _():
        packed[ff : 2 * ff, :] = w_out[...].astype(F32)
        packed[2 * ff :, :] = start[...].astype(F32)


def forward_kernel(
    token, w_in_h, w_out_h, start, w_in0, w_out0,
    in3, out3, slope3, state_t, act_t,
    w_in1, w_out1, upper_v, sems,
):
    copies = [
        pltpu.make_async_copy(w_in_h.at[1], w_in1, sems.at[0]),
        pltpu.make_async_copy(w_out_h.at[1], w_out1, sems.at[1]),
    ]
    for copy in copies:
        copy.start()
    h_zero = jnp.tanh(dot(start[...], w_in0[...]))
    slope3[1] = 1.0 - h_zero * h_zero
    act_zero = h_zero.astype(BF16)
    act_t[0] = act_zero.T
    upper_v[...] = (start[...].astype(F32) + dot(act_zero, w_out0[...])).astype(BF16)
    copies[0].wait()
    h_one = jnp.tanh(dot(upper_v[...], w_in1[...]))
    slope3[2] = 1.0 - h_one * h_one
    act_t[1] = h_one.astype(BF16).T
    in3[1] = w_in0[...].T
    out3[1] = w_out0[...].T
    in3[2] = w_in1[...].T
    state_t[0] = start[...].T
    state_t[1] = upper_v[...].T
    copies[1].wait()
    out3[2] = w_out1[...].T


def residual_kernel(token, moved, guess, in3, out3, slope3, resid):
    @on_core(0)
    def _():
        rows = slice(None)
        odd = apply_slot(moved[...], 1.0, 2, rows, in3, out3, slope3)
        resid[...] = apply_slot(odd, 1.0, 1, rows, in3, out3, slope3) - guess[...]


def adopt_kernel(token, packed, in_i, out_i, slope_i, in3, out3, slope3):
    @on_core(1)
    def _():
        ff, d = in3.shape[1:]
        state = packed[2 * ff :, :].astype(BF16)
        for i in range(ff // d):
            rows = slice(i * d, (i + 1) * d)
            part = packed[rows, :].astype(BF16)
            h = jnp.tanh(dot(state, part))
            slope3[0, :, rows] = 1.0 - h * h
            in3[0, rows, :] = part.T
        out3[0] = packed[ff : 2 * ff, :].astype(BF16).T


def value_kernel(low, size, token, moved_in, moved_x, terminal, guess, resid_even, in3, out3, slope3, above, resid, value):
    rows = pl.ds(low, size)
    at_end = lax.axis_index("depth") == lax.axis_size("depth") - 1

    @on_core(0)
    def _():
        above[...] = moved_in[rows, :]
        resid[...] = jnp.zeros(resid.shape, F32)
        value[...] = jnp.zeros(value.shape, F32)

    @on_core(1)
    def _():
        above[...] = moved_x[rows, :]

        @pl.when(at_end)
        def _():
            above[...] = terminal[rows, :]

        odd = apply_slot(above[...], 1.0, 2, rows, in3, out3, slope3)
        own = apply_slot(odd, 1.0, 1, rows, in3, out3, slope3) - guess[rows, :]
        resid[...] = own
        value[...] = apply_slot(own, 2.0, 0, rows, in3, out3, slope3) + resid_even[rows, :]


def phi_kernel(low, size, steps, period, phase, token, vector, in3, out3, slope3, *refs):
    result = refs[-1]
    place = lax.axis_index("depth")
    active = lax.rem(place, 2 * period) == 2 * phase + 1
    rows = pl.ds(low, size)

    def finish(total):
        for addend in refs[:-1]:
            total = total + addend[...]
        result[...] = total

    @pl.when(active)
    def _():
        value = vector[...]
        for slot, factor in steps:
            value = apply_slot(value, factor, slot, rows, in3, out3, slope3)
        finish(value)

    @pl.when(jnp.logical_not(active))
    def _():
        finish(jnp.zeros(result.shape, F32))


def final_kernel(low, size, token, arrived, resid, guess, above0, in3, out3, slope3, last_odd, even, above):
    @on_core(1)
    def _():
        rows = pl.ds(low, size)
        last = apply_slot(arrived[...], 2.0, 1, rows, in3, out3, slope3) + resid[...]
        last_odd[...] = last
        even[...] = guess[rows, :] + last
        above[...] = above0[...] + arrived[...]


def settle(low, size, sent_even, sent_odd, above0, guess, even, above):
    @on_core(0)
    def _():
        even[...] = guess[pl.ds(low, size), :] + sent_even[...]
        above[...] = above0[...] + sent_odd[...]


def part_kernel(low, size, token, in3, out3, slope3, guess, sent_even, sent_odd, above0, even_1, above_1, even, odd, above_b, odd_b, tan, above_v):
    rows = pl.ds(low, size)

    @on_core(1)
    def _():
        even[...] = even_1[...]
        above_v[...] = above_1[...]

    settle(low, size, sent_even, sent_odd, above0, guess, even, above_v)
    value = above_v[...]
    above_b[...] = value.astype(BF16)
    tan_one = tangent(value, out3[2], slope3[2, rows, :])
    tan[1] = tan_one
    value = value + dot(tan_one, in3[2])
    odd[...] = value
    odd_b[...] = value.astype(BF16)
    tan[0] = tangent(value, out3[1], slope3[1, rows, :])


def finish_kernel(lows, sizes, token, in3, out3, slope3, guess, sent_even, sent_odd, above0, even_1, above_1, state_t, act_t, *refs):
    chunks = len(lows)
    parts = [refs[5 * i : 5 * i + 5] for i in range(chunks - 1)]
    adjoint, grad_in, grad_out, even, odd, above, grad_in_v, grad_out_v, sems = refs[5 * (chunks - 1) :]
    low, size = lows[-1], sizes[-1]
    rows = pl.ds(low, size)
    copies = []

    def send(source, target):
        copy = pltpu.make_async_copy(source, target, sems.at[len(copies)])
        copy.start()
        copies.append(copy)

    for i in range(chunks - 1):
        send(parts[i][0], adjoint.at[0, pl.ds(lows[i], sizes[i]), :])
        send(parts[i][1], adjoint.at[1, pl.ds(lows[i], sizes[i]), :])

    @on_core(1)
    def _():
        even[...] = even_1[...]
        above[...] = above_1[...]

    settle(low, size, sent_even, sent_odd, above0, guess, even, above)
    send(even, adjoint.at[0, rows, :])

    def product(left, earlier, last):
        return dot(left, jnp.concatenate([*earlier, last], 0)).astype(BF16)

    value = above[...]
    grad_out_v[1] = product(act_t[1], [part[2][...] for part in parts], value.astype(BF16))
    send(grad_out_v.at[1], grad_out.at[1])
    tan_one = tangent(value, out3[2], slope3[2, rows, :])
    grad_in_v[1] = product(state_t[1], [part[4][1] for part in parts], tan_one)
    send(grad_in_v.at[1], grad_in.at[1])
    value = value + dot(tan_one, in3[2])
    odd[...] = value
    send(odd, adjoint.at[1, rows, :])
    grad_out_v[0] = product(act_t[0], [part[3][...] for part in parts], value.astype(BF16))
    send(grad_out_v.at[0], grad_out.at[0])
    tan_zero = tangent(value, out3[1], slope3[1, rows, :])
    tangents = jnp.concatenate([*[part[4][0] for part in parts], tan_zero], 0)
    pieces = 2
    piece = state_t.shape[1] // pieces
    for i in range(pieces):
        some = pl.ds(i * piece, piece)
        grad_in_v[0, some, :] = dot(state_t[0, some, :], tangents).astype(BF16)
        send(grad_in_v.at[0, some, :], grad_in.at[0, some, :])
    for copy in copies:
        copy.wait()


def local(w_in, w_out, checkpoint, guess, terminal):
    count = lax.axis_size("depth")
    rows, d = terminal.shape
    ff = w_in.shape[2]
    edges = [rows * i // CHUNKS // 16 * 16 for i in range(CHUNKS + 1)]
    lows, sizes = edges[:-1], [high - low for low, high in zip(edges, edges[1:])]
    token = []

    def run(kernel, shapes, operands, from_hbm=0, outs=None, mib=16, **options):
        specs = [VMEM] * len(token) + [ANY] * from_hbm + [VMEM] * (len(operands) - from_hbm)
        results = pl.pallas_call(
            kernel,
            out_shape=tuple(shapes),
            in_specs=specs,
            out_specs=outs or [VMEM] * len(shapes),
            compiler_params=pltpu.CompilerParams(vmem_limit_bytes=mib * 2**20),
            **options,
        )(*token, *operands)
        if outs:
            return results
        results = [held(result) for result in results]
        token[:] = [results[-1]]
        return results

    def permute(value, route):
        return held(lax.ppermute(value, "depth", route))

    def shift(value, period, phase, distance):
        route = [(2 * c + 1, 2 * (c - distance) + 1) for c in range(distance, count // 2) if c % period == phase]
        return permute(value, route)

    to_core_0 = [(i + 1, i) for i in range(0, count, 2)]
    to_core_1 = [(i, i + 1) for i in range(0, count, 2)]

    def vmem(*shape, kind=F32):
        return pltpu.VMEM(shape, kind)

    guess = guess.reshape(rows, d)
    packed, start, w_in0, w_out0 = run(
        pack_kernel,
        (vmem(2 * ff + rows, d), vmem(rows, d, kind=BF16), vmem(d, ff, kind=BF16), vmem(ff, d, kind=BF16)),
        (in_hbm(checkpoint), in_hbm(w_in), in_hbm(w_out)),
        from_hbm=3,
        scratch_shapes=[pltpu.SemaphoreType.DMA((3,))],
    )
    packed = permute(packed, to_core_1)
    moved_x = permute(guess, [(i, i - 1) for i in range(2, count, 2)])
    moved_in = permute(guess, to_core_0)
    guess, terminal = held(guess), held(terminal)
    layers = (vmem(3, ff, d, kind=BF16), vmem(3, d, ff, kind=BF16), vmem(3, rows, ff))
    *weights, state_t, act_t = run(
        forward_kernel,
        (*layers, vmem(2, d, rows, kind=BF16), vmem(2, ff, rows, kind=BF16)),
        (in_hbm(w_in), in_hbm(w_out), start, w_in0, w_out0),
        from_hbm=2,
        mib=24,
        scratch_shapes=[
            vmem(d, ff, kind=BF16),
            vmem(ff, d, kind=BF16),
            vmem(rows, d, kind=BF16),
            pltpu.SemaphoreType.DMA((2,)),
        ],
    )
    (resid_even,) = run(residual_kernel, (vmem(rows, d),), (moved_in, guess, *weights))
    resid_even = permute(resid_even, to_core_1)
    weights = run(adopt_kernel, layers, (packed, *weights), input_output_aliases={2: 0, 3: 1, 4: 2})

    def next_chip(value):
        return shift(value, 1, 0, 1)

    above0, resid, values, sent = [], [], [], []
    for low, size in zip(lows, sizes):
        outs = run(
            functools.partial(value_kernel, low, size),
            (vmem(size, d),) * 3,
            (moved_in, moved_x, terminal, guess, resid_even, *weights),
        )
        for group, value in zip((above0, resid, values), outs):
            group.append(value)
        sent.append(next_chip(outs[2]))

    def phi(received, steps, period, phase, send, *addends):
        results, sent = [], []
        for i in range(CHUNKS):
            (result,) = run(
                functools.partial(phi_kernel, lows[i], sizes[i], steps, period, phase),
                (vmem(sizes[i], d),),
                (received[i], *weights, *[addend[i] for addend in addends]),
            )
            results.append(result)
            sent.append(send(result))
        return results, sent

    def cycle(level, rhs, sent, addend, send):
        distance = 2 ** (level - 2)
        period, steps = 2 * distance, ((0, float(2**level)),)

        def down(value):
            return shift(value, period, distance, distance)

        def up(value):
            return shift(value, period, 0, distance)

        point, sent = phi(sent, steps, period, 0, up, rhs)
        if level < LEVELS - 1:
            _, sent = phi(sent, steps, period, distance, down)
            deeper = 2 * distance
            resid, sent = phi(sent, steps, period, 0, lambda value: shift(value, 2 * deeper, deeper, deeper))
            point, sent = cycle(level + 1, resid, sent, point, up)
        return phi(sent, steps, period, distance, send, point, addend)

    coarse, sent = phi(sent, ((1, 2.0), (0, 2.0)), 1, 0, lambda value: shift(value, 2, 1, 1))
    values, sent = cycle(2, coarse, sent, values, next_chip)

    sent_even = [permute(value, to_core_0) for value in values]
    lasts = []
    for i, (low, size) in enumerate(zip(lows, sizes)):
        odd, even, above = run(
            functools.partial(final_kernel, low, size),
            (vmem(size, d), vmem(size, d), vmem(size, d)),
            (sent[i], resid[i], guess, above0[i], *weights),
        )
        lasts.append((guess, sent_even[i], permute(odd, to_core_0), above0[i], even, above))
    parts = []
    for low, size, last in zip(lows[:-1], sizes, lasts):
        parts += run(
            functools.partial(part_kernel, low, size),
            (
                vmem(size, d),
                vmem(size, d),
                vmem(size, d, kind=BF16),
                vmem(size, d, kind=BF16),
                vmem(2, size, ff, kind=BF16),
            ),
            (*weights, *last),
            scratch_shapes=[vmem(size, d)],
        )
    return run(
        functools.partial(finish_kernel, lows, sizes),
        (
            jax.ShapeDtypeStruct((2, rows, d), F32),
            jax.ShapeDtypeStruct((2, d, ff), BF16),
            jax.ShapeDtypeStruct((2, ff, d), BF16),
        ),
        (*weights, *lasts[-1], state_t, act_t, *parts),
        outs=[ANY] * 3,
        mib=24,
        scratch_shapes=[
            vmem(sizes[-1], d),
            vmem(sizes[-1], d),
            vmem(sizes[-1], d),
            vmem(2, d, ff, kind=BF16),
            vmem(2, ff, d, kind=BF16),
            pltpu.SemaphoreType.DMA((2 * CHUNKS + 5,)),
        ],
    )


def solution(mesh):
    split = P("depth", None, None)

    return jax.shard_map(
        local,
        mesh=mesh,
        in_specs=(split, split, split, split, P()),
        out_specs=(split, split, split),
        check_vma=False,
    )
```

time: 91.3 us -> 90.7 us (level)
  waiting for transfers between devices: 43.6 us -> 41.2 us
  starting transfers between devices: 27.6 us -> 29.6 us
    ppermute x21 -> x24, waiting for transfers between devices: 43.6 us -> 41.2 us  [permute(): return held(lax.ppermute(value, 'depth', route))]
    ppermute x21 -> x24, starting transfers between devices: 27.6 us -> 29.6 us  [permute(): return held(lax.ppermute(value, 'depth', route))]
  transfers between devices with their start and end apart: 21 -> 24, of which waited for: 12 -> 12; matrix products, arithmetic and copies ran while one was open for 0% -> 0% of each run, Pallas kernels for 13% -> 13%
where the time goes in v4:
time: 90.7 us; the launch traced here: 89.8 us
  waiting for transfers between devices  41.2 us (45%)
  starting transfers between devices  29.6 us (33%)
  Pallas kernels  17.7 us (20%)
  between operations  1.28 us (1%)
    ppermute x24, waiting for transfers between devices, permute(): return held(lax.ppermute(value, 'depth', route))  41.2 us
    ppermute x24, starting transfers between devices, permute(): return held(lax.ppermute(value, 'depth', route))  29.6 us
    pallas_call x24, Pallas kernels, run(): pl.pallas_call(kernel, out_shape=tuple(shapes), in_specs=specs, out_specs...  17.7 us
  transfers between devices with their start and end apart: 24, of which 12 were waited for; matrix products, arithmetic and copies ran while one was open for 0% of the time, Pallas kernels for 13%

profile of v4, /device:TPU:1, one launch (start us, length us, event | category | flops | bytes accessed | tf_op | source)
XLA Modules:
  0.0 89.8 jit_solution(2336412828191514405)
XLA Ops:
  0.6 1.7 %shard_map.76 = (f32[2304,512]{1,0:T(8,128)S(1)}, bf16[256,512]{1,0:T(8,128)(2,1)S(1)}, bf16[512,1024]{1,0:T(8,128)(2,1)S(1)}, bf16[1024,512]{1,0:T(8,128)(2,1)S(1)}) custom-call(bf16[1,256,512]{2,1,0:T(8,128)(2,1)} %start_h.1, bf16[2,512,1024]{2,1,0:T(8,128)(2,1)} %w_in_h.3, bf16[2,1024,512]{2,1,0:T(8,128)(2,1)} %w_out_h.3), custom_call_target="tpu_custom_call" | custom-call | tf_op jit(solution)/shard_map/pallas_call | solution.py:266
  2.3 1.3 %collective-permute-start.1 = (f32[2304,512]{1,0:T(8,128)S(1)}, f32[2304,512]{1,0:T(8,128)S(1)}, u32[]{:S(2)}, u32[]{:S(2)}) collective-permute-start(f32[2304,512]{1,0:T(8,128)S(1)} %get-tuple-element.39), channel_id=1, source_target_pairs={{0,1},{2,3},{4,5},{6,7},{8,9},{10,11},{12,13},{14,15},{16,17},{18,... | collective-permute-start | bytes 14155784 | tf_op jit(solution)/shard_map/ppermute | solution.py:281
  3.6 3.4 %collective-permute-start = (f32[256,512]{1,0:T(8,128)S(1)}, f32[256,512]{1,0:T(8,128)S(1)}, u32[]{:S(2)}, u32[]{:S(2)}) collective-permute-start(f32[256,512]{1,0:T(8,128)S(1)} %bitcast.1), channel_id=1, source_target_pairs={{1,0},{3,2},{5,4},{7,6},{9,8},{11,10},{13,12},{15,14},{17,16},{19,... | collective-permute-start | bytes 1572872 | tf_op jit(solution)/shard_map/ppermute | solution.py:281
  7.0 1.3 %collective-permute-start.2 = (f32[256,512]{1,0:T(8,128)S(1)}, f32[256,512]{1,0:T(8,128)S(1)}, u32[]{:S(2)}, u32[]{:S(2)}) collective-permute-start(f32[256,512]{1,0:T(8,128)S(1)} %bitcast.2), channel_id=1, source_target_pairs={{2,1},{4,3},{6,5},{8,7},{10,9},{12,11},{14,13},{16,15},{18,17},{20... | collective-permute-start | bytes 1572872 | tf_op jit(solution)/shard_map/ppermute | solution.py:281
  8.3 2.8 %shard_map.77 = (bf16[3,1024,512]{2,1,0:T(8,128)(2,1)S(1)}, bf16[3,512,1024]{2,1,0:T(8,128)(2,1)S(1)}, f32[3,256,1024]{2,1,0:T(8,128)S(1)}, bf16[2,512,256]{2,1,0:T(8,128)(2,1)S(1)}, bf16[2,1024,256]{2,1,0:T(8,128)(2,1)S(1)}) custom-call(bf16[1024,512]{1,0:T(8,128)(2,1)S(1)} %get-tuple-element.32.token.w_out0, bf16[2,512,1024]{2,1,0:T(8,128)(2,1)} %w_in_h.3, ...), custom_call_target="tpu_custom_call" | custom-call | tf_op jit(solution)/shard_map/pallas_call | solution.py:266
  11.2 1.4 %collective-permute-start.3 = (f32[256,512]{1,0:T(8,128)S(1)}, f32[256,512]{1,0:T(8,128)S(1)}, u32[]{:S(2)}, u32[]{:S(2)}) collective-permute-start(f32[256,512]{1,0:T(8,128)S(1)} %shard_map.78.token), channel_id=1, source_target_pairs={{0,1},{2,3},{4,5},{6,7},{8,9},{10,11},{12,13},{14,15},{16,17},{18,... | collective-permute-start | bytes 1572872 | tf_op jit(solution)/shard_map/ppermute | solution.py:281
  13.3 4.2 %collective-permute-done.2.moved_x = f32[256,512]{1,0:T(8,128)S(1)} collective-permute-done((f32[256,512]{1,0:T(8,128)S(1)}, f32[256,512]{1,0:T(8,128)S(1)}, u32[]{:S(2)}, u32[]{:S(2)}) %collective-permute-start.2) | collective-permute-done | bytes 524320 | tf_op jit(solution)/shard_map/ppermute | solution.py:281
  17.5 1.3 %shard_map.80 = (f32[128,512]{1,0:T(8,128)S(1)}, f32[128,512]{1,0:T(8,128)S(1)}, f32[128,512]{1,0:T(8,128)S(1)}) custom-call(f32[3,256,1024]{2,1,0:T(8,128)S(1)} %get-tuple-element.40.token.slope3, f32[256,512]{1,0:T(8,128)S(1)} %collective-permute-done.moved.moved_in, f32[256,512]{1,0:T(8,128)S(1)} %collective-permute-done.2.moved_x, ...), custom_call_target="tpu_custom_call" | custom-call | tf_op jit(solution)/shard_map/pallas_call | solution.py:266
  18.8 1.3 %collective-permute-start.4 = (f32[128,512]{1,0:T(8,128)S(1)}, f32[128,512]{1,0:T(8,128)S(1)}, u32[]{:S(2)}, u32[]{:S(2)}) collective-permute-start(f32[128,512]{1,0:T(8,128)S(1)} %get-tuple-element.43.token.refs_1_), channel_id=1, source_target_pairs={{3,1},{5,3},{7,5},{9,7},{11,9},{13,11},{15,13},{17,15},{19,17},{21... | collective-permute-start | bytes 786440 | tf_op jit(solution)/shard_map/ppermute | solution.py:281
  20.1 1.3 %shard_map.81 = (f32[128,512]{1,0:T(8,128)S(1)}, f32[128,512]{1,0:T(8,128)S(1)}, f32[128,512]{1,0:T(8,128)S(1)}) custom-call(f32[128,512]{1,0:T(8,128)S(1)} %get-tuple-element.43.token.refs_1_, f32[256,512]{1,0:T(8,128)S(1)} %collective-permute-done.moved.moved_in, f32[256,512]{1,0:T(8,128)S(1)} %collective-permute-done.2.moved_x, f32[256,512]{1,0:T(8,128)S(1)} %copy-done.1, ...), custom_call_target="tpu_custom_call" | custom-call | tf_op jit(solution)/shard_map/pallas_call | solution.py:266
  21.5 1.3 %collective-permute-start.5 = (f32[128,512]{1,0:T(8,128)S(1)}, f32[128,512]{1,0:T(8,128)S(1)}, u32[]{:S(2)}, u32[]{:S(2)}) collective-permute-start(f32[128,512]{1,0:T(8,128)S(1)} %get-tuple-element.44.token.refs_1_), channel_id=1, source_target_pairs={{3,1},{5,3},{7,5},{9,7},{11,9},{13,11},{15,13},{17,15},{19,17},{21... | collective-permute-start | bytes 786440 | tf_op jit(solution)/shard_map/ppermute | solution.py:281
  22.8 4.6 %collective-permute-done.4.vector = f32[128,512]{1,0:T(8,128)S(1)} collective-permute-done((f32[128,512]{1,0:T(8,128)S(1)}, f32[128,512]{1,0:T(8,128)S(1)}, u32[]{:S(2)}, u32[]{:S(2)}) %collective-permute-start.4) | collective-permute-done | bytes 262176 | tf_op jit(solution)/shard_map/ppermute | solution.py:281
  28.3 1.3 %collective-permute-start.6 = (f32[128,512]{1,0:T(8,128)S(1)}, f32[128,512]{1,0:T(8,128)S(1)}, u32[]{:S(2)}, u32[]{:S(2)}) collective-permute-start(f32[128,512]{1,0:T(8,128)S(1)} %shard_map.82.token.refs_0_), channel_id=1, source_target_pairs={{3,1},{7,5},{11,9},{15,13},{19,17},{23,21},{27,25},{31,29}} | collective-permute-start | bytes 786440 | tf_op jit(solution)/shard_map/ppermute | solution.py:281
  31.6 1.3 %collective-permute-start.7 = (f32[128,512]{1,0:T(8,128)S(1)}, f32[128,512]{1,0:T(8,128)S(1)}, u32[]{:S(2)}, u32[]{:S(2)}) collective-permute-start(f32[128,512]{1,0:T(8,128)S(1)} %shard_map.83.token.refs_0_), channel_id=1, source_target_pairs={{3,1},{7,5},{11,9},{15,13},{19,17},{23,21},{27,25},{31,29}} | collective-permute-start | bytes 786440 | tf_op jit(solution)/shard_map/ppermute | solution.py:281
  32.9 2.8 %collective-permute-done.6.vector = f32[128,512]{1,0:T(8,128)S(1)} collective-permute-done((f32[128,512]{1,0:T(8,128)S(1)}, f32[128,512]{1,0:T(8,128)S(1)}, u32[]{:S(2)}, u32[]{:S(2)}) %collective-permute-start.6) | collective-permute-done | bytes 262176 | tf_op jit(solution)/shard_map/ppermute | solution.py:281
  36.9 2.1 %collective-permute-done.7.vector = f32[128,512]{1,0:T(8,128)S(1)} collective-permute-done((f32[128,512]{1,0:T(8,128)S(1)}, f32[128,512]{1,0:T(8,128)S(1)}, u32[]{:S(2)}, u32[]{:S(2)}) %collective-permute-start.7) | collective-permute-done | bytes 262176 | tf_op jit(solution)/shard_map/ppermute | solution.py:281
  40.2 1.3 %collective-permute-start.10 = (f32[128,512]{1,0:T(8,128)S(1)}, f32[128,512]{1,0:T(8,128)S(1)}, u32[]{:S(2)}, u32[]{:S(2)}) collective-permute-start(f32[128,512]{1,0:T(8,128)S(1)} %shard_map.86.token), channel_id=1, source_target_pairs={{3,1},{7,5},{11,9},{15,13},{19,17},{23,21},{27,25},{31,29}} | collective-permute-start | bytes 786440 | tf_op jit(solution)/shard_map/ppermute | solution.py:281
  41.5 1.3 %collective-permute-start.11 = (f32[128,512]{1,0:T(8,128)S(1)}, f32[128,512]{1,0:T(8,128)S(1)}, u32[]{:S(2)}, u32[]{:S(2)}) collective-permute-start(f32[128,512]{1,0:T(8,128)S(1)} %shard_map.87.token), channel_id=1, source_target_pairs={{3,1},{7,5},{11,9},{15,13},{19,17},{23,21},{27,25},{31,29}} | collective-permute-start | bytes 786440 | tf_op jit(solution)/shard_map/ppermute | solution.py:281
  42.8 8.1 %collective-permute-done.10.vector = f32[128,512]{1,0:T(8,128)S(1)} collective-permute-done((f32[128,512]{1,0:T(8,128)S(1)}, f32[128,512]{1,0:T(8,128)S(1)}, u32[]{:S(2)}, u32[]{:S(2)}) %collective-permute-start.10) | collective-permute-done | bytes 262176 | tf_op jit(solution)/shard_map/ppermute | solution.py:281
  51.5 1.3 %collective-permute-start.12 = (f32[128,512]{1,0:T(8,128)S(1)}, f32[128,512]{1,0:T(8,128)S(1)}, u32[]{:S(2)}, u32[]{:S(2)}) collective-permute-start(f32[128,512]{1,0:T(8,128)S(1)} %shard_map.88.token.refs_0_), channel_id=1, source_target_pairs={{5,1},{13,9},{21,17},{29,25}} | collective-permute-start | bytes 786440 | tf_op jit(solution)/shard_map/ppermute | solution.py:281
  52.8 1.5 %collective-permute-done.11.vector = f32[128,512]{1,0:T(8,128)S(1)} collective-permute-done((f32[128,512]{1,0:T(8,128)S(1)}, f32[128,512]{1,0:T(8,128)S(1)}, u32[]{:S(2)}, u32[]{:S(2)}) %collective-permute-start.11) | collective-permute-done | bytes 262176 | tf_op jit(solution)/shard_map/ppermute | solution.py:281
  54.7 1.3 %collective-permute-start.13 = (f32[128,512]{1,0:T(8,128)S(1)}, f32[128,512]{1,0:T(8,128)S(1)}, u32[]{:S(2)}, u32[]{:S(2)}) collective-permute-start(f32[128,512]{1,0:T(8,128)S(1)} %shard_map.89.token.refs_0_), channel_id=1, source_target_pairs={{5,1},{13,9},{21,17},{29,25}} | collective-permute-start | bytes 786440 | tf_op jit(solution)/shard_map/ppermute | solution.py:281
  56.0 2.5 %collective-permute-done.12.vector = f32[128,512]{1,0:T(8,128)S(1)} collective-permute-done((f32[128,512]{1,0:T(8,128)S(1)}, f32[128,512]{1,0:T(8,128)S(1)}, u32[]{:S(2)}, u32[]{:S(2)}) %collective-permute-start.12) | collective-permute-done | bytes 262176 | tf_op jit(solution)/shard_map/ppermute | solution.py:281
  59.7 2.4 %collective-permute-done.13.vector = f32[128,512]{1,0:T(8,128)S(1)} collective-permute-done((f32[128,512]{1,0:T(8,128)S(1)}, f32[128,512]{1,0:T(8,128)S(1)}, u32[]{:S(2)}, u32[]{:S(2)}) %collective-permute-start.13) | collective-permute-done | bytes 262176 | tf_op jit(solution)/shard_map/ppermute | solution.py:281
  64.9 1.3 %collective-permute-start.18 = (f32[128,512]{1,0:T(8,128)S(1)}, f32[128,512]{1,0:T(8,128)S(1)}, u32[]{:S(2)}, u32[]{:S(2)}) collective-permute-start(f32[128,512]{1,0:T(8,128)S(1)} %shard_map.94.token), channel_id=1, source_target_pairs={{3,1},{5,3},{7,5},{9,7},{11,9},{13,11},{15,13},{17,15},{19,17},{21... | collective-permute-start | bytes 786440 | tf_op jit(solution)/shard_map/ppermute | solution.py:281
  67.5 1.3 %collective-permute-start.20 = (f32[128,512]{1,0:T(8,128)S(1)}, f32[128,512]{1,0:T(8,128)S(1)}, u32[]{:S(2)}, u32[]{:S(2)}) collective-permute-start(f32[128,512]{1,0:T(8,128)S(1)} %shard_map.94.token), channel_id=1, source_target_pairs={{1,0},{3,2},{5,4},{7,6},{9,8},{11,10},{13,12},{15,14},{17,16},{19,... | collective-permute-start | bytes 786440 | tf_op jit(solution)/shard_map/ppermute | solution.py:281
  68.8 1.3 %collective-permute-start.22 = (f32[128,512]{1,0:T(8,128)S(1)}, f32[128,512]{1,0:T(8,128)S(1)}, u32[]{:S(2)}, u32[]{:S(2)}) collective-permute-start(f32[128,512]{1,0:T(8,128)S(1)} %shard_map.95.token), channel_id=1, source_target_pairs={{1,0},{3,2},{5,4},{7,6},{9,8},{11,10},{13,12},{15,14},{17,16},{19,... | collective-permute-start | bytes 786440 | tf_op jit(solution)/shard_map/ppermute | solution.py:281
  70.1 10.1 %collective-permute-done.18.arrived = f32[128,512]{1,0:T(8,128)S(1)} collective-permute-done((f32[128,512]{1,0:T(8,128)S(1)}, f32[128,512]{1,0:T(8,128)S(1)}, u32[]{:S(2)}, u32[]{:S(2)}) %collective-permute-start.18) | collective-permute-done | bytes 262176 | tf_op jit(solution)/shard_map/ppermute | solution.py:281
  80.7 1.3 %collective-permute-start.21 = (f32[128,512]{1,0:T(8,128)S(1)}, f32[128,512]{1,0:T(8,128)S(1)}, u32[]{:S(2)}, u32[]{:S(2)}) collective-permute-start(f32[128,512]{1,0:T(8,128)S(1)} %get-tuple-element.51), channel_id=1, source_target_pairs={{1,0},{3,2},{5,4},{7,6},{9,8},{11,10},{13,12},{15,14},{17,16},{19,... | collective-permute-start | bytes 786440 | tf_op jit(solution)/shard_map/ppermute | solution.py:281
  82.0 1.4 %collective-permute-done.19.arrived = f32[128,512]{1,0:T(8,128)S(1)} collective-permute-done((f32[128,512]{1,0:T(8,128)S(1)}, f32[128,512]{1,0:T(8,128)S(1)}, u32[]{:S(2)}, u32[]{:S(2)}) %collective-permute-start.19) | collective-permute-done | bytes 262176 | tf_op jit(solution)/shard_map/ppermute | solution.py:281
  84.0 1.3 %collective-permute-start.23 = (f32[128,512]{1,0:T(8,128)S(1)}, f32[128,512]{1,0:T(8,128)S(1)}, u32[]{:S(2)}, u32[]{:S(2)}) collective-permute-start(f32[128,512]{1,0:T(8,128)S(1)} %get-tuple-element.54), channel_id=1, source_target_pairs={{1,0},{3,2},{5,4},{7,6},{9,8},{11,10},{13,12},{15,14},{17,16},{19,... | collective-permute-start | bytes 786440 | tf_op jit(solution)/shard_map/ppermute | solution.py:281
  86.4 3.2 %shard_map.99 = (f32[2,256,512]{2,1,0:T(8,128)}, bf16[2,512,1024]{2,1,0:T(8,128)(2,1)}, bf16[2,1024,512]{2,1,0:T(8,128)(2,1)}) custom-call(bf16[2,128,1024]{2,1,0:T(8,128)(2,1)S(1)} %get-tuple-element.53.token.refs_4_, bf16[3,1024,512]{2,1,0:T(8,128)(2,1)S(1)} %get-tuple-element.41.in3, bf16[3,512,1024]{2,1,0:T(8,128)(2,1)S(1)} %get-tuple-element.42.out3, ...), custom_call_target="tpu_custom_call" | custom-call | tf_op jit(solution)/shard_map/pallas_call | solution.py:266
  (44 shorter events, 14.2 us)
Async XLA Ops:
  0.6 3.0 %copy-start = (f32[1,256,512]{2,1,0:T(8,128)S(1)}, f32[1,256,512]{2,1,0:T(8,128)}, u32[]{:S(2)}) copy-start(f32[1,256,512]{2,1,0:T(8,128)} %param.8) | copy-start | bytes 1572868
  2.3 10.3 %collective-permute-start.1 = (f32[2304,512]{1,0:T(8,128)S(1)}, f32[2304,512]{1,0:T(8,128)S(1)}, u32[]{:S(2)}, u32[]{:S(2)}) collective-permute-start(f32[2304,512]{1,0:T(8,128)S(1)} %get-tuple-element.39), channel_id=1, source_target_pairs={{0,1},{2,3},{4,5},{6,7},{8,9},{10,11},{12,13},{14,15},{16,17},{18,... | collective-permute-start | bytes 14155784 | tf_op jit(solution)/shard_map/ppermute | solution.py:281
  3.6 7.5 %collective-permute-start = (f32[256,512]{1,0:T(8,128)S(1)}, f32[256,512]{1,0:T(8,128)S(1)}, u32[]{:S(2)}, u32[]{:S(2)}) collective-permute-start(f32[256,512]{1,0:T(8,128)S(1)} %bitcast.1), channel_id=1, source_target_pairs={{1,0},{3,2},{5,4},{7,6},{9,8},{11,10},{13,12},{15,14},{17,16},{19,... | collective-permute-start | bytes 1572872 | tf_op jit(solution)/shard_map/ppermute | solution.py:281
  7.0 10.5 %collective-permute-start.2 = (f32[256,512]{1,0:T(8,128)S(1)}, f32[256,512]{1,0:T(8,128)S(1)}, u32[]{:S(2)}, u32[]{:S(2)}) collective-permute-start(f32[256,512]{1,0:T(8,128)S(1)} %bitcast.2), channel_id=1, source_target_pairs={{2,1},{4,3},{6,5},{8,7},{10,9},{12,11},{14,13},{16,15},{18,17},{20... | collective-permute-start | bytes 1572872 | tf_op jit(solution)/shard_map/ppermute | solution.py:281
  11.2 6.3 %copy-start.1 = (f32[256,512]{1,0:T(8,128)S(1)}, f32[256,512]{1,0:T(8,128)}, u32[]{:S(2)}) copy-start(f32[256,512]{1,0:T(8,128)} %terminal.3) | copy-start | bytes 1572868
  11.2 6.3 %collective-permute-start.3 = (f32[256,512]{1,0:T(8,128)S(1)}, f32[256,512]{1,0:T(8,128)S(1)}, u32[]{:S(2)}, u32[]{:S(2)}) collective-permute-start(f32[256,512]{1,0:T(8,128)S(1)} %shard_map.78.token), channel_id=1, source_target_pairs={{0,1},{2,3},{4,5},{6,7},{8,9},{10,11},{12,13},{14,15},{16,17},{18,... | collective-permute-start | bytes 1572872 | tf_op jit(solution)/shard_map/ppermute | solution.py:281
  18.8 8.6 %collective-permute-start.4 = (f32[128,512]{1,0:T(8,128)S(1)}, f32[128,512]{1,0:T(8,128)S(1)}, u32[]{:S(2)}, u32[]{:S(2)}) collective-permute-start(f32[128,512]{1,0:T(8,128)S(1)} %get-tuple-element.43.token.refs_1_), channel_id=1, source_target_pairs={{3,1},{5,3},{7,5},{9,7},{11,9},{13,11},{15,13},{17,15},{19,17},{21... | collective-permute-start | bytes 786440 | tf_op jit(solution)/shard_map/ppermute | solution.py:281
  21.5 9.2 %collective-permute-start.5 = (f32[128,512]{1,0:T(8,128)S(1)}, f32[128,512]{1,0:T(8,128)S(1)}, u32[]{:S(2)}, u32[]{:S(2)}) collective-permute-start(f32[128,512]{1,0:T(8,128)S(1)} %get-tuple-element.44.token.refs_1_), channel_id=1, source_target_pairs={{3,1},{5,3},{7,5},{9,7},{11,9},{13,11},{15,13},{17,15},{19,17},{21... | collective-permute-start | bytes 786440 | tf_op jit(solution)/shard_map/ppermute | solution.py:281
  28.3 7.4 %collective-permute-start.6 = (f32[128,512]{1,0:T(8,128)S(1)}, f32[128,512]{1,0:T(8,128)S(1)}, u32[]{:S(2)}, u32[]{:S(2)}) collective-permute-start(f32[128,512]{1,0:T(8,128)S(1)} %shard_map.82.token.refs_0_), channel_id=1, source_target_pairs={{3,1},{7,5},{11,9},{15,13},{19,17},{23,21},{27,25},{31,29}} | collective-permute-start | bytes 786440 | tf_op jit(solution)/shard_map/ppermute | solution.py:281
  31.6 7.4 %collective-permute-start.7 = (f32[128,512]{1,0:T(8,128)S(1)}, f32[128,512]{1,0:T(8,128)S(1)}, u32[]{:S(2)}, u32[]{:S(2)}) collective-permute-start(f32[128,512]{1,0:T(8,128)S(1)} %shard_map.83.token.refs_0_), channel_id=1, source_target_pairs={{3,1},{7,5},{11,9},{15,13},{19,17},{23,21},{27,25},{31,29}} | collective-permute-start | bytes 786440 | tf_op jit(solution)/shard_map/ppermute | solution.py:281
  36.2 3.9 %collective-permute-start.8 = (f32[128,512]{1,0:T(8,128)S(1)}, f32[128,512]{1,0:T(8,128)S(1)}, u32[]{:S(2)}, u32[]{:S(2)}) collective-permute-start(f32[128,512]{1,0:T(8,128)S(1)} %shard_map.84.token.refs_1_), channel_id=1, source_target_pairs={{5,3},{9,7},{13,11},{17,15},{21,19},{25,23},{29,27}} | collective-permute-start | bytes 786440 | tf_op jit(solution)/shard_map/ppermute | solution.py:281
  39.5 2.0 %collective-permute-start.9 = (f32[128,512]{1,0:T(8,128)S(1)}, f32[128,512]{1,0:T(8,128)S(1)}, u32[]{:S(2)}, u32[]{:S(2)}) collective-permute-start(f32[128,512]{1,0:T(8,128)S(1)} %shard_map.85.token.refs_1_), channel_id=1, source_target_pairs={{5,3},{9,7},{13,11},{17,15},{21,19},{25,23},{29,27}} | collective-permute-start | bytes 786440 | tf_op jit(solution)/shard_map/ppermute | solution.py:281
  40.2 10.8 %collective-permute-start.10 = (f32[128,512]{1,0:T(8,128)S(1)}, f32[128,512]{1,0:T(8,128)S(1)}, u32[]{:S(2)}, u32[]{:S(2)}) collective-permute-start(f32[128,512]{1,0:T(8,128)S(1)} %shard_map.86.token), channel_id=1, source_target_pairs={{3,1},{7,5},{11,9},{15,13},{19,17},{23,21},{27,25},{31,29}} | collective-permute-start | bytes 786440 | tf_op jit(solution)/shard_map/ppermute | solution.py:281
  41.5 12.7 %collective-permute-start.11 = (f32[128,512]{1,0:T(8,128)S(1)}, f32[128,512]{1,0:T(8,128)S(1)}, u32[]{:S(2)}, u32[]{:S(2)}) collective-permute-start(f32[128,512]{1,0:T(8,128)S(1)} %shard_map.87.token), channel_id=1, source_target_pairs={{3,1},{7,5},{11,9},{15,13},{19,17},{23,21},{27,25},{31,29}} | collective-permute-start | bytes 786440 | tf_op jit(solution)/shard_map/ppermute | solution.py:281
  51.5 7.1 %collective-permute-start.12 = (f32[128,512]{1,0:T(8,128)S(1)}, f32[128,512]{1,0:T(8,128)S(1)}, u32[]{:S(2)}, u32[]{:S(2)}) collective-permute-start(f32[128,512]{1,0:T(8,128)S(1)} %shard_map.88.token.refs_0_), channel_id=1, source_target_pairs={{5,1},{13,9},{21,17},{29,25}} | collective-permute-start | bytes 786440 | tf_op jit(solution)/shard_map/ppermute | solution.py:281
  54.7 7.4 %collective-permute-start.13 = (f32[128,512]{1,0:T(8,128)S(1)}, f32[128,512]{1,0:T(8,128)S(1)}, u32[]{:S(2)}, u32[]{:S(2)}) collective-permute-start(f32[128,512]{1,0:T(8,128)S(1)} %shard_map.89.token.refs_0_), channel_id=1, source_target_pairs={{5,1},{13,9},{21,17},{29,25}} | collective-permute-start | bytes 786440 | tf_op jit(solution)/shard_map/ppermute | solution.py:281
  59.1 4.2 %collective-permute-start.14 = (f32[128,512]{1,0:T(8,128)S(1)}, f32[128,512]{1,0:T(8,128)S(1)}, u32[]{:S(2)}, u32[]{:S(2)}) collective-permute-start(f32[128,512]{1,0:T(8,128)S(1)} %shard_map.90.token.refs_0_), channel_id=1, source_target_pairs={{9,5},{17,13},{25,21}} | collective-permute-start | bytes 786440 | tf_op jit(solution)/shard_map/ppermute | solution.py:281
  62.6 1.4 %collective-permute-start.15 = (f32[128,512]{1,0:T(8,128)S(1)}, f32[128,512]{1,0:T(8,128)S(1)}, u32[]{:S(2)}, u32[]{:S(2)}) collective-permute-start(f32[128,512]{1,0:T(8,128)S(1)} %shard_map.91.token.refs_0_), channel_id=1, source_target_pairs={{9,5},{17,13},{25,21}} | collective-permute-start | bytes 786440 | tf_op jit(solution)/shard_map/ppermute | solution.py:281
  63.4 1.4 %collective-permute-start.16 = (f32[128,512]{1,0:T(8,128)S(1)}, f32[128,512]{1,0:T(8,128)S(1)}, u32[]{:S(2)}, u32[]{:S(2)}) collective-permute-start(f32[128,512]{1,0:T(8,128)S(1)} %shard_map.92.token.refs_0_), channel_id=1, source_target_pairs={{5,3},{9,7},{13,11},{17,15},{21,19},{25,23},{29,27}} | collective-permute-start | bytes 786440 | tf_op jit(solution)/shard_map/ppermute | solution.py:281
  64.1 2.1 %collective-permute-start.17 = (f32[128,512]{1,0:T(8,128)S(1)}, f32[128,512]{1,0:T(8,128)S(1)}, u32[]{:S(2)}, u32[]{:S(2)}) collective-permute-start(f32[128,512]{1,0:T(8,128)S(1)} %shard_map.93.token.refs_0_), channel_id=1, source_target_pairs={{5,3},{9,7},{13,11},{17,15},{21,19},{25,23},{29,27}} | collective-permute-start | bytes 786440 | tf_op jit(solution)/shard_map/ppermute | solution.py:281
  64.9 15.4 %collective-permute-start.18 = (f32[128,512]{1,0:T(8,128)S(1)}, f32[128,512]{1,0:T(8,128)S(1)}, u32[]{:S(2)}, u32[]{:S(2)}) collective-permute-start(f32[128,512]{1,0:T(8,128)S(1)} %shard_map.94.token), channel_id=1, source_target_pairs={{3,1},{5,3},{7,5},{9,7},{11,9},{13,11},{15,13},{17,15},{19,17},{21... | collective-permute-start | bytes 786440 | tf_op jit(solution)/shard_map/ppermute | solution.py:281
  66.2 17.3 %collective-permute-start.19 = (f32[128,512]{1,0:T(8,128)S(1)}, f32[128,512]{1,0:T(8,128)S(1)}, u32[]{:S(2)}, u32[]{:S(2)}) collective-permute-start(f32[128,512]{1,0:T(8,128)S(1)} %shard_map.95.token), channel_id=1, source_target_pairs={{3,1},{5,3},{7,5},{9,7},{11,9},{13,11},{15,13},{17,15},{19,17},{21... | collective-permute-start | bytes 786440 | tf_op jit(solution)/shard_map/ppermute | solution.py:281
  67.5 17.8 %collective-permute-start.20 = (f32[128,512]{1,0:T(8,128)S(1)}, f32[128,512]{1,0:T(8,128)S(1)}, u32[]{:S(2)}, u32[]{:S(2)}) collective-permute-start(f32[128,512]{1,0:T(8,128)S(1)} %shard_map.94.token), channel_id=1, source_target_pairs={{1,0},{3,2},{5,4},{7,6},{9,8},{11,10},{13,12},{15,14},{17,16},{19,... | collective-permute-start | bytes 786440 | tf_op jit(solution)/shard_map/ppermute | solution.py:281
  68.8 17.3 %collective-permute-start.22 = (f32[128,512]{1,0:T(8,128)S(1)}, f32[128,512]{1,0:T(8,128)S(1)}, u32[]{:S(2)}, u32[]{:S(2)}) collective-permute-start(f32[128,512]{1,0:T(8,128)S(1)} %shard_map.95.token), channel_id=1, source_target_pairs={{1,0},{3,2},{5,4},{7,6},{9,8},{11,10},{13,12},{15,14},{17,16},{19,... | collective-permute-start | bytes 786440 | tf_op jit(solution)/shard_map/ppermute | solution.py:281
  80.7 4.6 %collective-permute-start.21 = (f32[128,512]{1,0:T(8,128)S(1)}, f32[128,512]{1,0:T(8,128)S(1)}, u32[]{:S(2)}, u32[]{:S(2)}) collective-permute-start(f32[128,512]{1,0:T(8,128)S(1)} %get-tuple-element.51), channel_id=1, source_target_pairs={{1,0},{3,2},{5,4},{7,6},{9,8},{11,10},{13,12},{15,14},{17,16},{19,... | collective-permute-start | bytes 786440 | tf_op jit(solution)/shard_map/ppermute | solution.py:281
  84.0 2.4 %collective-permute-start.23 = (f32[128,512]{1,0:T(8,128)S(1)}, f32[128,512]{1,0:T(8,128)S(1)}, u32[]{:S(2)}, u32[]{:S(2)}) collective-permute-start(f32[128,512]{1,0:T(8,128)S(1)} %get-tuple-element.54), channel_id=1, source_target_pairs={{1,0},{3,2},{5,4},{7,6},{9,8},{11,10},{13,12},{15,14},{17,16},{19,... | collective-permute-start | bytes 786440 | tf_op jit(solution)/shard_map/ppermute | solution.py:281

commit v5 on v4

--- a/solution.py
+++ b/solution.py
@@ -8,7 +8,6 @@
 from jax.sharding import PartitionSpec as P
 
 
-LEVELS = 4
 CHUNKS = 2
 F32, BF16 = jnp.float32, jnp.bfloat16
 VMEM = pl.BlockSpec(memory_space=pltpu.VMEM)
@@ -143,37 +142,63 @@
         value[...] = apply_slot(own, 2.0, 0, rows, in3, out3, slope3) + resid_even[rows, :]
 
 
-def phi_kernel(low, size, steps, period, phase, token, vector, in3, out3, slope3, *refs):
-    result = refs[-1]
+def phi_kernel(low, size, steps, period, phases, counts, token, in3, out3, slope3, *refs):
+    vectors, addends, extras, results = [], [], [], []
+    groups, left = (vectors, addends, extras), list(refs)
+    for group, count in zip(groups, counts):
+        group += left[:count]
+        left = left[count:]
+    results = left
     place = lax.axis_index("depth")
-    active = lax.rem(place, 2 * period) == 2 * phase + 1
+    chip = lax.rem(place // 2, period)
+    active = functools.reduce(jnp.logical_or, [chip == phase for phase in phases])
+    active = jnp.logical_and(active, core() == 1)
     rows = pl.ds(low, size)
 
+    def added(total, parts):
+        for part in parts:
+            total = total + part[...]
+        return total
+
     def finish(total):
-        for addend in refs[:-1]:
-            total = total + addend[...]
-        result[...] = total
+        total = added(total, addends)
+        results[0][...] = total
+        if extras:
+            results[1][...] = added(total, extras)
 
     @pl.when(active)
     def _():
-        value = vector[...]
+        value = added(vectors[0][...], vectors[1:])
         for slot, factor in steps:
             value = apply_slot(value, factor, slot, rows, in3, out3, slope3)
         finish(value)
 
     @pl.when(jnp.logical_not(active))
     def _():
-        finish(jnp.zeros(result.shape, F32))
-
-
-def final_kernel(low, size, token, arrived, resid, guess, above0, in3, out3, slope3, last_odd, even, above):
+        finish(jnp.zeros(results[0].shape, F32))
+
+
+def final_kernel(low, size, token, resid, guess, above0, in3, out3, slope3, *refs):
+    arrived, summed, (last_odd, even, above) = refs[0], refs[1:-3], refs[-3:]
+    odd_chip = lax.rem(lax.axis_index("depth") // 2, 2) == 1
+
     @on_core(1)
     def _():
         rows = pl.ds(low, size)
-        last = apply_slot(arrived[...], 2.0, 1, rows, in3, out3, slope3) + resid[...]
+
+        @pl.when(odd_chip)
+        def _():
+            above[...] = summed[0][...] + summed[1][...] + summed[2][...]
+
+        @pl.when(jnp.logical_not(odd_chip))
+        def _():
+            above[...] = arrived[...]
+
+        upper = above[...]
+        last = apply_slot(upper, 2.0, 1, rows, in3, out3, slope3) + resid[...]
         last_odd[...] = last
         even[...] = guess[rows, :] + last
-        above[...] = above0[...] + arrived[...]
+        above[...] = above0[...] + upper
 
 
 def settle(low, size, sent_even, sent_odd, above0, guess, even, above):
@@ -320,52 +345,57 @@
     resid_even = permute(resid_even, to_core_1)
     weights = run(adopt_kernel, layers, (packed, *weights), input_output_aliases={2: 0, 3: 1, 4: 2})
 
-    def next_chip(value):
-        return shift(value, 1, 0, 1)
-
-    above0, resid, values, sent = [], [], [], []
-    for low, size in zip(lows, sizes):
-        outs = run(
-            functools.partial(value_kernel, low, size),
-            (vmem(size, d),) * 3,
+    def phi(i, vectors, steps, period, phases, addends=(), extras=()):
+        counts = (len(vectors), len(addends), len(extras))
+        return run(
+            functools.partial(phi_kernel, lows[i], sizes[i], steps, period, phases, counts),
+            (vmem(sizes[i], d),) * (2 if extras else 1),
+            (*weights, *vectors, *addends, *extras),
+        )
+
+    parts = range(CHUNKS)
+    fill = [None] * CHUNKS
+    above0, resid, values, upper, rhs, hop, point = (list(fill) for _ in range(7))
+    both, second, third = ((1, 2.0), (0, 2.0)), ((0, 4.0),), ((0, 8.0),)
+    for i in parts:
+        above0[i], resid[i], values[i] = run(
+            functools.partial(value_kernel, lows[i], sizes[i]),
+            (vmem(sizes[i], d),) * 3,
             (moved_in, moved_x, terminal, guess, resid_even, *weights),
         )
-        for group, value in zip((above0, resid, values), outs):
-            group.append(value)
-        sent.append(next_chip(outs[2]))
-
-    def phi(received, steps, period, phase, send, *addends):
-        results, sent = [], []
-        for i in range(CHUNKS):
-            (result,) = run(
-                functools.partial(phi_kernel, lows[i], sizes[i], steps, period, phase),
-                (vmem(sizes[i], d),),
-                (received[i], *weights, *[addend[i] for addend in addends]),
-            )
-            results.append(result)
-            sent.append(send(result))
-        return results, sent
-
-    def cycle(level, rhs, sent, addend, send):
-        distance = 2 ** (level - 2)
-        period, steps = 2 * distance, ((0, float(2**level)),)
-
-        def down(value):
-            return shift(value, period, distance, distance)
-
-        def up(value):
-            return shift(value, period, 0, distance)
-
-        point, sent = phi(sent, steps, period, 0, up, rhs)
-        if level < LEVELS - 1:
-            _, sent = phi(sent, steps, period, distance, down)
-            deeper = 2 * distance
-            resid, sent = phi(sent, steps, period, 0, lambda value: shift(value, 2 * deeper, deeper, deeper))
-            point, sent = cycle(level + 1, resid, sent, point, up)
-        return phi(sent, steps, period, distance, send, point, addend)
-
-    coarse, sent = phi(sent, ((1, 2.0), (0, 2.0)), 1, 0, lambda value: shift(value, 2, 1, 1))
-    values, sent = cycle(2, coarse, sent, values, next_chip)
+        upper[i] = shift(values[i], 1, 0, 1)
+    for i in parts:
+        (rhs[i],) = phi(i, [upper[i]], both, 1, (0,))
+        hop[i] = shift(rhs[i], 2, 1, 1)
+    up_3, up_1, tangent_2, tangent_0, resid_2, resid_0, hop_8 = (list(fill) for _ in range(7))
+    for i in parts:
+        (point[i],) = phi(i, [hop[i]], second, 2, (0,), (rhs[i],))
+        up_3[i] = shift(point[i], 4, 0, 1)
+    for i in parts:
+        (value,) = phi(i, [up_3[i]], second, 4, (3,))
+        tangent_2[i] = shift(value, 4, 3, 1)
+    for i in parts:
+        up_1[i] = shift(point[i], 4, 2, 1)
+    for i in parts:
+        (value,) = phi(i, [up_1[i]], second, 4, (1,))
+        tangent_0[i] = shift(value, 4, 1, 1)
+        (resid_2[i],) = phi(i, [tangent_2[i]], second, 4, (2,))
+        hop_8[i] = shift(resid_2[i], 4, 2, 2)
+    hop_9, deep, low_3, low_1 = (list(fill) for _ in range(4))
+    for i in parts:
+        (resid_0[i],) = phi(i, [tangent_0[i]], second, 4, (0,))
+        value, deep[i] = phi(i, [hop_8[i]], third, 4, (0,), (resid_0[i],), (point[i],))
+        hop_9[i] = shift(value, 4, 0, 2)
+    for i in parts:
+        low_3[i] = shift(deep[i], 4, 0, 1)
+    for i in parts:
+        (deep[i],) = phi(i, [hop_9[i]], third, 4, (2,), (resid_2[i], deep[i]))
+        low_1[i] = shift(deep[i], 4, 2, 1)
+    sent = list(fill)
+    for i in parts:
+        (values[i],) = phi(i, [low_3[i], low_1[i]], second, 2, (1,), (deep[i], values[i]))
+        sent[i] = shift(values[i], 2, 1, 1)
+    arrived = [(sent[i], upper[i], low_3[i], low_1[i]) for i in parts]
 
     sent_even = [permute(value, to_core_0) for value in values]
     lasts = []
@@ -373,7 +403,7 @@
         odd, even, above = run(
             functools.partial(final_kernel, low, size),
             (vmem(size, d), vmem(size, d), vmem(size, d)),
-            (sent[i], resid[i], guess, above0[i], *weights),
+            (resid[i], guess, above0[i], *weights, *arrived[i]),
         )
         lasts.append((guess, sent_even[i], permute(odd, to_core_0), above0[i], even, above))
     parts = []

time: 90.7 us -> 89.7 us (0.989)
  waiting for transfers between devices: 41.2 us -> 35.5 us
  starting transfers between devices: 29.6 us -> 33.6 us
    ppermute x24 -> x30, waiting for transfers between devices: 41.2 us -> 35.5 us  [permute(): return held(lax.ppermute(value, 'depth', route))]
    ppermute x24 -> x30, starting transfers between devices: 29.6 us -> 33.6 us  [permute(): return held(lax.ppermute(value, 'depth', route))]
    pallas_call x24 -> x28, Pallas kernels: 17.7 us -> 18.1 us  [run(): pl.pallas_call(kernel, out_shape=tuple(shapes), in_specs=specs, out_specs...]
  transfers between devices with their start and end apart: 24 -> 30, of which waited for: 12 -> 11; matrix products, arithmetic and copies ran while one was open for 0% -> 0% of each run, Pallas kernels for 13% -> 14%
where the time goes in v5:
time: 89.7 us; the launch traced here: 88.7 us
  waiting for transfers between devices  35.5 us (40%)
  starting transfers between devices  33.6 us (37%)
  Pallas kernels  18.1 us (20%)
  between operations  1.41 us (2%)
    ppermute x30, waiting for transfers between devices, permute(): return held(lax.ppermute(value, 'depth', route))  35.5 us
    ppermute x30, starting transfers between devices, permute(): return held(lax.ppermute(value, 'depth', route))  33.6 us
    pallas_call x28, Pallas kernels, run(): pl.pallas_call(kernel, out_shape=tuple(shapes), in_specs=specs, out_specs...  18.1 us
  transfers between devices with their start and end apart: 30, of which 11 were waited for; matrix products, arithmetic and copies ran while one was open for 0% of the time, Pallas kernels for 14%

profile of v5, /device:TPU:1, one launch (start us, length us, event | category | flops | bytes accessed | tf_op | source)
XLA Modules:
  0.0 88.7 jit_solution(2245799657108415251)
XLA Ops:
  0.6 1.7 %shard_map.76 = (f32[2304,512]{1,0:T(8,128)S(1)}, bf16[256,512]{1,0:T(8,128)(2,1)S(1)}, bf16[512,1024]{1,0:T(8,128)(2,1)S(1)}, bf16[1024,512]{1,0:T(8,128)(2,1)S(1)}) custom-call(bf16[1,256,512]{2,1,0:T(8,128)(2,1)} %start_h.1, bf16[2,512,1024]{2,1,0:T(8,128)(2,1)} %w_in_h.3, bf16[2,1024,512]{2,1,0:T(8,128)(2,1)} %w_out_h.3), custom_call_target="tpu_custom_call" | custom-call | tf_op jit(solution)/shard_map/pallas_call | solution.py:291
  2.3 1.3 %collective-permute-start.1 = (f32[2304,512]{1,0:T(8,128)S(1)}, f32[2304,512]{1,0:T(8,128)S(1)}, u32[]{:S(2)}, u32[]{:S(2)}) collective-permute-start(f32[2304,512]{1,0:T(8,128)S(1)} %get-tuple-element.43), channel_id=1, source_target_pairs={{0,1},{2,3},{4,5},{6,7},{8,9},{10,11},{12,13},{14,15},{16,17},{18,... | collective-permute-start | bytes 14155784 | tf_op jit(solution)/shard_map/ppermute | solution.py:306
  3.6 3.4 %collective-permute-start = (f32[256,512]{1,0:T(8,128)S(1)}, f32[256,512]{1,0:T(8,128)S(1)}, u32[]{:S(2)}, u32[]{:S(2)}) collective-permute-start(f32[256,512]{1,0:T(8,128)S(1)} %bitcast.1), channel_id=1, source_target_pairs={{1,0},{3,2},{5,4},{7,6},{9,8},{11,10},{13,12},{15,14},{17,16},{19,... | collective-permute-start | bytes 1572872 | tf_op jit(solution)/shard_map/ppermute | solution.py:306
  7.0 1.3 %collective-permute-start.2 = (f32[256,512]{1,0:T(8,128)S(1)}, f32[256,512]{1,0:T(8,128)S(1)}, u32[]{:S(2)}, u32[]{:S(2)}) collective-permute-start(f32[256,512]{1,0:T(8,128)S(1)} %bitcast.2), channel_id=1, source_target_pairs={{2,1},{4,3},{6,5},{8,7},{10,9},{12,11},{14,13},{16,15},{18,17},{20... | collective-permute-start | bytes 1572872 | tf_op jit(solution)/shard_map/ppermute | solution.py:306
  8.3 2.8 %shard_map.77 = (bf16[3,1024,512]{2,1,0:T(8,128)(2,1)S(1)}, bf16[3,512,1024]{2,1,0:T(8,128)(2,1)S(1)}, f32[3,256,1024]{2,1,0:T(8,128)S(1)}, bf16[2,512,256]{2,1,0:T(8,128)(2,1)S(1)}, bf16[2,1024,256]{2,1,0:T(8,128)(2,1)S(1)}) custom-call(bf16[1024,512]{1,0:T(8,128)(2,1)S(1)} %get-tuple-element.36.token.w_out0, bf16[2,512,1024]{2,1,0:T(8,128)(2,1)} %w_in_h.3, ...), custom_call_target="tpu_custom_call" | custom-call | tf_op jit(solution)/shard_map/pallas_call | solution.py:291
  11.2 1.4 %collective-permute-start.3 = (f32[256,512]{1,0:T(8,128)S(1)}, f32[256,512]{1,0:T(8,128)S(1)}, u32[]{:S(2)}, u32[]{:S(2)}) collective-permute-start(f32[256,512]{1,0:T(8,128)S(1)} %shard_map.78.token), channel_id=1, source_target_pairs={{0,1},{2,3},{4,5},{6,7},{8,9},{10,11},{12,13},{14,15},{16,17},{18,... | collective-permute-start | bytes 1572872 | tf_op jit(solution)/shard_map/ppermute | solution.py:306
  13.3 4.2 %collective-permute-done.2.moved_x = f32[256,512]{1,0:T(8,128)S(1)} collective-permute-done((f32[256,512]{1,0:T(8,128)S(1)}, f32[256,512]{1,0:T(8,128)S(1)}, u32[]{:S(2)}, u32[]{:S(2)}) %collective-permute-start.2) | collective-permute-done | bytes 524320 | tf_op jit(solution)/shard_map/ppermute | solution.py:306
  17.5 1.3 %shard_map.80 = (f32[128,512]{1,0:T(8,128)S(1)}, f32[128,512]{1,0:T(8,128)S(1)}, f32[128,512]{1,0:T(8,128)S(1)}) custom-call(f32[3,256,1024]{2,1,0:T(8,128)S(1)} %get-tuple-element.44.token.slope3, f32[256,512]{1,0:T(8,128)S(1)} %collective-permute-done.moved.moved_in, f32[256,512]{1,0:T(8,128)S(1)} %collective-permute-done.2.moved_x, ...), custom_call_target="tpu_custom_call" | custom-call | tf_op jit(solution)/shard_map/pallas_call | solution.py:291
  18.8 1.3 %collective-permute-start.4 = (f32[128,512]{1,0:T(8,128)S(1)}, f32[128,512]{1,0:T(8,128)S(1)}, u32[]{:S(2)}, u32[]{:S(2)}) collective-permute-start(f32[128,512]{1,0:T(8,128)S(1)} %get-tuple-element.47.token.refs_3_), channel_id=1, source_target_pairs={{3,1},{5,3},{7,5},{9,7},{11,9},{13,11},{15,13},{17,15},{19,17},{21... | collective-permute-start | bytes 786440 | tf_op jit(solution)/shard_map/ppermute | solution.py:306
  20.1 1.3 %shard_map.81 = (f32[128,512]{1,0:T(8,128)S(1)}, f32[128,512]{1,0:T(8,128)S(1)}, f32[128,512]{1,0:T(8,128)S(1)}) custom-call(f32[128,512]{1,0:T(8,128)S(1)} %get-tuple-element.47.token.refs_3_, f32[256,512]{1,0:T(8,128)S(1)} %collective-permute-done.moved.moved_in, f32[256,512]{1,0:T(8,128)S(1)} %collective-permute-done.2.moved_x, f32[256,512]{1,0:T(8,128)S(1)} %copy-done.1, ...), custom_call_target="tpu_custom_call" | custom-call | tf_op jit(solution)/shard_map/pallas_call | solution.py:291
  21.5 1.3 %collective-permute-start.5 = (f32[128,512]{1,0:T(8,128)S(1)}, f32[128,512]{1,0:T(8,128)S(1)}, u32[]{:S(2)}, u32[]{:S(2)}) collective-permute-start(f32[128,512]{1,0:T(8,128)S(1)} %get-tuple-element.48.token.refs_3_), channel_id=1, source_target_pairs={{3,1},{5,3},{7,5},{9,7},{11,9},{13,11},{15,13},{17,15},{19,17},{21... | collective-permute-start | bytes 786440 | tf_op jit(solution)/shard_map/ppermute | solution.py:306
  22.8 4.6 %collective-permute-done.4.refs_0_.refs_1_ = f32[128,512]{1,0:T(8,128)S(1)} collective-permute-done((f32[128,512]{1,0:T(8,128)S(1)}, f32[128,512]{1,0:T(8,128)S(1)}, u32[]{:S(2)}, u32[]{:S(2)}) %collective-permute-start.4) | collective-permute-done | bytes 262176 | tf_op jit(solution)/shard_map/ppermute | solution.py:306
  28.3 1.3 %collective-permute-start.6 = (f32[128,512]{1,0:T(8,128)S(1)}, f32[128,512]{1,0:T(8,128)S(1)}, u32[]{:S(2)}, u32[]{:S(2)}) collective-permute-start(f32[128,512]{1,0:T(8,128)S(1)} %shard_map.82.token.refs_1_), channel_id=1, source_target_pairs={{3,1},{7,5},{11,9},{15,13},{19,17},{23,21},{27,25},{31,29}} | collective-permute-start | bytes 786440 | tf_op jit(solution)/shard_map/ppermute | solution.py:306
  31.6 1.3 %collective-permute-start.7 = (f32[128,512]{1,0:T(8,128)S(1)}, f32[128,512]{1,0:T(8,128)S(1)}, u32[]{:S(2)}, u32[]{:S(2)}) collective-permute-start(f32[128,512]{1,0:T(8,128)S(1)} %shard_map.83.token.refs_1_), channel_id=1, source_target_pairs={{3,1},{7,5},{11,9},{15,13},{19,17},{23,21},{27,25},{31,29}} | collective-permute-start | bytes 786440 | tf_op jit(solution)/shard_map/ppermute | solution.py:306
  32.9 2.8 %collective-permute-done.6.refs_0_ = f32[128,512]{1,0:T(8,128)S(1)} collective-permute-done((f32[128,512]{1,0:T(8,128)S(1)}, f32[128,512]{1,0:T(8,128)S(1)}, u32[]{:S(2)}, u32[]{:S(2)}) %collective-permute-start.6) | collective-permute-done | bytes 262176 | tf_op jit(solution)/shard_map/ppermute | solution.py:306
  36.9 2.1 %collective-permute-done.7.refs_0_ = f32[128,512]{1,0:T(8,128)S(1)} collective-permute-done((f32[128,512]{1,0:T(8,128)S(1)}, f32[128,512]{1,0:T(8,128)S(1)}, u32[]{:S(2)}, u32[]{:S(2)}) %collective-permute-start.7) | collective-permute-done | bytes 262176 | tf_op jit(solution)/shard_map/ppermute | solution.py:306
  43.1 1.3 %collective-permute-start.14 = (f32[128,512]{1,0:T(8,128)S(1)}, f32[128,512]{1,0:T(8,128)S(1)}, u32[]{:S(2)}, u32[]{:S(2)}) collective-permute-start(f32[128,512]{1,0:T(8,128)S(1)} %shard_map.88.token), channel_id=1, source_target_pairs={{3,1},{11,9},{19,17},{27,25}} | collective-permute-start | bytes 786440 | tf_op jit(solution)/shard_map/ppermute | solution.py:306
  44.4 1.3 %collective-permute-start.15 = (f32[128,512]{1,0:T(8,128)S(1)}, f32[128,512]{1,0:T(8,128)S(1)}, u32[]{:S(2)}, u32[]{:S(2)}) collective-permute-start(f32[128,512]{1,0:T(8,128)S(1)} %shard_map.89.token.refs_1_), channel_id=1, source_target_pairs={{5,1},{13,9},{21,17},{29,25}} | collective-permute-start | bytes 786440 | tf_op jit(solution)/shard_map/ppermute | solution.py:306
  46.0 1.3 %collective-permute-start.16 = (f32[128,512]{1,0:T(8,128)S(1)}, f32[128,512]{1,0:T(8,128)S(1)}, u32[]{:S(2)}, u32[]{:S(2)}) collective-permute-start(f32[128,512]{1,0:T(8,128)S(1)} %shard_map.90.token), channel_id=1, source_target_pairs={{3,1},{11,9},{19,17},{27,25}} | collective-permute-start | bytes 786440 | tf_op jit(solution)/shard_map/ppermute | solution.py:306
  47.3 1.3 %collective-permute-start.17 = (f32[128,512]{1,0:T(8,128)S(1)}, f32[128,512]{1,0:T(8,128)S(1)}, u32[]{:S(2)}, u32[]{:S(2)}) collective-permute-start(f32[128,512]{1,0:T(8,128)S(1)} %shard_map.91.token.refs_1_), channel_id=1, source_target_pairs={{5,1},{13,9},{21,17},{29,25}} | collective-permute-start | bytes 786440 | tf_op jit(solution)/shard_map/ppermute | solution.py:306
  48.6 6.3 %collective-permute-done.14.refs_0_ = f32[128,512]{1,0:T(8,128)S(1)} collective-permute-done((f32[128,512]{1,0:T(8,128)S(1)}, f32[128,512]{1,0:T(8,128)S(1)}, u32[]{:S(2)}, u32[]{:S(2)}) %collective-permute-start.14) | collective-permute-done | bytes 262176 | tf_op jit(solution)/shard_map/ppermute | solution.py:306
  55.4 2.9 %collective-permute-done.15.refs_0_ = f32[128,512]{1,0:T(8,128)S(1)} collective-permute-done((f32[128,512]{1,0:T(8,128)S(1)}, f32[128,512]{1,0:T(8,128)S(1)}, u32[]{:S(2)}, u32[]{:S(2)}) %collective-permute-start.15) | collective-permute-done | bytes 262176 | tf_op jit(solution)/shard_map/ppermute | solution.py:306
  60.0 2.1 %collective-permute-done.17.refs_0_ = f32[128,512]{1,0:T(8,128)S(1)} collective-permute-done((f32[128,512]{1,0:T(8,128)S(1)}, f32[128,512]{1,0:T(8,128)S(1)}, u32[]{:S(2)}, u32[]{:S(2)}) %collective-permute-start.17) | collective-permute-done | bytes 262176 | tf_op jit(solution)/shard_map/ppermute | solution.py:306
  66.3 1.3 %collective-permute-start.24 = (f32[128,512]{1,0:T(8,128)S(1)}, f32[128,512]{1,0:T(8,128)S(1)}, u32[]{:S(2)}, u32[]{:S(2)}) collective-permute-start(f32[128,512]{1,0:T(8,128)S(1)} %shard_map.98.token), channel_id=1, source_target_pairs={{3,1},{7,5},{11,9},{15,13},{19,17},{23,21},{27,25},{31,29}} | collective-permute-start | bytes 786440 | tf_op jit(solution)/shard_map/ppermute | solution.py:306
  67.6 1.3 %collective-permute-start.25 = (f32[128,512]{1,0:T(8,128)S(1)}, f32[128,512]{1,0:T(8,128)S(1)}, u32[]{:S(2)}, u32[]{:S(2)}) collective-permute-start(f32[128,512]{1,0:T(8,128)S(1)} %shard_map.99.token), channel_id=1, source_target_pairs={{3,1},{7,5},{11,9},{15,13},{19,17},{23,21},{27,25},{31,29}} | collective-permute-start | bytes 786440 | tf_op jit(solution)/shard_map/ppermute | solution.py:306
  68.9 1.3 %collective-permute-start.26 = (f32[128,512]{1,0:T(8,128)S(1)}, f32[128,512]{1,0:T(8,128)S(1)}, u32[]{:S(2)}, u32[]{:S(2)}) collective-permute-start(f32[128,512]{1,0:T(8,128)S(1)} %shard_map.98.token), channel_id=1, source_target_pairs={{1,0},{3,2},{5,4},{7,6},{9,8},{11,10},{13,12},{15,14},{17,16},{19,... | collective-permute-start | bytes 786440 | tf_op jit(solution)/shard_map/ppermute | solution.py:306
  70.2 1.3 %collective-permute-start.28 = (f32[128,512]{1,0:T(8,128)S(1)}, f32[128,512]{1,0:T(8,128)S(1)}, u32[]{:S(2)}, u32[]{:S(2)}) collective-permute-start(f32[128,512]{1,0:T(8,128)S(1)} %shard_map.99.token), channel_id=1, source_target_pairs={{1,0},{3,2},{5,4},{7,6},{9,8},{11,10},{13,12},{15,14},{17,16},{19,... | collective-permute-start | bytes 786440 | tf_op jit(solution)/shard_map/ppermute | solution.py:306
  71.6 7.2 %collective-permute-done.24.refs_0_ = f32[128,512]{1,0:T(8,128)S(1)} collective-permute-done((f32[128,512]{1,0:T(8,128)S(1)}, f32[128,512]{1,0:T(8,128)S(1)}, u32[]{:S(2)}, u32[]{:S(2)}) %collective-permute-start.24) | collective-permute-done | bytes 262176 | tf_op jit(solution)/shard_map/ppermute | solution.py:306
  79.3 1.3 %collective-permute-start.27 = (f32[128,512]{1,0:T(8,128)S(1)}, f32[128,512]{1,0:T(8,128)S(1)}, u32[]{:S(2)}, u32[]{:S(2)}) collective-permute-start(f32[128,512]{1,0:T(8,128)S(1)} %get-tuple-element.59), channel_id=1, source_target_pairs={{1,0},{3,2},{5,4},{7,6},{9,8},{11,10},{13,12},{15,14},{17,16},{19,... | collective-permute-start | bytes 786440 | tf_op jit(solution)/shard_map/ppermute | solution.py:306
  80.6 1.8 %collective-permute-done.25.refs_0_ = f32[128,512]{1,0:T(8,128)S(1)} collective-permute-done((f32[128,512]{1,0:T(8,128)S(1)}, f32[128,512]{1,0:T(8,128)S(1)}, u32[]{:S(2)}, u32[]{:S(2)}) %collective-permute-start.25) | collective-permute-done | bytes 262176 | tf_op jit(solution)/shard_map/ppermute | solution.py:306
  82.9 1.3 %collective-permute-start.29 = (f32[128,512]{1,0:T(8,128)S(1)}, f32[128,512]{1,0:T(8,128)S(1)}, u32[]{:S(2)}, u32[]{:S(2)}) collective-permute-start(f32[128,512]{1,0:T(8,128)S(1)} %get-tuple-element.62), channel_id=1, source_target_pairs={{1,0},{3,2},{5,4},{7,6},{9,8},{11,10},{13,12},{15,14},{17,16},{19,... | collective-permute-start | bytes 786440 | tf_op jit(solution)/shard_map/ppermute | solution.py:306
  85.3 3.2 %shard_map.103 = (f32[2,256,512]{2,1,0:T(8,128)}, bf16[2,512,1024]{2,1,0:T(8,128)(2,1)}, bf16[2,1024,512]{2,1,0:T(8,128)(2,1)}) custom-call(bf16[2,128,1024]{2,1,0:T(8,128)(2,1)S(1)} %get-tuple-element.61.token.refs_4_, bf16[3,1024,512]{2,1,0:T(8,128)(2,1)S(1)} %get-tuple-element.45.in3, bf16[3,512,1024]{2,1,0:T(8,128)(2,1)S(1)} %get-tuple-element.46.out3, ...), custom_call_target="tpu_custom_call" | custom-call | tf_op jit(solution)/shard_map/pallas_call | solution.py:291
  (60 shorter events, 17.4 us)
Async XLA Ops:
  0.6 3.0 %copy-start = (f32[1,256,512]{2,1,0:T(8,128)S(1)}, f32[1,256,512]{2,1,0:T(8,128)}, u32[]{:S(2)}) copy-start(f32[1,256,512]{2,1,0:T(8,128)} %param.8) | copy-start | bytes 1572868
  2.3 10.3 %collective-permute-start.1 = (f32[2304,512]{1,0:T(8,128)S(1)}, f32[2304,512]{1,0:T(8,128)S(1)}, u32[]{:S(2)}, u32[]{:S(2)}) collective-permute-start(f32[2304,512]{1,0:T(8,128)S(1)} %get-tuple-element.43), channel_id=1, source_target_pairs={{0,1},{2,3},{4,5},{6,7},{8,9},{10,11},{12,13},{14,15},{16,17},{18,... | collective-permute-start | bytes 14155784 | tf_op jit(solution)/shard_map/ppermute | solution.py:306
  3.6 7.5 %collective-permute-start = (f32[256,512]{1,0:T(8,128)S(1)}, f32[256,512]{1,0:T(8,128)S(1)}, u32[]{:S(2)}, u32[]{:S(2)}) collective-permute-start(f32[256,512]{1,0:T(8,128)S(1)} %bitcast.1), channel_id=1, source_target_pairs={{1,0},{3,2},{5,4},{7,6},{9,8},{11,10},{13,12},{15,14},{17,16},{19,... | collective-permute-start | bytes 1572872 | tf_op jit(solution)/shard_map/ppermute | solution.py:306
  7.0 10.5 %collective-permute-start.2 = (f32[256,512]{1,0:T(8,128)S(1)}, f32[256,512]{1,0:T(8,128)S(1)}, u32[]{:S(2)}, u32[]{:S(2)}) collective-permute-start(f32[256,512]{1,0:T(8,128)S(1)} %bitcast.2), channel_id=1, source_target_pairs={{2,1},{4,3},{6,5},{8,7},{10,9},{12,11},{14,13},{16,15},{18,17},{20... | collective-permute-start | bytes 1572872 | tf_op jit(solution)/shard_map/ppermute | solution.py:306
  11.2 6.3 %copy-start.1 = (f32[256,512]{1,0:T(8,128)S(1)}, f32[256,512]{1,0:T(8,128)}, u32[]{:S(2)}) copy-start(f32[256,512]{1,0:T(8,128)} %terminal.3) | copy-start | bytes 1572868
  11.2 6.3 %collective-permute-start.3 = (f32[256,512]{1,0:T(8,128)S(1)}, f32[256,512]{1,0:T(8,128)S(1)}, u32[]{:S(2)}, u32[]{:S(2)}) collective-permute-start(f32[256,512]{1,0:T(8,128)S(1)} %shard_map.78.token), channel_id=1, source_target_pairs={{0,1},{2,3},{4,5},{6,7},{8,9},{10,11},{12,13},{14,15},{16,17},{18,... | collective-permute-start | bytes 1572872 | tf_op jit(solution)/shard_map/ppermute | solution.py:306
  18.8 8.6 %collective-permute-start.4 = (f32[128,512]{1,0:T(8,128)S(1)}, f32[128,512]{1,0:T(8,128)S(1)}, u32[]{:S(2)}, u32[]{:S(2)}) collective-permute-start(f32[128,512]{1,0:T(8,128)S(1)} %get-tuple-element.47.token.refs_3_), channel_id=1, source_target_pairs={{3,1},{5,3},{7,5},{9,7},{11,9},{13,11},{15,13},{17,15},{19,17},{21... | collective-permute-start | bytes 786440 | tf_op jit(solution)/shard_map/ppermute | solution.py:306
  21.5 9.2 %collective-permute-start.5 = (f32[128,512]{1,0:T(8,128)S(1)}, f32[128,512]{1,0:T(8,128)S(1)}, u32[]{:S(2)}, u32[]{:S(2)}) collective-permute-start(f32[128,512]{1,0:T(8,128)S(1)} %get-tuple-element.48.token.refs_3_), channel_id=1, source_target_pairs={{3,1},{5,3},{7,5},{9,7},{11,9},{13,11},{15,13},{17,15},{19,17},{21... | collective-permute-start | bytes 786440 | tf_op jit(solution)/shard_map/ppermute | solution.py:306
  28.3 7.4 %collective-permute-start.6 = (f32[128,512]{1,0:T(8,128)S(1)}, f32[128,512]{1,0:T(8,128)S(1)}, u32[]{:S(2)}, u32[]{:S(2)}) collective-permute-start(f32[128,512]{1,0:T(8,128)S(1)} %shard_map.82.token.refs_1_), channel_id=1, source_target_pairs={{3,1},{7,5},{11,9},{15,13},{19,17},{23,21},{27,25},{31,29}} | collective-permute-start | bytes 786440 | tf_op jit(solution)/shard_map/ppermute | solution.py:306
  31.6 7.4 %collective-permute-start.7 = (f32[128,512]{1,0:T(8,128)S(1)}, f32[128,512]{1,0:T(8,128)S(1)}, u32[]{:S(2)}, u32[]{:S(2)}) collective-permute-start(f32[128,512]{1,0:T(8,128)S(1)} %shard_map.83.token.refs_1_), channel_id=1, source_target_pairs={{3,1},{7,5},{11,9},{15,13},{19,17},{23,21},{27,25},{31,29}} | collective-permute-start | bytes 786440 | tf_op jit(solution)/shard_map/ppermute | solution.py:306
  36.2 4.6 %collective-permute-start.8 = (f32[128,512]{1,0:T(8,128)S(1)}, f32[128,512]{1,0:T(8,128)S(1)}, u32[]{:S(2)}, u32[]{:S(2)}) collective-permute-start(f32[128,512]{1,0:T(8,128)S(1)} %shard_map.84.token.refs_2_), channel_id=1, source_target_pairs={{9,7},{17,15},{25,23}} | collective-permute-start | bytes 786440 | tf_op jit(solution)/shard_map/ppermute | solution.py:306
  39.5 2.8 %collective-permute-start.9 = (f32[128,512]{1,0:T(8,128)S(1)}, f32[128,512]{1,0:T(8,128)S(1)}, u32[]{:S(2)}, u32[]{:S(2)}) collective-permute-start(f32[128,512]{1,0:T(8,128)S(1)} %shard_map.85.token.refs_2_), channel_id=1, source_target_pairs={{9,7},{17,15},{25,23}} | collective-permute-start | bytes 786440 | tf_op jit(solution)/shard_map/ppermute | solution.py:306
  40.1 2.9 %collective-permute-start.10 = (f32[128,512]{1,0:T(8,128)S(1)}, f32[128,512]{1,0:T(8,128)S(1)}, u32[]{:S(2)}, u32[]{:S(2)}) collective-permute-start(f32[128,512]{1,0:T(8,128)S(1)} %shard_map.84.token.refs_2_), channel_id=1, source_target_pairs={{5,3},{13,11},{21,19},{29,27}} | collective-permute-start | bytes 786440 | tf_op jit(solution)/shard_map/ppermute | solution.py:306
  40.9 3.5 %collective-permute-start.11 = (f32[128,512]{1,0:T(8,128)S(1)}, f32[128,512]{1,0:T(8,128)S(1)}, u32[]{:S(2)}, u32[]{:S(2)}) collective-permute-start(f32[128,512]{1,0:T(8,128)S(1)} %shard_map.86.token), channel_id=1, source_target_pairs={{7,5},{15,13},{23,21},{31,29}} | collective-permute-start | bytes 786440 | tf_op jit(solution)/shard_map/ppermute | solution.py:306
  41.6 4.2 %collective-permute-start.12 = (f32[128,512]{1,0:T(8,128)S(1)}, f32[128,512]{1,0:T(8,128)S(1)}, u32[]{:S(2)}, u32[]{:S(2)}) collective-permute-start(f32[128,512]{1,0:T(8,128)S(1)} %shard_map.85.token.refs_2_), channel_id=1, source_target_pairs={{5,3},{13,11},{21,19},{29,27}} | collective-permute-start | bytes 786440 | tf_op jit(solution)/shard_map/ppermute | solution.py:306
  42.3 4.9 %collective-permute-start.13 = (f32[128,512]{1,0:T(8,128)S(1)}, f32[128,512]{1,0:T(8,128)S(1)}, u32[]{:S(2)}, u32[]{:S(2)}) collective-permute-start(f32[128,512]{1,0:T(8,128)S(1)} %shard_map.87.token), channel_id=1, source_target_pairs={{7,5},{15,13},{23,21},{31,29}} | collective-permute-start | bytes 786440 | tf_op jit(solution)/shard_map/ppermute | solution.py:306
  43.1 11.9 %collective-permute-start.14 = (f32[128,512]{1,0:T(8,128)S(1)}, f32[128,512]{1,0:T(8,128)S(1)}, u32[]{:S(2)}, u32[]{:S(2)}) collective-permute-start(f32[128,512]{1,0:T(8,128)S(1)} %shard_map.88.token), channel_id=1, source_target_pairs={{3,1},{11,9},{19,17},{27,25}} | collective-permute-start | bytes 786440 | tf_op jit(solution)/shard_map/ppermute | solution.py:306
  44.4 13.9 %collective-permute-start.15 = (f32[128,512]{1,0:T(8,128)S(1)}, f32[128,512]{1,0:T(8,128)S(1)}, u32[]{:S(2)}, u32[]{:S(2)}) collective-permute-start(f32[128,512]{1,0:T(8,128)S(1)} %shard_map.89.token.refs_1_), channel_id=1, source_target_pairs={{5,1},{13,9},{21,17},{29,25}} | collective-permute-start | bytes 786440 | tf_op jit(solution)/shard_map/ppermute | solution.py:306
  46.0 13.5 %collective-permute-start.16 = (f32[128,512]{1,0:T(8,128)S(1)}, f32[128,512]{1,0:T(8,128)S(1)}, u32[]{:S(2)}, u32[]{:S(2)}) collective-permute-start(f32[128,512]{1,0:T(8,128)S(1)} %shard_map.90.token), channel_id=1, source_target_pairs={{3,1},{11,9},{19,17},{27,25}} | collective-permute-start | bytes 786440 | tf_op jit(solution)/shard_map/ppermute | solution.py:306
  47.3 14.8 %collective-permute-start.17 = (f32[128,512]{1,0:T(8,128)S(1)}, f32[128,512]{1,0:T(8,128)S(1)}, u32[]{:S(2)}, u32[]{:S(2)}) collective-permute-start(f32[128,512]{1,0:T(8,128)S(1)} %shard_map.91.token.refs_1_), channel_id=1, source_target_pairs={{5,1},{13,9},{21,17},{29,25}} | collective-permute-start | bytes 786440 | tf_op jit(solution)/shard_map/ppermute | solution.py:306
  58.8 5.2 %collective-permute-start.18 = (f32[128,512]{1,0:T(8,128)S(1)}, f32[128,512]{1,0:T(8,128)S(1)}, u32[]{:S(2)}, u32[]{:S(2)}) collective-permute-start(f32[128,512]{1,0:T(8,128)S(1)} %get-tuple-element.51), channel_id=1, source_target_pairs={{9,5},{17,13},{25,21}} | collective-permute-start | bytes 786440 | tf_op jit(solution)/shard_map/ppermute | solution.py:306
  62.6 2.8 %collective-permute-start.19 = (f32[128,512]{1,0:T(8,128)S(1)}, f32[128,512]{1,0:T(8,128)S(1)}, u32[]{:S(2)}, u32[]{:S(2)}) collective-permute-start(f32[128,512]{1,0:T(8,128)S(1)} %get-tuple-element.52), channel_id=1, source_target_pairs={{9,5},{17,13},{25,21}} | collective-permute-start | bytes 786440 | tf_op jit(solution)/shard_map/ppermute | solution.py:306
  63.3 2.9 %collective-permute-start.20 = (f32[128,512]{1,0:T(8,128)S(1)}, f32[128,512]{1,0:T(8,128)S(1)}, u32[]{:S(2)}, u32[]{:S(2)}) collective-permute-start(f32[128,512]{1,0:T(8,128)S(1)} %get-tuple-element.49.token.refs_2_), channel_id=1, source_target_pairs={{9,7},{17,15},{25,23}} | collective-permute-start | bytes 786440 | tf_op jit(solution)/shard_map/ppermute | solution.py:306
  64.0 2.1 %collective-permute-start.21 = (f32[128,512]{1,0:T(8,128)S(1)}, f32[128,512]{1,0:T(8,128)S(1)}, u32[]{:S(2)}, u32[]{:S(2)}) collective-permute-start(f32[128,512]{1,0:T(8,128)S(1)} %shard_map.96.token.refs_2_), channel_id=1, source_target_pairs={{5,3},{13,11},{21,19},{29,27}} | collective-permute-start | bytes 786440 | tf_op jit(solution)/shard_map/ppermute | solution.py:306
  64.7 2.8 %collective-permute-start.22 = (f32[128,512]{1,0:T(8,128)S(1)}, f32[128,512]{1,0:T(8,128)S(1)}, u32[]{:S(2)}, u32[]{:S(2)}) collective-permute-start(f32[128,512]{1,0:T(8,128)S(1)} %get-tuple-element.50.token.refs_2_), channel_id=1, source_target_pairs={{9,7},{17,15},{25,23}} | collective-permute-start | bytes 786440 | tf_op jit(solution)/shard_map/ppermute | solution.py:306
  65.5 2.1 %collective-permute-start.23 = (f32[128,512]{1,0:T(8,128)S(1)}, f32[128,512]{1,0:T(8,128)S(1)}, u32[]{:S(2)}, u32[]{:S(2)}) collective-permute-start(f32[128,512]{1,0:T(8,128)S(1)} %shard_map.97.token.refs_2_), channel_id=1, source_target_pairs={{5,3},{13,11},{21,19},{29,27}} | collective-permute-start | bytes 786440 | tf_op jit(solution)/shard_map/ppermute | solution.py:306
  66.3 12.5 %collective-permute-start.24 = (f32[128,512]{1,0:T(8,128)S(1)}, f32[128,512]{1,0:T(8,128)S(1)}, u32[]{:S(2)}, u32[]{:S(2)}) collective-permute-start(f32[128,512]{1,0:T(8,128)S(1)} %shard_map.98.token), channel_id=1, source_target_pairs={{3,1},{7,5},{11,9},{15,13},{19,17},{23,21},{27,25},{31,29}} | collective-permute-start | bytes 786440 | tf_op jit(solution)/shard_map/ppermute | solution.py:306
  67.6 14.7 %collective-permute-start.25 = (f32[128,512]{1,0:T(8,128)S(1)}, f32[128,512]{1,0:T(8,128)S(1)}, u32[]{:S(2)}, u32[]{:S(2)}) collective-permute-start(f32[128,512]{1,0:T(8,128)S(1)} %shard_map.99.token), channel_id=1, source_target_pairs={{3,1},{7,5},{11,9},{15,13},{19,17},{23,21},{27,25},{31,29}} | collective-permute-start | bytes 786440 | tf_op jit(solution)/shard_map/ppermute | solution.py:306
  68.9 15.3 %collective-permute-start.26 = (f32[128,512]{1,0:T(8,128)S(1)}, f32[128,512]{1,0:T(8,128)S(1)}, u32[]{:S(2)}, u32[]{:S(2)}) collective-permute-start(f32[128,512]{1,0:T(8,128)S(1)} %shard_map.98.token), channel_id=1, source_target_pairs={{1,0},{3,2},{5,4},{7,6},{9,8},{11,10},{13,12},{15,14},{17,16},{19,... | collective-permute-start | bytes 786440 | tf_op jit(solution)/shard_map/ppermute | solution.py:306
  70.2 14.8 %collective-permute-start.28 = (f32[128,512]{1,0:T(8,128)S(1)}, f32[128,512]{1,0:T(8,128)S(1)}, u32[]{:S(2)}, u32[]{:S(2)}) collective-permute-start(f32[128,512]{1,0:T(8,128)S(1)} %shard_map.99.token), channel_id=1, source_target_pairs={{1,0},{3,2},{5,4},{7,6},{9,8},{11,10},{13,12},{15,14},{17,16},{19,... | collective-permute-start | bytes 786440 | tf_op jit(solution)/shard_map/ppermute | solution.py:306
  79.3 4.9 %collective-permute-start.27 = (f32[128,512]{1,0:T(8,128)S(1)}, f32[128,512]{1,0:T(8,128)S(1)}, u32[]{:S(2)}, u32[]{:S(2)}) collective-permute-start(f32[128,512]{1,0:T(8,128)S(1)} %get-tuple-element.59), channel_id=1, source_target_pairs={{1,0},{3,2},{5,4},{7,6},{9,8},{11,10},{13,12},{15,14},{17,16},{19,... | collective-permute-start | bytes 786440 | tf_op jit(solution)/shard_map/ppermute | solution.py:306
  82.9 2.4 %collective-permute-start.29 = (f32[128,512]{1,0:T(8,128)S(1)}, f32[128,512]{1,0:T(8,128)S(1)}, u32[]{:S(2)}, u32[]{:S(2)}) collective-permute-start(f32[128,512]{1,0:T(8,128)S(1)} %get-tuple-element.62), channel_id=1, source_target_pairs={{1,0},{3,2},{5,4},{7,6},{9,8},{11,10},{13,12},{15,14},{17,16},{19,... | collective-permute-start | bytes 786440 | tf_op jit(solution)/shard_map/ppermute | solution.py:306
